TPU v7x, 32 devices: a whole 2x2x4 slice. The times are simulated.
32 devices in a mesh: strip: 8 (over y, x, core), vec: 4 (over z).
Axes of the slice: x: 2, y: 2, z: 4, core: 2. Of those that a mesh axis runs over, the one named last changes fastest.
Arguments:
- start_vectors: float32 [64, 256, 1024], P('vec', 'strip'), may hold values from -40 to 40
- potential: int32 [256, 1024], P('strip'), may hold values from 0 to 15
- bounds: int32 [4], replicated, may hold values from -96 to 96, as said below
Outputs:
- ortho_basis: float32 [64, 256, 1024], P('vec', 'strip')
- ritz_matrix: float32 [64, 64], replicated
Inputs may be any that keep to these rules, and one draw needn't show every extreme that they name: bounds[0] and bounds[1] enclose the spectrum of H: bounds[0] is at most -84 and bounds[1] at least 84; bounds[0] < bounds[2] < bounds[3] < bounds[1].
All inputs are finite; a program needn't handle non-finite values.
Results may differ from a plain program's by a relative error of at most 0.00021.
Values sent between devices are 32-bit elements; how exact they have to be, the bound alone decides.
No kernel may reach another device: no remote copies, remote signals or barrier semaphores. Data moves between devices by JAX's collectives and lax.ppermute only.
A program may use at most 64 MiB of HBM per device.

v0:
```python
import functools
import math

import jax
import jax.numpy as jnp
from jax import lax
from jax.experimental import pallas as pl
from jax.experimental.pallas import tpu as pltpu
from jax.sharding import PartitionSpec as P

DEGREE = 32
DEPTH = 8
POT_LEVELS = 16
LANES = 128
SUBLANES = 8

grid_unit = 0.0625
disorder = 2.0


def filter_terms(bounds):
    edges = bounds.astype(jnp.float32) * grid_unit
    center = (edges[0] + edges[1]) * 0.5
    spread = (edges[1] - edges[0]) * 0.5
    theta_lo = jnp.arccos((edges[2] - center) / spread)
    theta_hi = jnp.arccos((edges[3] - center) / spread)
    orders = jnp.arange(1, DEGREE + 1).astype(jnp.float32)
    others = 2.0 * (jnp.sin(orders * theta_lo) - jnp.sin(orders * theta_hi)) / (orders * math.pi)
    first = jnp.reshape((theta_lo - theta_hi) / math.pi, (1,))
    return (jnp.concatenate([first, others]), center, spread)


def extended(value, sides, width):
    for axis, dim in sides:
        count, length = (lax.axis_size(axis), value.shape[dim])
        up = [(i, (i + 1) % count) for i in range(count)]
        down = [(j, i) for i, j in up]
        last = lax.slice_in_dim(value, length - width, length, axis=dim)
        leading = lax.slice_in_dim(value, 0, width, axis=dim)
        before = lax.ppermute(last, axis, up)
        after = lax.ppermute(leading, axis, down)
        value = jnp.concatenate([before, value, after], axis=dim)
    return value


def stencil(padded, pot_rows, center, spread):
    middle = padded[:, 1:-1]
    beside = padded[:, 2:] + padded[:, :-2] + jnp.roll(middle, 1, 2) + jnp.roll(middle, -1, 2)
    return ((pot_rows[None] - center) * middle - beside) / spread


def deep_filter(start_vectors, pot_padded, coeffs, center, spread):
    rows = start_vectors.shape[1]

    def one_round(rounds, carry):
        before, current, filtered = carry
        stacked = jnp.stack([before, current])
        padded = extended(stacked, (("strip", 2),), DEPTH)
        old_part = padded[0]
        new_part = padded[1]
        for inner in range(DEPTH):
            counter = rounds * DEPTH + inner
            factor = jnp.where(counter == 0, 1.0, 2.0).astype(jnp.float32)
            pot_rows = pot_padded[inner + 1 : rows + 2 * DEPTH - inner - 1]
            after = factor * stencil(new_part, pot_rows, center, spread) - old_part[:, 1:-1]
            offset = DEPTH - inner - 1
            filtered = filtered + coeffs[counter + 1] * after[:, offset : offset + rows]
            old_part = new_part[:, 1:-1]
            new_part = after
        return (old_part, new_part, filtered)

    initial = (jnp.zeros_like(start_vectors), start_vectors, coeffs[0] * start_vectors)
    return lax.fori_loop(0, DEGREE // DEPTH, one_round, initial)[2]


def halo_shards(start_vectors, potential, bounds):
    _, rows, columns = start_vectors.shape
    pot_field = disorder * (potential.astype(jnp.float32) / (POT_LEVELS - 1) - 0.5)
    coeffs, center, spread = filter_terms(bounds)
    pot_padded = extended(pot_field, (("strip", 0),), DEPTH)
    filtered = deep_filter(start_vectors, pot_padded, coeffs, center, spread)
    padded = extended(filtered, (("strip", 1),), 1)
    applied = stencil(padded, pot_field, 0.0, 1.0)
    slab_vecs, slab_applied = (
        lax.all_to_all(filtered, "vec", split_axis=1, concat_axis=0, tiled=True),
        lax.all_to_all(applied, "vec", split_axis=1, concat_axis=0, tiled=True),
    )
    total_vecs = slab_vecs.shape[0]
    y_rows = slab_vecs.reshape(total_vecs, -1)
    hy_rows = slab_applied.reshape(total_vecs, -1)
    gram_part = jnp.dot(
        y_rows, y_rows.T, precision=lax.Precision.HIGHEST, preferred_element_type=jnp.float32
    )
    cross_part = jnp.dot(
        y_rows, hy_rows.T, precision=lax.Precision.HIGHEST, preferred_element_type=jnp.float32
    )
    gram_sum, cross_sum = lax.psum((gram_part, cross_part), ("strip", "vec"))
    lower_factor = jnp.linalg.cholesky(gram_sum)
    site_count = lax.axis_size("strip") * rows * columns
    ortho = jax.scipy.linalg.solve_triangular(lower_factor, y_rows, lower=True)
    ortho_slab = (math.sqrt(site_count) * ortho).reshape(slab_vecs.shape)
    ortho_basis = lax.all_to_all(ortho_slab, "vec", split_axis=0, concat_axis=1, tiled=True)
    half_done = jax.scipy.linalg.solve_triangular(lower_factor, cross_sum, lower=True)
    ritz_matrix = float(rows) * jax.scipy.linalg.solve_triangular(
        lower_factor, half_done.T, lower=True
    )
    return (ortho_basis, ritz_matrix)


def filter_kernel(coef_ref, me_ref, vec_ref, *rest, slabs, first):
    if first:
        own_ref, other_ref, out_ref, site, pot_ref, sems, flip, grid, field, state_a, state_b = rest
    else:
        site, out_ref, flip, grid, field, state_a, state_b = rest
    rows, parts, strips, lanes = field.shape
    total_rows = rows * strips
    blocks = total_rows // lanes
    per_block = lanes // rows
    slab_rows = rows // slabs
    center = coef_ref[DEGREE + 1]

    def stage(read, target, change):
        for part in range(parts):
            for block in range(blocks):
                tile = jnp.concatenate(
                    [read(block * per_block + p, part * lanes) for p in range(per_block)], axis=0
                )
                flip[block, part * lanes : (part + 1) * lanes, :] = tile.T
        for part in range(parts):
            for block in range(blocks):
                tile = flip[block, pl.ds(part, lanes, stride=parts), :]
                grid[part, block * lanes : (block + 1) * lanes, :] = tile.T

        for j in range(rows):
            for part in range(parts):
                target(j, part, change(grid[part, pl.ds(j, strips, stride=rows), :]))

    def put_site(j, part, value):
        site[j, part] = value

    if first:
        me = me_ref[0]
        copies = [
            pltpu.make_async_copy((own_ref, other_ref)[d & 1].at[d >> 1], pot_ref.at[me ^ d], sems.at[d])
            for d in range(strips)
        ]
        for copy in copies:
            copy.start()
        for copy in copies:
            copy.wait()
        stage(
            lambda p, start: pot_ref[p, :, start : start + lanes],
            put_site,
            lambda level: disorder * (level * (1.0 / (POT_LEVELS - 1)) - 0.5) - center,
        )
    top = coef_ref[DEGREE]

    def put_field(j, part, value):
        field[j, part] = value
        state_a[j + 1, part] = top * value
        state_b[j + 1, part] = jnp.zeros_like(value)

    stage(lambda p, start: vec_ref[p, :, start : start + lanes], put_field, lambda value: value)

    def wrap(state):
        for part in range(parts):
            state[0, part] = pltpu.roll(state[rows, part], 1, 0)
            state[rows + 1, part] = pltpu.roll(state[1, part], strips - 1, 0)

    def sweep(new, cur, weight, scale):
        def next_column(line):
            return line[1:] + [pltpu.roll(line[0], lanes - 1, 1)]

        def corner(here, below):
            sums = [a + b for a, b in zip(next_column(here), below)]
            return sums, [pltpu.roll(sums[-1], 1, 1)] + sums[:-1]

        def load(j):
            return [cur[j, part] for part in range(parts)]

        here = load(1)
        _, moved = corner(load(0), here)

        for j in range(rows):
            below = load(j + 2)
            sums, moved_next = corner(here, below)
            for part in range(parts):
                image = site[j, part] * here[part] - (sums[part] + moved[part])
                if scale is not None:
                    image = scale * image
                new[j + 1, part] = image + (weight * field[j, part] - new[j + 1, part])
            here, moved = below, moved_next

    square = coef_ref[DEGREE + 2]
    wrap(state_a)

    def two(step, carry):
        order = DEGREE - 1 - 2 * step
        sweep(state_b, state_a, coef_ref[order], square)
        wrap(state_b)
        sweep(state_a, state_b, coef_ref[order - 1], None)
        wrap(state_a)
        return carry

    lax.fori_loop(0, (DEGREE - 2) // 2, two, 0)
    sweep(state_b, state_a, coef_ref[1], square)
    wrap(state_b)
    sweep(state_a, state_b, coef_ref[0], 0.5)

    for j in range(rows):
        for part in range(parts):
            grid[part, pl.ds(j, strips, stride=rows), :] = state_a[j + 1, part]
    for part in range(parts):
        for block in range(blocks):
            flip[block, pl.ds(part, lanes, stride=parts), :] = grid[part, block * lanes : (block + 1) * lanes, :].T
    for part in range(parts):
        for block in range(blocks):
            tile = flip[block, part * lanes : (part + 1) * lanes, :].T
            for p in range(per_block):
                for slab in range(slabs):
                    start = p * rows + slab * slab_rows
                    out_ref[slab, block * per_block + p, :, part * lanes : (part + 1) * lanes] = tile[
                        start : start + slab_rows
                    ]


def outer(left, right):
    return lax.dot_general(
        left,
        right,
        (((1,), (1,)), ((), ())),
        precision=lax.Precision.HIGHEST,
        preferred_element_type=jnp.float32,
    )


def gram_kernel(*refs, chunks):
    slab_refs = refs[:chunks]
    pot_ref, out_ref, lines_ref = refs[chunks:]
    slab_rows, total, columns = lines_ref.shape
    acc = jnp.zeros(out_ref.shape, jnp.float32)
    for chunk in range(chunks):
        for group in range(total // (chunks * SUBLANES)):
            here = slice(group * SUBLANES, (group + 1) * SUBLANES)
            start = (group * chunks + chunk) * SUBLANES
            lines_ref[:, start : start + SUBLANES, :] = jnp.swapaxes(slab_refs[chunk][here], 0, 1)
    for j in range(slab_rows):
        here = lines_ref[j]
        level = pot_ref[j : j + 1, :]
        pot = disorder * (level * (1.0 / (POT_LEVELS - 1)) - 0.5)
        image = pot * here - (pltpu.roll(here, 1, 1) + pltpu.roll(here, columns - 1, 1))
        if j < slab_rows - 1:
            image = image - 2.0 * lines_ref[j + 1]
        acc = acc + outer(here, jnp.concatenate([here, image], axis=0))
    out_ref[...] = acc


def edge_kernel(*refs, chunks):
    next_refs = refs[:chunks]
    sums_ref, last_ref, out_ref = refs[chunks:]
    total = sums_ref.shape[0]
    parts = []
    for group in range(total // (chunks * SUBLANES)):
        for chunk in range(chunks):
            parts.append(next_refs[chunk][group * SUBLANES : (group + 1) * SUBLANES, :])
    below = jnp.concatenate(parts, axis=0)
    both = jnp.concatenate([jnp.zeros_like(below), below], axis=0)
    out_ref[...] = sums_ref[...] - 2.0 * outer(last_ref[0], both)


def eliminate(sums):
    total, width = sums.shape
    blocks = total // SUBLANES
    lane = lax.broadcasted_iota(jnp.int32, (SUBLANES, width), 1)
    sublane = lax.broadcasted_iota(jnp.int32, (SUBLANES, width), 0)
    work = []
    for block in range(blocks):
        unit = (lane == sublane + (total + block * SUBLANES)).astype(jnp.float32)
        work.append(jnp.where(lane < total, sums[block * SUBLANES : (block + 1) * SUBLANES], unit))
    for k in range(total):
        home, inside = k // SUBLANES, k % SUBLANES
        columns = [
            jnp.broadcast_to(work[block][:, k : k + 1], (SUBLANES, width)) for block in range(home, blocks)
        ]
        pivot = columns[0][inside : inside + 1, :]
        row = work[home][inside : inside + 1, :] / pivot
        row = jnp.broadcast_to(row, (SUBLANES, width))
        columns[0] = jnp.where(sublane > inside, columns[0], 0.0)
        for block in range(home, blocks):
            work[block] = work[block] - columns[block - home] * row
    result = []
    for block in range(blocks):
        pivots = jnp.sum(
            jnp.where(lane == sublane + block * SUBLANES, work[block], 0.0), axis=1, keepdims=True
        )
        result.append(work[block] / jnp.sqrt(pivots))
    return jnp.concatenate(result, axis=0)[:, total:]


def products(inv_ref, lines_ref, done_ref, out_refs, place, scale, targets, half):
    slab_rows = lines_ref.shape[0]
    vec_local = out_refs[0].shape[0]
    first = ((place ^ targets[0]) // half) * half
    weights = scale * inv_ref[pl.ds(pl.multiple_of(first * vec_local, SUBLANES), half * vec_local), :]
    for j in range(slab_rows):
        done_ref[j] = jnp.dot(
            weights, lines_ref[j], precision=lax.Precision.HIGHEST, preferred_element_type=jnp.float32
        )
    for d, out_ref in zip(targets, out_refs):
        start = ((place ^ d) - first) * vec_local
        for vec in range(0, vec_local, SUBLANES):
            rows = pl.ds(pl.multiple_of(start + vec, SUBLANES), SUBLANES)
            out_ref[vec : vec + SUBLANES] = jnp.swapaxes(done_ref[:, rows, :], 0, 1)


def solve_kernel(place_ref, mine_ref, other_ref, lines_ref, inv_ref, sums_ref, *rest, scale, targets, half):
    sums = mine_ref[...] + other_ref[...]
    sums_ref[...] = sums
    inv_ref[...] = eliminate(sums)
    products(inv_ref, lines_ref, rest[-1], rest[:-1], place_ref[0], scale, targets, half)


def near_kernel(place_ref, inv_ref, lines_ref, *rest, scale, targets, half):
    products(inv_ref, lines_ref, rest[-1], rest[:-1], place_ref[0], scale, targets, half)


def place_kernel(place_ref, *refs, targets):
    out_ref, sems = refs[-2:]
    slab_rows = refs[0].shape[1]
    copies = []
    for n, d in enumerate(targets):
        start = pl.multiple_of((place_ref[0] ^ d) * slab_rows, SUBLANES)
        copies.append(pltpu.make_async_copy(refs[n], out_ref.at[:, pl.ds(start, slab_rows), :], sems.at[n]))
    for copy in copies:
        copy.start()
    for copy in copies:
        copy.wait()


def whole_shards(start_vectors, potential, bounds):
    vec_local, rows, columns = start_vectors.shape
    strips = lax.axis_size("strip")
    groups = lax.axis_size("vec")
    both = ("vec", "strip")
    total_vecs = vec_local * groups
    vecs = vec_local // strips
    slab_rows = rows // groups
    devices = strips * groups

    coeffs, center, spread = filter_terms(bounds)
    beta = 2.0 / spread
    odd = jnp.arange(DEGREE + 1) % 2 == 1
    terms = jnp.concatenate([jnp.where(odd, beta, 1.0) * coeffs, center[None], (beta * beta)[None]])
    me = lax.axis_index("strip").astype(jnp.int32)
    level = potential.astype(jnp.float32)

    def swap(value, bit):
        return lax.ppermute(value, "strip", [(i, i ^ bit) for i in range(strips)])

    inner = []
    for chunk in range(vecs):
        part = start_vectors[chunk * strips : (chunk + 1) * strips]
        inner.append(lax.all_to_all(part, "strip", split_axis=0, concat_axis=0, tiled=True))
    own_pots = jnp.stack([level] + [swap(level, bit) for bit in range(2, strips, 2)])
    other_pots = swap(own_pots, 1)

    parts = columns // LANES
    lattice = (rows, parts, strips, LANES)
    padded = (rows + 2, parts, strips, LANES)
    smem = pl.BlockSpec(memory_space=pltpu.SMEM)
    vmem = pl.BlockSpec(memory_space=pltpu.VMEM)
    hbm = pl.BlockSpec(memory_space=pl.ANY)
    slab_shape = jax.ShapeDtypeStruct((groups, strips, slab_rows, columns), jnp.float32)
    site = None
    slabs, nexts = [], []
    ring = [((i + 1) % devices, i) for i in range(devices)]
    for chunk in range(vecs):
        first = chunk == 0
        done = pl.pallas_call(
            functools.partial(filter_kernel, slabs=groups, first=first),
            in_specs=[smem, smem, vmem] + ([hbm, hbm] if first else [vmem]),
            out_specs=[vmem, vmem] if first else [vmem],
            out_shape=[slab_shape] + ([jax.ShapeDtypeStruct(lattice, jnp.float32)] if first else []),
            scratch_shapes=(
                [pltpu.VMEM((strips, rows, columns), jnp.float32), pltpu.SemaphoreType.DMA((strips,))]
                if first
                else []
            )
            + [
                pltpu.VMEM((strips * rows // LANES, columns, LANES), jnp.float32),
                pltpu.VMEM((parts, strips * rows, LANES), jnp.float32),
                pltpu.VMEM(lattice, jnp.float32),
                pltpu.VMEM(padded, jnp.float32),
                pltpu.VMEM(padded, jnp.float32),
            ],
            name="filter",
        )(terms, me[None], inner[chunk], *((own_pots, other_pots) if first else (site,)))
        if first:
            site = done[1]
        slab = lax.all_to_all(
            done[0].reshape(devices, slab_rows, columns), both, split_axis=0, concat_axis=0, tiled=True
        )
        slabs.append(slab)
        nexts.append(lax.ppermute(slab[:, 0], ("strip", "vec"), ring))

    place = lax.axis_index("vec").astype(jnp.int32)
    own_pot = lax.dynamic_slice_in_dim(level, place * slab_rows, slab_rows, axis=0)
    lines_shape = (slab_rows, total_vecs, columns)
    sums_shape = jax.ShapeDtypeStruct((total_vecs, 2 * total_vecs), jnp.float32)
    sums, lines = pl.pallas_call(
        functools.partial(gram_kernel, chunks=vecs),
        in_specs=[vmem] * (vecs + 1),
        out_specs=[vmem, vmem],
        out_shape=[sums_shape, jax.ShapeDtypeStruct(lines_shape, jnp.float32)],
        name="gram",
    )(*slabs, own_pot)
    sums = pl.pallas_call(
        functools.partial(edge_kernel, chunks=vecs),
        grid=(1,),
        in_specs=[vmem] * (vecs + 1)
        + [pl.BlockSpec((1, total_vecs, columns), lambda i: (slab_rows - 1, 0, 0))],
        out_specs=vmem,
        out_shape=sums_shape,
        name="edge",
    )(*nexts, sums, lines)

    pending = None
    for axis, count in (("strip", strips), ("vec", groups)):
        bit = 1
        while bit < count:
            if pending is not None:
                sums = sums + pending
            pending = lax.ppermute(sums, axis, [(i, i ^ bit) for i in range(count)])
            bit *= 2

    scale = math.sqrt(strips * rows * columns)
    half = groups // 2
    far, near = tuple(range(half, groups)), tuple(range(half))
    piece = jax.ShapeDtypeStruct((vec_local, slab_rows, columns), jnp.float32)
    products_scratch = [pltpu.VMEM((slab_rows, half * vec_local, columns), jnp.float32)]
    inverse, gram_cross, *far_blocks = pl.pallas_call(
        functools.partial(solve_kernel, scale=scale, targets=far, half=half),
        in_specs=[smem, vmem, vmem, vmem],
        out_specs=[vmem] * (2 + half),
        out_shape=[jax.ShapeDtypeStruct((total_vecs, total_vecs), jnp.float32), sums_shape] + [piece] * half,
        scratch_shapes=products_scratch,
        name="solve",
    )(place[None], sums, pending, lines)
    near_blocks = pl.pallas_call(
        functools.partial(near_kernel, scale=scale, targets=near, half=half),
        in_specs=[smem, vmem, vmem],
        out_specs=[vmem] * half,
        out_shape=[piece] * half,
        scratch_shapes=products_scratch,
        name="near",
    )(place[None], inverse, lines)

    def across(block, d):
        return lax.ppermute(block, "vec", [(i, i ^ d) for i in range(groups)]) if d else block

    far_blocks = [across(block, d) for d, block in zip(far, far_blocks)]
    near_blocks = [across(block, d) for d, block in zip(near, near_blocks)]
    out_shape = jax.ShapeDtypeStruct((vec_local, rows, columns), jnp.float32)
    ortho_basis = pl.pallas_call(
        functools.partial(place_kernel, targets=near),
        in_specs=[smem] + [hbm] * half,
        out_specs=hbm,
        out_shape=out_shape,
        scratch_shapes=[pltpu.SemaphoreType.DMA((half,))],
        name="place_near",
    )(place[None], *near_blocks)
    ortho_basis = pl.pallas_call(
        functools.partial(place_kernel, targets=far),
        in_specs=[smem] + [hbm] * (half + 1),
        out_specs=hbm,
        out_shape=out_shape,
        scratch_shapes=[pltpu.SemaphoreType.DMA((half,))],
        input_output_aliases={half + 1: 0},
        name="place_far",
    )(place[None], *far_blocks, ortho_basis)

    cross_half = gram_cross[:, total_vecs:]
    cross_sum = 0.5 * (cross_half + cross_half.T)
    half_done = jnp.dot(inverse, cross_sum, precision=lax.Precision.HIGHEST)
    ritz_matrix = float(rows) * jnp.dot(inverse, half_done.T, precision=lax.Precision.HIGHEST)
    return (ortho_basis, ritz_matrix)


def is_whole(vec_local, rows, columns, strips, groups):
    devices = strips * groups
    return (
        strips == SUBLANES
        and vec_local % strips == 0
        and rows % (groups * SUBLANES) == 0
        and columns % (LANES * SUBLANES) == 0
        and LANES % rows == 0
        and strips * rows % LANES == 0
        and groups >= 2
        and devices & (devices - 1) == 0
        and vec_local % SUBLANES == 0
        and 2 * vec_local * groups == LANES
        and DEGREE % 2 == 0
    )


def solution(mesh):
    strips, groups = mesh.shape["strip"], mesh.shape["vec"]
    in_specs = (P("vec", "strip", None), P("strip", None), P())
    out_specs = (P("vec", "strip", None), P())

    def step(start_vectors, potential, bounds):
        total_vecs, total_rows, columns = start_vectors.shape
        vec_local, rows = total_vecs // groups, total_rows // strips
        whole = is_whole(vec_local, rows, columns, strips, groups)

        def form(*local):
            return (whole_shards if whole else halo_shards)(*local)

        sharded = jax.shard_map(form, mesh=mesh, in_specs=in_specs, out_specs=out_specs, check_vma=False)
        return sharded(start_vectors, potential, bounds)

    return step
```

profile of v0, /device:TPU:0, one launch (start us, length us, event | category | flops | bytes accessed | tf_op | source)
XLA Modules:
  0.0 248.7 jit_solution(16025394993705501095)
XLA Ops:
  0.6 3.1 %fusion.7 = (f32[8,32,1024]{2,1,0:T(8,128)}, f32[8,32,1024]{2,1,0:T(8,128)}) fusion(f32[16,32,1024]{2,1,0:T(8,128)} %param.3), kind=kLoop, calls=%fused_computation.18 | loop fusion | bytes 4194304 | tf_op jit(solution)/shard_map/slice | solution.py:362
  3.8 5.3 %all-to-all-start = ((f32[8,32,1024]{2,1,0:T(8,128)}), f32[8,32,1024]{2,1,0:T(8,128)S(1)}, u32[]{:S(2)}, u32[]{:S(2)}) async-start(f32[8,32,1024]{2,1,0:T(8,128)} %get-tuple-element.23), calls=%async_computation | async-start | bytes 2097152 | tf_op jit(solution)/shard_map/all_to_all | solution.py:363
  9.2 3.0 %collective-permute-start.2 = (f32[32,1024]{1,0:T(8,128)S(1)}, f32[32,1024]{1,0:T(8,128)S(1)}, u32[]{:S(2)}, u32[]{:S(2)}) collective-permute-start(f32[32,1024]{1,0:T(8,128)S(1)} %get-tuple-element.25), channel_id=1, source_target_pairs={{0,24},{4,28},{8,16},{12,20},{16,8},{20,12},{24,0},{28,4},{1,25},{... | collective-permute-start | bytes 393224 | tf_op jit(solution)/shard_map/ppermute | solution.py:358
  12.1 0.6 collective-permute-start.1
  12.7 0.1 collective-permute-start
  12.8 12.4 %all-to-all-done.vec_ref = f32[8,32,1024]{2,1,0:T(8,128)S(1)} async-done(((f32[8,32,1024]{2,1,0:T(8,128)}), f32[8,32,1024]{2,1,0:T(8,128)S(1)}, u32[]{:S(2)}, u32[]{:S(2)}) %all-to-all-start) | async-done | bytes 1048608 | tf_op jit(solution)/shard_map/all_to_all | solution.py:363
  25.2 3.6 %all-to-all-start.2 = ((f32[8,32,1024]{2,1,0:T(8,128)}), f32[8,32,1024]{2,1,0:T(8,128)S(1)}, u32[]{:S(2)}, u32[]{:S(2)}) async-start(f32[8,32,1024]{2,1,0:T(8,128)} %get-tuple-element.22), calls=%async_computation.2 | async-start | bytes 2097152 | tf_op jit(solution)/shard_map/all_to_all | solution.py:363
  28.7 0.4 collective-permute-done.1
  29.2 0.1 collective-permute-done
  29.4 0.7 fusion.8
  34.5 0.1 fusion.4
  34.5 0.6 pad_maximum_fusion.1.coef_ref
  35.1 0.8 copy-done.5
  35.9 16.8 %filter.2 = (f32[4,8,8,1024]{3,2,1,0:T(8,128)}, f32[32,8,8,128]{3,2,1,0:T(8,128)}) custom-call(f32[35]{0:T(128)} %pad_maximum_fusion.1.coef_ref, s32[1]{0:T(128)} %bitcast.6.me_ref, f32[8,32,1024]{2,1,0:T(8,128)} %copy-done.3, f32[4,32,1024]{2,1,0:T(8,128)} %copy-done.4, f32[4,32,1024]{2,1,0:T(8,128)} %copy-done.5), custom_call_target="tpu_custom_call" | custom-call | tf_op jit(solution)/shard_map/filter/pallas_call | solution.py:379
  52.7 5.9 %all-to-all-start.1 = ((f32[32,8,1024]{2,1,0:T(8,128)}), f32[32,8,1024]{2,1,0:T(8,128)S(1)}, u32[]{:S(2)}, u32[]{:S(2)}) async-start(f32[32,8,1024]{2,1,0:T(8,128)} %bitcast.29), calls=%async_computation.1 | async-start | bytes 2097152 | tf_op jit(solution)/shard_map/all_to_all | solution.py:400
  58.6 14.6 %filter.3 = f32[4,8,8,1024]{3,2,1,0:T(8,128)} custom-call(f32[35]{0:T(128)} %pad_maximum_fusion.1.coef_ref, s32[1]{0:T(128)} %bitcast.6.me_ref, f32[8,32,1024]{2,1,0:T(8,128)} %copy-done.2, f32[32,8,8,128]{3,2,1,0:T(8,128)} %get-tuple-element.13.rest_0_), custom_call_target="tpu_custom_call" | custom-call | tf_op jit(solution)/shard_map/filter/pallas_call | solution.py:379
  73.2 11.6 %all-to-all-done.1.refs_0_ = f32[32,8,1024]{2,1,0:T(8,128)S(1)} async-done(((f32[32,8,1024]{2,1,0:T(8,128)}), f32[32,8,1024]{2,1,0:T(8,128)S(1)}, u32[]{:S(2)}, u32[]{:S(2)}) %all-to-all-start.1) | async-done | bytes 1048608 | tf_op jit(solution)/shard_map/all_to_all | solution.py:400
  84.8 3.6 %all-to-all-start.3 = ((f32[32,8,1024]{2,1,0:T(8,128)}), f32[32,8,1024]{2,1,0:T(8,128)S(1)}, u32[]{:S(2)}, u32[]{:S(2)}) async-start(f32[32,8,1024]{2,1,0:T(8,128)} %bitcast.28), calls=%async_computation.3 | async-start | bytes 2097152 | tf_op jit(solution)/shard_map/all_to_all | solution.py:400
  88.5 26.1 %all-to-all-done.3.refs_1_ = f32[32,8,1024]{2,1,0:T(8,128)S(1)} async-done(((f32[32,8,1024]{2,1,0:T(8,128)}), f32[32,8,1024]{2,1,0:T(8,128)S(1)}, u32[]{:S(2)}, u32[]{:S(2)}) %all-to-all-start.3) | async-done | bytes 1048608 | tf_op jit(solution)/shard_map/all_to_all | solution.py:400
  114.7 3.0 %collective-permute-start.5 = (f32[32,1024]{1,0:T(8,128)S(1)}, f32[32,1024]{1,0:T(8,128)S(1)}, u32[]{:S(2)}, u32[]{:S(2)}) collective-permute-start(f32[32,1024]{1,0:T(8,128)S(1)} %bitcast.31), channel_id=1, source_target_pairs={{1,0},{2,1},{3,2},{4,3},{5,4},{6,5},{7,6},{8,7},{9,8},{10,9},{11,1... | collective-permute-start | bytes 393224 | tf_op jit(solution)/shard_map/ppermute | solution.py:404
  117.7 0.3 collective-permute-start.4
  118.0 0.6 constant_dynamic-slice_fusion.refs_2_
  118.6 7.0 %gram.1 = (f32[64,128]{1,0:T(8,128)}, f32[8,64,1024]{2,1,0:T(8,128)}) custom-call(f32[32,8,1024]{2,1,0:T(8,128)} %copy-done, f32[32,8,1024]{2,1,0:T(8,128)} %copy-done.1, f32[8,1024]{1,0:T(8,128)} %constant_dynamic-slice_fusion.refs_2_), custom_call_target="tpu_custom_call" | custom-call | tf_op jit(solution)/shard_map/gram/pallas_call | solution.py:410
  125.6 0.6 copy-done.12
  126.3 2.4 edge.1
  128.6 1.4 collective-permute-done.6
  130.0 0.8 add.43
  130.8 0.6 collective-permute-start.7
  131.4 3.3 %collective-permute-done.7 = f32[64,128]{1,0:T(8,128)S(1)} collective-permute-done((f32[64,128]{1,0:T(8,128)S(1)}, f32[64,128]{1,0:T(8,128)S(1)}, u32[]{:S(2)}, u32[]{:S(2)}) %collective-permute-start.7) | collective-permute-done | bytes 32800 | tf_op jit(solution)/shard_map/ppermute | solution.py:433
  134.7 3.9 %collective-permute-done.8 = f32[64,128]{1,0:T(8,128)S(1)} collective-permute-done((f32[64,128]{1,0:T(8,128)S(1)}, f32[64,128]{1,0:T(8,128)S(1)}, u32[]{:S(2)}, u32[]{:S(2)}) %collective-permute-start.8) | collective-permute-done | bytes 32800 | tf_op jit(solution)/shard_map/ppermute | solution.py:433
  138.6 1.8 collective-permute-start.9
  140.4 2.1 collective-permute-done.9
  142.6 0.4 collective-permute-start.10
  143.0 4.5 %collective-permute-done.10.other_ref = f32[64,128]{1,0:T(8,128)S(1)} collective-permute-done((f32[64,128]{1,0:T(8,128)S(1)}, f32[64,128]{1,0:T(8,128)S(1)}, u32[]{:S(2)}, u32[]{:S(2)}) %collective-permute-start.10) | collective-permute-done | bytes 32800 | tf_op jit(solution)/shard_map/ppermute | solution.py:433
  147.5 0.6 copy-done.15
  148.1 9.2 %solve.1 = (f32[64,64]{1,0:T(8,128)}, f32[64,128]{1,0:T(8,128)}, f32[16,8,1024]{2,1,0:T(8,128)}, f32[16,8,1024]{2,1,0:T(8,128)}) custom-call(s32[1]{0:T(128)} %bitcast.place_ref, f32[64,128]{1,0:T(8,128)} %copy-done.10, f32[64,128]{1,0:T(8,128)} %copy-done.15, f32[8,64,1024]{2,1,0:T(8,128)} %get-tuple-element.15.refs_3_.lines_ref), custom_call_target="tpu_custom_call" | custom-call | tf_op jit(solution)/shard_map/solve/pallas_call | solution.py:441
  157.2 3.7 %near.1 = (f32[16,8,1024]{2,1,0:T(8,128)}, f32[16,8,1024]{2,1,0:T(8,128)}) custom-call(s32[1]{0:T(128)} %bitcast.place_ref, f32[64,64]{1,0:T(8,128)} %get-tuple-element.18.inv_ref, f32[8,64,1024]{2,1,0:T(8,128)} %get-tuple-element.15.refs_3_.lines_ref), custom_call_target="tpu_custom_call" | custom-call | tf_op jit(solution)/shard_map/near/pallas_call | solution.py:449
  161.0 1.8 collective-permute-start.13
  162.7 0.4 collective-permute-start.11
  163.1 2.3 collective-permute-start.12
  165.5 0.2 fusion.1
  165.8 0.8 convolution_multiply_fusion
  166.6 13.7 %collective-permute-done.13.refs_1_ = f32[16,8,1024]{2,1,0:T(8,128)S(1)} collective-permute-done((f32[16,8,1024]{2,1,0:T(8,128)}, f32[16,8,1024]{2,1,0:T(8,128)S(1)}, u32[]{:S(2)}, u32[]{:S(2)}) %collective-permute-start.13) | collective-permute-done | bytes 524320 | tf_op jit(solution)/shard_map/ppermute | solution.py:459
  180.3 0.8 copy-done.6
  181.1 32.9 %place_near.1.refs_2_ = f32[16,32,1024]{2,1,0:T(8,128)} custom-call(s32[1]{0:T(128)} %bitcast.place_ref, f32[16,8,1024]{2,1,0:T(8,128)} %get-tuple-element.19.refs_0_, f32[16,8,1024]{2,1,0:T(8,128)} %copy-done.6), custom_call_target="tpu_custom_call" | custom-call | tf_op jit(solution)/shard_map/place_near/pallas_call | solution.py:464
  214.0 0.8 copy-done.7
  214.8 0.8 copy-done.8
  215.6 32.9 %place_far.1 = f32[16,32,1024]{2,1,0:T(8,128)} custom-call(s32[1]{0:T(128)} %bitcast.place_ref, f32[16,8,1024]{2,1,0:T(8,128)} %copy-done.7, f32[16,8,1024]{2,1,0:T(8,128)} %copy-done.8, f32[16,32,1024]{2,1,0:T(8,128)} %place_near.1.refs_2_), custom_call_target="tpu_custom_call", output_to_operand_aliasing={{}: (3, {})} | custom-call | tf_op jit(solution)/shard_map/place_far/pallas_call | solution.py:472
  (55 shorter events, 0.7 us)
Async XLA Ops:
  3.8 5.3 %copy-start.11 = (s32[32,1024]{1,0:T(8,128)S(1)}, s32[32,1024]{1,0:T(8,128)}, u32[]{:S(2)}) copy-start(s32[32,1024]{1,0:T(8,128)} %param.4) | copy-start | bytes 393220
  3.8 21.4 %all-to-all-start = ((f32[8,32,1024]{2,1,0:T(8,128)}), f32[8,32,1024]{2,1,0:T(8,128)S(1)}, u32[]{:S(2)}, u32[]{:S(2)}) async-start(f32[8,32,1024]{2,1,0:T(8,128)} %get-tuple-element.23), calls=%async_computation | async-start | bytes 2097152 | tf_op jit(solution)/shard_map/all_to_all | solution.py:363
  9.1 20.3 %copy-start.18 = (s32[4]{0:T(128)S(1)}, s32[4]{0:T(128)}, u32[]{:S(2)}) copy-start(s32[4]{0:T(128)} %param.5) | copy-start | bytes 52
  9.2 19.6 %collective-permute-start.2 = (f32[32,1024]{1,0:T(8,128)S(1)}, f32[32,1024]{1,0:T(8,128)S(1)}, u32[]{:S(2)}, u32[]{:S(2)}) collective-permute-start(f32[32,1024]{1,0:T(8,128)S(1)} %get-tuple-element.25), channel_id=1, source_target_pairs={{0,24},{4,28},{8,16},{12,20},{16,8},{20,12},{24,0},{28,4},{1,25},{... | collective-permute-start | bytes 393224 | tf_op jit(solution)/shard_map/ppermute | solution.py:358
  12.1 17.0 %collective-permute-start.1 = (f32[32,1024]{1,0:T(8,128)S(1)}, f32[32,1024]{1,0:T(8,128)S(1)}, u32[]{:S(2)}, u32[]{:S(2)}) collective-permute-start(f32[32,1024]{1,0:T(8,128)S(1)} %get-tuple-element.25), channel_id=1, source_target_pairs={{0,16},{4,20},{8,24},{12,28},{16,0},{20,4},{24,8},{28,12},{1,17},{... | collective-permute-start | bytes 393224 | tf_op jit(solution)/shard_map/ppermute | solution.py:358
  12.7 16.6 %collective-permute-start = (f32[32,1024]{1,0:T(8,128)S(1)}, f32[32,1024]{1,0:T(8,128)S(1)}, u32[]{:S(2)}, u32[]{:S(2)}) collective-permute-start(f32[32,1024]{1,0:T(8,128)S(1)} %get-tuple-element.25), channel_id=1, source_target_pairs={{0,8},{4,12},{8,0},{12,4},{16,24},{20,28},{24,16},{28,20},{1,9},{5... | collective-permute-start | bytes 393224 | tf_op jit(solution)/shard_map/ppermute | solution.py:358
  25.2 10.0 %copy-start.3 = (f32[8,32,1024]{2,1,0:T(8,128)}, f32[8,32,1024]{2,1,0:T(8,128)S(1)}, u32[]{:S(2)}) copy-start(f32[8,32,1024]{2,1,0:T(8,128)S(1)} %all-to-all-done.vec_ref) | copy-start | bytes 3145732
  25.2 27.5 %all-to-all-start.2 = ((f32[8,32,1024]{2,1,0:T(8,128)}), f32[8,32,1024]{2,1,0:T(8,128)S(1)}, u32[]{:S(2)}, u32[]{:S(2)}) async-start(f32[8,32,1024]{2,1,0:T(8,128)} %get-tuple-element.22), calls=%async_computation.2 | async-start | bytes 2097152 | tf_op jit(solution)/shard_map/all_to_all | solution.py:363
  29.3 5.8 %copy-start.4 = (f32[4,32,1024]{2,1,0:T(8,128)}, f32[4,32,1024]{2,1,0:T(8,128)S(1)}, u32[]{:S(2)}) copy-start(f32[4,32,1024]{2,1,0:T(8,128)S(1)} %pad_maximum_fusion.rest_0_) | copy-start | bytes 1572868
  29.3 5.8 %collective-permute-start.3 = (f32[4,32,1024]{2,1,0:T(8,128)S(1)}, f32[4,32,1024]{2,1,0:T(8,128)S(1)}, u32[]{:S(2)}, u32[]{:S(2)}) collective-permute-start(f32[4,32,1024]{2,1,0:T(8,128)S(1)} %pad_maximum_fusion.rest_0_), channel_id=1, source_target_pairs={{0,4},{4,0},{8,12},{12,8},{16,20},{20,16},{24,28},{28,24},{1,5},{5... | collective-permute-start | bytes 1572872 | tf_op jit(solution)/shard_map/ppermute | solution.py:358
  35.1 0.8 copy-start.5
  52.7 5.9 %copy-start.2 = (f32[8,32,1024]{2,1,0:T(8,128)}, f32[8,32,1024]{2,1,0:T(8,128)S(1)}, u32[]{:S(2)}) copy-start(f32[8,32,1024]{2,1,0:T(8,128)S(1)} %all-to-all-done.2.vec_ref) | copy-start | bytes 3145732
  52.7 32.1 %all-to-all-start.1 = ((f32[32,8,1024]{2,1,0:T(8,128)}), f32[32,8,1024]{2,1,0:T(8,128)S(1)}, u32[]{:S(2)}, u32[]{:S(2)}) async-start(f32[32,8,1024]{2,1,0:T(8,128)} %bitcast.29), calls=%async_computation.1 | async-start | bytes 2097152 | tf_op jit(solution)/shard_map/all_to_all | solution.py:400
  84.8 33.8 %copy-start = (f32[32,8,1024]{2,1,0:T(8,128)}, f32[32,8,1024]{2,1,0:T(8,128)S(1)}, u32[]{:S(2)}) copy-start(f32[32,8,1024]{2,1,0:T(8,128)S(1)} %all-to-all-done.1.refs_0_) | copy-start | bytes 3145732
  84.8 29.8 %all-to-all-start.3 = ((f32[32,8,1024]{2,1,0:T(8,128)}), f32[32,8,1024]{2,1,0:T(8,128)S(1)}, u32[]{:S(2)}, u32[]{:S(2)}) async-start(f32[32,8,1024]{2,1,0:T(8,128)} %bitcast.28), calls=%async_computation.3 | async-start | bytes 2097152 | tf_op jit(solution)/shard_map/all_to_all | solution.py:400
  114.6 4.0 %copy-start.1 = (f32[32,8,1024]{2,1,0:T(8,128)}, f32[32,8,1024]{2,1,0:T(8,128)S(1)}, u32[]{:S(2)}) copy-start(f32[32,8,1024]{2,1,0:T(8,128)S(1)} %all-to-all-done.3.refs_1_) | copy-start | bytes 3145732
  114.7 10.8 %collective-permute-start.5 = (f32[32,1024]{1,0:T(8,128)S(1)}, f32[32,1024]{1,0:T(8,128)S(1)}, u32[]{:S(2)}, u32[]{:S(2)}) collective-permute-start(f32[32,1024]{1,0:T(8,128)S(1)} %bitcast.31), channel_id=1, source_target_pairs={{1,0},{2,1},{3,2},{4,3},{5,4},{6,5},{7,6},{8,7},{9,8},{10,9},{11,1... | collective-permute-start | bytes 393224 | tf_op jit(solution)/shard_map/ppermute | solution.py:404
  117.7 7.8 %collective-permute-start.4 = (f32[32,1024]{1,0:T(8,128)S(1)}, f32[32,1024]{1,0:T(8,128)S(1)}, u32[]{:S(2)}, u32[]{:S(2)}) collective-permute-start(f32[32,1024]{1,0:T(8,128)S(1)} %bitcast.30), channel_id=1, source_target_pairs={{1,0},{2,1},{3,2},{4,3},{5,4},{6,5},{7,6},{8,7},{9,8},{10,9},{11,1... | collective-permute-start | bytes 393224 | tf_op jit(solution)/shard_map/ppermute | solution.py:404
  125.5 0.7 copy-start.12
  125.6 0.7 copy-start.13
  128.6 1.4 collective-permute-start.6
  130.8 3.9 %collective-permute-start.7 = (f32[64,128]{1,0:T(8,128)S(1)}, f32[64,128]{1,0:T(8,128)S(1)}, u32[]{:S(2)}, u32[]{:S(2)}) collective-permute-start(f32[64,128]{1,0:T(8,128)S(1)} %add.43), channel_id=1, source_target_pairs={{0,8},{4,12},{8,0},{12,4},{16,24},{20,28},{24,16},{28,20},{1,9},{5... | collective-permute-start | bytes 98312 | tf_op jit(solution)/shard_map/ppermute | solution.py:433
  134.7 3.9 %collective-permute-start.8 = (f32[64,128]{1,0:T(8,128)S(1)}, f32[64,128]{1,0:T(8,128)S(1)}, u32[]{:S(2)}, u32[]{:S(2)}) collective-permute-start(f32[64,128]{1,0:T(8,128)S(1)} %add.44), channel_id=1, source_target_pairs={{0,16},{4,20},{8,24},{12,28},{16,0},{20,4},{24,8},{28,12},{1,17},{... | collective-permute-start | bytes 98312 | tf_op jit(solution)/shard_map/ppermute | solution.py:433
  138.6 3.9 %collective-permute-start.9 = (f32[64,128]{1,0:T(8,128)S(1)}, f32[64,128]{1,0:T(8,128)S(1)}, u32[]{:S(2)}, u32[]{:S(2)}) collective-permute-start(f32[64,128]{1,0:T(8,128)S(1)} %add.45), channel_id=1, source_target_pairs={{0,1},{1,0},{2,3},{3,2},{4,5},{5,4},{6,7},{7,6},{8,9},{9,8},{10,11... | collective-permute-start | bytes 98312 | tf_op jit(solution)/shard_map/ppermute | solution.py:433
  142.6 4.9 %copy-start.10 = (f32[64,128]{1,0:T(8,128)}, f32[64,128]{1,0:T(8,128)S(1)}, u32[]{:S(2)}) copy-start(f32[64,128]{1,0:T(8,128)S(1)} %add.46.mine_ref) | copy-start | bytes 98308
  142.6 4.9 %collective-permute-start.10 = (f32[64,128]{1,0:T(8,128)S(1)}, f32[64,128]{1,0:T(8,128)S(1)}, u32[]{:S(2)}, u32[]{:S(2)}) collective-permute-start(f32[64,128]{1,0:T(8,128)S(1)} %add.46.mine_ref), channel_id=1, source_target_pairs={{0,2},{1,3},{2,0},{3,1},{4,6},{5,7},{6,4},{7,5},{8,10},{9,11},{10,... | collective-permute-start | bytes 98312 | tf_op jit(solution)/shard_map/ppermute | solution.py:433
  147.5 0.6 copy-start.15
  157.2 5.5 %copy-start.17 = (f32[16,8,1024]{2,1,0:T(8,128)S(1)}, f32[16,8,1024]{2,1,0:T(8,128)}, u32[]{:S(2)}) copy-start(f32[16,8,1024]{2,1,0:T(8,128)} %get-tuple-element.16) | copy-start | bytes 1572868
  157.2 5.9 %copy-start.16 = (f32[16,8,1024]{2,1,0:T(8,128)S(1)}, f32[16,8,1024]{2,1,0:T(8,128)}, u32[]{:S(2)}) copy-start(f32[16,8,1024]{2,1,0:T(8,128)} %get-tuple-element.17) | copy-start | bytes 1572868
  157.2 8.2 %copy-start.14 = (f32[64,128]{1,0:T(8,128)S(1)}, f32[64,128]{1,0:T(8,128)}, u32[]{:S(2)}) copy-start(f32[64,128]{1,0:T(8,128)} %get-tuple-element.21) | copy-start | bytes 98308
  157.2 8.3 %copy-start.9 = (f32[64,64]{1,0:T(8,128)S(1)}, f32[64,64]{1,0:T(8,128)}, u32[]{:S(2)}) copy-start(f32[64,64]{1,0:T(8,128)} %get-tuple-element.18.inv_ref) | copy-start | bytes 49156
  161.0 19.3 %collective-permute-start.13 = (f32[16,8,1024]{2,1,0:T(8,128)}, f32[16,8,1024]{2,1,0:T(8,128)S(1)}, u32[]{:S(2)}, u32[]{:S(2)}) collective-permute-start(f32[16,8,1024]{2,1,0:T(8,128)} %get-tuple-element.20), channel_id=1, source_target_pairs={{0,1},{1,0},{2,3},{3,2},{4,5},{5,4},{6,7},{7,6},{8,9},{9,8},{10,11... | collective-permute-start | bytes 1572872 | tf_op jit(solution)/shard_map/ppermute | solution.py:459
  162.7 51.2 %collective-permute-start.11 = (f32[16,8,1024]{2,1,0:T(8,128)S(1)}, f32[16,8,1024]{2,1,0:T(8,128)S(1)}, u32[]{:S(2)}, u32[]{:S(2)}) collective-permute-start(f32[16,8,1024]{2,1,0:T(8,128)S(1)} %copy-done.17), channel_id=1, source_target_pairs={{0,2},{1,3},{2,0},{3,1},{4,6},{5,7},{6,4},{7,5},{8,10},{9,11},{10,... | collective-permute-start | bytes 1572872 | tf_op jit(solution)/shard_map/ppermute | solution.py:459
  163.1 50.9 %collective-permute-start.12 = (f32[16,8,1024]{2,1,0:T(8,128)S(1)}, f32[16,8,1024]{2,1,0:T(8,128)S(1)}, u32[]{:S(2)}, u32[]{:S(2)}) collective-permute-start(f32[16,8,1024]{2,1,0:T(8,128)S(1)} %copy-done.16), channel_id=1, source_target_pairs={{0,3},{1,2},{2,1},{3,0},{4,7},{5,6},{6,5},{7,4},{8,11},{9,10},{10,... | collective-permute-start | bytes 1572872 | tf_op jit(solution)/shard_map/ppermute | solution.py:459
  180.3 0.8 copy-start.6
  214.0 0.8 copy-start.7
  214.8 0.8 copy-start.8
where the time goes:
time: 249 us
  Pallas kernels  119 us (48%)
  waiting for transfers between devices  79.5 us (32%)
  starting transfers between devices  32.4 us (13%)
  local copies, waits for them, and re-layouts  9.31 us (4%)
  between operations  5.39 us (2%)
    all_to_all x2, waiting for transfers between devices, whole_shards(): lax.all_to_all(done[0].reshape(devices, slab_rows, columns), both, split_...  37.6 us
    pallas_call x1, Pallas kernels, whole_shards(): pl.pallas_call(functools.partial(place_kernel, targets=near), in_specs=[s...  32.9 us
    pallas_call x1, Pallas kernels, whole_shards(): pl.pallas_call(functools.partial(place_kernel, targets=far), in_specs=[sm...  32.9 us
    pallas_call x2, Pallas kernels, whole_shards(): pl.pallas_call(functools.partial(filter_kernel, slabs=groups, first=first...  31.4 us
    ppermute x5, waiting for transfers between devices, whole_shards(): pending = lax.ppermute(sums, axis, [(i, i ^ bit) for i in range(count)])  15.3 us
    ppermute x3, waiting for transfers between devices, across(): lax.ppermute(block, 'vec', [(i, i ^ d) for i in range(groups)])  13.7 us
    all_to_all x2, waiting for transfers between devices, whole_shards(): lax.all_to_all(part, 'strip', split_axis=0, concat_axis=0, tiled=True)  12.4 us
    all_to_all x2, starting transfers between devices, whole_shards(): lax.all_to_all(done[0].reshape(devices, slab_rows, columns), both, split_...  9.48 us
  transfers between devices with their start and end apart: 18, of which 11 were waited for; matrix products, arithmetic and copies ran while one was open for 1% of the time, Pallas kernels for 29%

commit v1 on v0

--- a/solution.py
+++ b/solution.py
@@ -109,7 +109,7 @@
 
 def filter_kernel(coef_ref, me_ref, vec_ref, *rest, slabs, first):
     if first:
-        own_ref, other_ref, out_ref, site, pot_ref, sems, flip, grid, field, state_a, state_b = rest
+        here_ref, beside_ref, own_ref, other_ref, out_ref, site, pot_ref, sems, flip, grid, field, state_a, state_b = rest
     else:
         site, out_ref, flip, grid, field, state_a, state_b = rest
     rows, parts, strips, lanes = field.shape
@@ -140,9 +140,11 @@
 
     if first:
         me = me_ref[0]
+        sources = [here_ref, beside_ref]
+        for d in range(2, strips):
+            sources.append((own_ref, other_ref)[d & 1].at[(d >> 1) - 1])
         copies = [
-            pltpu.make_async_copy((own_ref, other_ref)[d & 1].at[d >> 1], pot_ref.at[me ^ d], sems.at[d])
-            for d in range(strips)
+            pltpu.make_async_copy(sources[d], pot_ref.at[me ^ d], sems.at[d]) for d in range(strips)
         ]
         for copy in copies:
             copy.start()
@@ -361,7 +363,9 @@
     for chunk in range(vecs):
         part = start_vectors[chunk * strips : (chunk + 1) * strips]
         inner.append(lax.all_to_all(part, "strip", split_axis=0, concat_axis=0, tiled=True))
-    own_pots = jnp.stack([level] + [swap(level, bit) for bit in range(2, strips, 2)])
+    beside = swap(level, 1)
+    pieces = [swap(level, bit) for bit in range(2, strips, 2)]
+    own_pots = jnp.stack(pieces)
     other_pots = swap(own_pots, 1)
 
     parts = columns // LANES
@@ -378,7 +382,7 @@
         first = chunk == 0
         done = pl.pallas_call(
             functools.partial(filter_kernel, slabs=groups, first=first),
-            in_specs=[smem, smem, vmem] + ([hbm, hbm] if first else [vmem]),
+            in_specs=[smem, smem, vmem] + ([hbm] * 4 if first else [vmem]),
             out_specs=[vmem, vmem] if first else [vmem],
             out_shape=[slab_shape] + ([jax.ShapeDtypeStruct(lattice, jnp.float32)] if first else []),
             scratch_shapes=(
@@ -394,7 +398,7 @@
                 pltpu.VMEM(padded, jnp.float32),
             ],
             name="filter",
-        )(terms, me[None], inner[chunk], *((own_pots, other_pots) if first else (site,)))
+        )(terms, me[None], inner[chunk], *((level, beside, own_pots, other_pots) if first else (site,)))
         if first:
             site = done[1]
         slab = lax.all_to_all(
@@ -463,7 +467,7 @@
     out_shape = jax.ShapeDtypeStruct((vec_local, rows, columns), jnp.float32)
     ortho_basis = pl.pallas_call(
         functools.partial(place_kernel, targets=near),
-        in_specs=[smem] + [hbm] * half,
+        in_specs=[smem] + [vmem] * half,
         out_specs=hbm,
         out_shape=out_shape,
         scratch_shapes=[pltpu.SemaphoreType.DMA((half,))],
@@ -471,7 +475,7 @@
     )(place[None], *near_blocks)
     ortho_basis = pl.pallas_call(
         functools.partial(place_kernel, targets=far),
-        in_specs=[smem] + [hbm] * (half + 1),
+        in_specs=[smem] + [vmem] * half + [hbm],
         out_specs=hbm,
         out_shape=out_shape,
         scratch_shapes=[pltpu.SemaphoreType.DMA((half,))],

time: 249 us -> 243 us (0.976); the launches traced: 249 us -> 240 us
  Pallas kernels: 119 us -> 57.9 us
  blocking collectives: 0 us -> 50.8 us
  waiting for transfers between devices: 79.5 us -> 86.6 us
  starting transfers between devices: 32.4 us -> 25.9 us
    all_to_all x0 -> x2, blocking collectives: none -> 50.8 us  [the longest x1 30.3 us: whole_shards(): lax.all_to_all(done[0].reshape(devices, slab_rows, columns), both, split_...]
    pallas_call x1, Pallas kernels: 32.9 us -> 2.18 us  [whole_shards(): pl.pallas_call(functools.partial(place_kernel, targets=far), in_specs=[sm...]
    pallas_call x1, Pallas kernels: 32.9 us -> 2.18 us  [whole_shards(): pl.pallas_call(functools.partial(place_kernel, targets=near), in_specs=[s...]
    ppermute x4 -> x5, waiting for transfers between devices: 0.51 us -> 17.4 us  [swap(): return lax.ppermute(value, 'strip', [(i, i ^ bit) for i in range(strips)])]
    all_to_all x2 -> x1, waiting for transfers between devices: 37.6 us -> 21.4 us  [whole_shards(): lax.all_to_all(done[0].reshape(devices, slab_rows, columns), both, split_...]
    ppermute x3, waiting for transfers between devices: 13.7 us -> 29.8 us  [across(): lax.ppermute(block, 'vec', [(i, i ^ d) for i in range(groups)])]
    all_to_all x2 -> x1, waiting for transfers between devices: 12.4 us -> 0.01 us  [whole_shards(): lax.all_to_all(part, 'strip', split_axis=0, concat_axis=0, tiled=True)]
    ppermute x2, starting transfers between devices: 3.23 us -> 10.6 us  [whole_shards(): nexts.append(lax.ppermute(slab[:, 0], ('strip', 'vec'), ring))]
  transfers between devices with their start and end apart: 18 -> 17, of which waited for: 11 -> 10; matrix products, arithmetic and copies ran while one was open for 1% -> 2% of each run, Pallas kernels for 29% -> 11%
where the time goes in v1:
time: 243 us; the launch traced here: 240 us
  waiting for transfers between devices  86.6 us (36%)
  Pallas kernels  57.9 us (24%)
  blocking collectives  50.8 us (21%)
  starting transfers between devices  25.9 us (11%)
  local copies, waits for them, and re-layouts  10.5 us (4%)
  between operations  5.16 us (2%)
    pallas_call x2, Pallas kernels, whole_shards(): pl.pallas_call(functools.partial(filter_kernel, slabs=groups, first=first...  31.4 us
    all_to_all x1, blocking collectives, whole_shards(): lax.all_to_all(done[0].reshape(devices, slab_rows, columns), both, split_...  30.3 us
    ppermute x3, waiting for transfers between devices, across(): lax.ppermute(block, 'vec', [(i, i ^ d) for i in range(groups)])  29.8 us
    all_to_all x1, waiting for transfers between devices, whole_shards(): lax.all_to_all(done[0].reshape(devices, slab_rows, columns), both, split_...  21.4 us
    all_to_all x1, blocking collectives, whole_shards(): lax.all_to_all(part, 'strip', split_axis=0, concat_axis=0, tiled=True)  20.6 us
    ppermute x5, waiting for transfers between devices, whole_shards(): pending = lax.ppermute(sums, axis, [(i, i ^ bit) for i in range(count)])  18.1 us
    ppermute x5, waiting for transfers between devices, swap(): return lax.ppermute(value, 'strip', [(i, i ^ bit) for i in range(strips)])  17.4 us
    ppermute x2, starting transfers between devices, whole_shards(): nexts.append(lax.ppermute(slab[:, 0], ('strip', 'vec'), ring))  10.6 us
  transfers between devices with their start and end apart: 17, of which 10 were waited for; matrix products, arithmetic and copies ran while one was open for 2% of the time, Pallas kernels for 11%

profile of v1, /device:TPU:0, one launch (start us, length us, event | category | flops | bytes accessed | tf_op | source)
XLA Modules:
  0.0 239.7 jit_solution(4846256057302336183)
XLA Ops:
  0.6 2.7 %fusion.7 = (f32[8,32,1024]{2,1,0:T(8,128)}, f32[8,32,1024]{2,1,0:T(8,128)S(1)}) fusion(f32[16,32,1024]{2,1,0:T(8,128)} %param.3), kind=kLoop, calls=%fused_computation.17 | loop fusion | bytes 4194304 | tf_op jit(solution)/shard_map/slice | solution.py:364
  3.3 20.6 %all_to_all.20.vec_ref = f32[8,32,1024]{2,1,0:T(8,128)} all-to-all(f32[8,32,1024]{2,1,0:T(8,128)S(1)} %get-tuple-element.23), channel_id=1, replica_groups=mesh['strip'=8,'vec'=4] {'strip'}, dimensions={0} | all-to-all | bytes 2097152 | tf_op jit(solution)/shard_map/all_to_all | solution.py:365
  23.9 3.6 %all-to-all-start.2 = ((f32[8,32,1024]{2,1,0:T(8,128)}), f32[8,32,1024]{2,1,0:T(8,128)S(1)}, u32[]{:S(2)}, u32[]{:S(2)}) async-start(f32[8,32,1024]{2,1,0:T(8,128)} %get-tuple-element.22), calls=%async_computation.2 | async-start | bytes 2097152 | tf_op jit(solution)/shard_map/all_to_all | solution.py:365
  27.5 2.0 collective-permute-start.1
  29.5 1.5 collective-permute-start.2
  31.0 0.1 collective-permute-start.3
  31.1 14.2 %collective-permute-done.1 = f32[32,1024]{1,0:T(8,128)S(1)} collective-permute-done((f32[32,1024]{1,0:T(8,128)S(1)}, f32[32,1024]{1,0:T(8,128)S(1)}, u32[]{:S(2)}, u32[]{:S(2)}) %collective-permute-start.1) | collective-permute-done | bytes 131104 | tf_op jit(solution)/shard_map/ppermute | solution.py:360
  45.3 3.2 %collective-permute-done.3 = f32[32,1024]{1,0:T(8,128)S(1)} collective-permute-done((f32[32,1024]{1,0:T(8,128)S(1)}, f32[32,1024]{1,0:T(8,128)S(1)}, u32[]{:S(2)}, u32[]{:S(2)}) %collective-permute-start.3) | collective-permute-done | bytes 131104 | tf_op jit(solution)/shard_map/ppermute | solution.py:360
  48.5 0.1 collective-permute-start.4
  48.5 0.7 fusion.8
  53.4 0.1 fusion.4
  53.5 0.7 pad_maximum_fusion.1.coef_ref
  54.2 0.6 copy-done.15
  54.8 0.2 copy-done.8
  54.9 16.8 %filter.2 = (f32[4,8,8,1024]{3,2,1,0:T(8,128)}, f32[32,8,8,128]{3,2,1,0:T(8,128)}) custom-call(f32[35]{0:T(128)} %pad_maximum_fusion.1.coef_ref, s32[1]{0:T(128)} %bitcast.6.me_ref, f32[8,32,1024]{2,1,0:T(8,128)} %all_to_all.20.vec_ref, f32[32,1024]{1,0:T(8,128)} %copy-done.4, f32[32,1024]{1,0:T(8,128)} %copy-done.15, f32[3,32,1024]{2,1,0:T(8,128)} %copy-done.3, ...), custom_call_target="tpu_custom_call" | custom-call | tf_op jit(solution)/shard_map/filter/pallas_call | solution.py:383
  71.7 1.0 copy-done.2
  72.7 14.6 %filter.3 = f32[4,8,8,1024]{3,2,1,0:T(8,128)} custom-call(f32[35]{0:T(128)} %pad_maximum_fusion.1.coef_ref, s32[1]{0:T(128)} %bitcast.6.me_ref, f32[8,32,1024]{2,1,0:T(8,128)} %copy-done.2, f32[32,8,8,128]{3,2,1,0:T(8,128)} %get-tuple-element.13.rest_0_), custom_call_target="tpu_custom_call" | custom-call | tf_op jit(solution)/shard_map/filter/pallas_call | solution.py:383
  87.3 30.3 %all_to_all.21.refs_1_ = f32[32,8,1024]{2,1,0:T(8,128)S(1)} all-to-all(f32[32,8,1024]{2,1,0:T(8,128)} %bitcast.26), channel_id=1, replica_groups=mesh['strip'=8,'vec'=4] {'vec','strip'}, dimensions={0} | all-to-all | bytes 2097152 | tf_op jit(solution)/shard_map/all_to_all | solution.py:404
  117.6 3.6 %all-to-all-start.1 = ((f32[32,8,1024]{2,1,0:T(8,128)}), f32[32,8,1024]{2,1,0:T(8,128)S(1)}, u32[]{:S(2)}, u32[]{:S(2)}) async-start(f32[32,8,1024]{2,1,0:T(8,128)} %bitcast.10), calls=%async_computation.1 | async-start | bytes 2097152 | tf_op jit(solution)/shard_map/all_to_all | solution.py:404
  121.3 5.3 %collective-permute-start.6 = (f32[32,1024]{1,0:T(8,128)S(1)}, f32[32,1024]{1,0:T(8,128)S(1)}, u32[]{:S(2)}, u32[]{:S(2)}) collective-permute-start(f32[32,1024]{1,0:T(8,128)S(1)} %bitcast.27), channel_id=1, source_target_pairs={{1,0},{2,1},{3,2},{4,3},{5,4},{6,5},{7,6},{8,7},{9,8},{10,9},{11,1... | collective-permute-start | bytes 393224 | tf_op jit(solution)/shard_map/ppermute | solution.py:408
  126.6 21.4 %all-to-all-done.1.refs_0_ = f32[32,8,1024]{2,1,0:T(8,128)S(1)} async-done(((f32[32,8,1024]{2,1,0:T(8,128)}), f32[32,8,1024]{2,1,0:T(8,128)S(1)}, u32[]{:S(2)}, u32[]{:S(2)}) %all-to-all-start.1) | async-done | bytes 1048608 | tf_op jit(solution)/shard_map/all_to_all | solution.py:404
  148.1 5.4 %collective-permute-start.5 = (f32[32,1024]{1,0:T(8,128)S(1)}, f32[32,1024]{1,0:T(8,128)S(1)}, u32[]{:S(2)}, u32[]{:S(2)}) collective-permute-start(f32[32,1024]{1,0:T(8,128)S(1)} %bitcast.28), channel_id=1, source_target_pairs={{1,0},{2,1},{3,2},{4,3},{5,4},{6,5},{7,6},{8,7},{9,8},{10,9},{11,1... | collective-permute-start | bytes 393224 | tf_op jit(solution)/shard_map/ppermute | solution.py:408
  153.5 1.4 constant_dynamic-slice_fusion.refs_2_
  154.9 7.0 %gram.1 = (f32[64,128]{1,0:T(8,128)}, f32[8,64,1024]{2,1,0:T(8,128)}) custom-call(f32[32,8,1024]{2,1,0:T(8,128)} %copy-done.1, f32[32,8,1024]{2,1,0:T(8,128)} %copy-done, f32[8,1024]{1,0:T(8,128)} %constant_dynamic-slice_fusion.refs_2_), custom_call_target="tpu_custom_call" | custom-call | tf_op jit(solution)/shard_map/gram/pallas_call | solution.py:414
  161.9 0.6 copy-done.11
  162.5 2.4 edge.1
  164.9 1.4 collective-permute-done.7
  166.3 0.8 add.43
  167.1 3.9 %collective-permute-done.8 = f32[64,128]{1,0:T(8,128)S(1)} collective-permute-done((f32[64,128]{1,0:T(8,128)S(1)}, f32[64,128]{1,0:T(8,128)S(1)}, u32[]{:S(2)}, u32[]{:S(2)}) %collective-permute-start.8) | collective-permute-done | bytes 32800 | tf_op jit(solution)/shard_map/ppermute | solution.py:437
  171.0 3.9 %collective-permute-done.9 = f32[64,128]{1,0:T(8,128)S(1)} collective-permute-done((f32[64,128]{1,0:T(8,128)S(1)}, f32[64,128]{1,0:T(8,128)S(1)}, u32[]{:S(2)}, u32[]{:S(2)}) %collective-permute-start.9) | collective-permute-done | bytes 32800 | tf_op jit(solution)/shard_map/ppermute | solution.py:437
  174.9 3.9 %collective-permute-done.10 = f32[64,128]{1,0:T(8,128)S(1)} collective-permute-done((f32[64,128]{1,0:T(8,128)S(1)}, f32[64,128]{1,0:T(8,128)S(1)}, u32[]{:S(2)}, u32[]{:S(2)}) %collective-permute-start.10) | collective-permute-done | bytes 32800 | tf_op jit(solution)/shard_map/ppermute | solution.py:437
  178.9 4.9 %collective-permute-done.11.other_ref = f32[64,128]{1,0:T(8,128)S(1)} collective-permute-done((f32[64,128]{1,0:T(8,128)S(1)}, f32[64,128]{1,0:T(8,128)S(1)}, u32[]{:S(2)}, u32[]{:S(2)}) %collective-permute-start.11) | collective-permute-done | bytes 32800 | tf_op jit(solution)/shard_map/ppermute | solution.py:437
  183.9 0.6 copy-done.16
  184.5 9.1 %solve.1 = (f32[64,64]{1,0:T(8,128)}, f32[64,128]{1,0:T(8,128)}, f32[16,8,1024]{2,1,0:T(8,128)}, f32[16,8,1024]{2,1,0:T(8,128)}) custom-call(s32[1]{0:T(128)} %bitcast.place_ref, f32[64,128]{1,0:T(8,128)} %copy-done.10, f32[64,128]{1,0:T(8,128)} %copy-done.16, f32[8,64,1024]{2,1,0:T(8,128)} %get-tuple-element.15.refs_3_.lines_ref), custom_call_target="tpu_custom_call" | custom-call | tf_op jit(solution)/shard_map/solve/pallas_call | solution.py:445
  193.6 3.7 %near.1 = (f32[16,8,1024]{2,1,0:T(8,128)}, f32[16,8,1024]{2,1,0:T(8,128)}) custom-call(s32[1]{0:T(128)} %bitcast.place_ref, f32[64,64]{1,0:T(8,128)} %get-tuple-element.18.inv_ref, f32[8,64,1024]{2,1,0:T(8,128)} %get-tuple-element.15.refs_3_.lines_ref), custom_call_target="tpu_custom_call" | custom-call | tf_op jit(solution)/shard_map/near/pallas_call | solution.py:453
  197.4 0.2 collective-permute-start.14
  197.6 4.2 %collective-permute-start.13 = (f32[16,8,1024]{2,1,0:T(8,128)S(1)}, f32[16,8,1024]{2,1,0:T(8,128)S(1)}, u32[]{:S(2)}, u32[]{:S(2)}) collective-permute-start(f32[16,8,1024]{2,1,0:T(8,128)S(1)} %copy-done.17), channel_id=1, source_target_pairs={{0,3},{1,2},{2,1},{3,0},{4,7},{5,6},{6,5},{7,4},{8,11},{9,10},{10,... | collective-permute-start | bytes 1572872 | tf_op jit(solution)/shard_map/ppermute | solution.py:463
  201.8 0.1 slice.37
  201.8 0.1 copy.13
  201.9 0.2 fusion.1
  202.2 0.8 convolution_multiply_fusion
  203.0 13.6 %collective-permute-done.14.refs_1_ = f32[16,8,1024]{2,1,0:T(8,128)S(1)} collective-permute-done((f32[16,8,1024]{2,1,0:T(8,128)}, f32[16,8,1024]{2,1,0:T(8,128)S(1)}, u32[]{:S(2)}, u32[]{:S(2)}) %collective-permute-start.14) | collective-permute-done | bytes 524320 | tf_op jit(solution)/shard_map/ppermute | solution.py:463
  216.6 0.8 copy-done.5
  217.4 2.2 place_near.1.refs_2_
  219.5 16.2 %collective-permute-done.12.refs_0_ = f32[16,8,1024]{2,1,0:T(8,128)S(1)} collective-permute-done((f32[16,8,1024]{2,1,0:T(8,128)S(1)}, f32[16,8,1024]{2,1,0:T(8,128)S(1)}, u32[]{:S(2)}, u32[]{:S(2)}) %collective-permute-start.12) | collective-permute-done | bytes 524320 | tf_op jit(solution)/shard_map/ppermute | solution.py:463
  235.8 0.8 copy-done.6
  236.5 0.8 copy-done.7
  237.4 2.2 place_far.1
  (57 shorter events, 0.5 us)
Async XLA Ops:
  3.3 24.1 %copy-start.13 = (s32[32,1024]{1,0:T(8,128)S(1)}, s32[32,1024]{1,0:T(8,128)}, u32[]{:S(2)}) copy-start(s32[32,1024]{1,0:T(8,128)} %param.4) | copy-start | bytes 393220
  3.3 27.7 %copy-start.19 = (s32[4]{0:T(128)S(1)}, s32[4]{0:T(128)}, u32[]{:S(2)}) copy-start(s32[4]{0:T(128)} %param.5) | copy-start | bytes 52
  23.9 47.8 %all-to-all-start.2 = ((f32[8,32,1024]{2,1,0:T(8,128)}), f32[8,32,1024]{2,1,0:T(8,128)S(1)}, u32[]{:S(2)}, u32[]{:S(2)}) async-start(f32[8,32,1024]{2,1,0:T(8,128)} %get-tuple-element.22), calls=%async_computation.2 | async-start | bytes 2097152 | tf_op jit(solution)/shard_map/all_to_all | solution.py:365
  27.5 26.7 %copy-start.4 = (f32[32,1024]{1,0:T(8,128)}, f32[32,1024]{1,0:T(8,128)S(1)}, u32[]{:S(2)}) copy-start(f32[32,1024]{1,0:T(8,128)S(1)} %convert_element_type.15.rest_0_) | copy-start | bytes 393220
  27.5 17.8 %collective-permute-start.1 = (f32[32,1024]{1,0:T(8,128)S(1)}, f32[32,1024]{1,0:T(8,128)S(1)}, u32[]{:S(2)}, u32[]{:S(2)}) collective-permute-start(f32[32,1024]{1,0:T(8,128)S(1)} %convert_element_type.15.rest_0_), channel_id=1, source_target_pairs={{0,8},{4,12},{8,0},{12,4},{16,24},{20,28},{24,16},{28,20},{1,9},{5... | collective-permute-start | bytes 393224 | tf_op jit(solution)/shard_map/ppermute | solution.py:360
  29.5 15.8 %collective-permute-start.2 = (f32[32,1024]{1,0:T(8,128)S(1)}, f32[32,1024]{1,0:T(8,128)S(1)}, u32[]{:S(2)}, u32[]{:S(2)}) collective-permute-start(f32[32,1024]{1,0:T(8,128)S(1)} %convert_element_type.15.rest_0_), channel_id=1, source_target_pairs={{0,16},{4,20},{8,24},{12,28},{16,0},{20,4},{24,8},{28,12},{1,17},{... | collective-permute-start | bytes 393224 | tf_op jit(solution)/shard_map/ppermute | solution.py:360
  31.0 17.5 %collective-permute-start.3 = (f32[32,1024]{1,0:T(8,128)S(1)}, f32[32,1024]{1,0:T(8,128)S(1)}, u32[]{:S(2)}, u32[]{:S(2)}) collective-permute-start(f32[32,1024]{1,0:T(8,128)S(1)} %convert_element_type.15.rest_0_), channel_id=1, source_target_pairs={{0,24},{4,28},{8,16},{12,20},{16,8},{20,12},{24,0},{28,4},{1,25},{... | collective-permute-start | bytes 393224 | tf_op jit(solution)/shard_map/ppermute | solution.py:360
  31.1 23.1 %collective-permute-start = (f32[32,1024]{1,0:T(8,128)S(1)}, f32[32,1024]{1,0:T(8,128)S(1)}, u32[]{:S(2)}, u32[]{:S(2)}) collective-permute-start(f32[32,1024]{1,0:T(8,128)S(1)} %convert_element_type.15.rest_0_), channel_id=1, source_target_pairs={{0,4},{4,0},{8,12},{12,8},{16,20},{20,16},{24,28},{28,24},{1,5},{5... | collective-permute-start | bytes 393224 | tf_op jit(solution)/shard_map/ppermute | solution.py:360
  48.5 5.7 %copy-start.3 = (f32[3,32,1024]{2,1,0:T(8,128)}, f32[3,32,1024]{2,1,0:T(8,128)S(1)}, u32[]{:S(2)}) copy-start(f32[3,32,1024]{2,1,0:T(8,128)S(1)} %pad_maximum_fusion.rest_2_) | copy-start | bytes 1179652
  48.5 5.7 %collective-permute-start.4 = (f32[3,32,1024]{2,1,0:T(8,128)S(1)}, f32[3,32,1024]{2,1,0:T(8,128)S(1)}, u32[]{:S(2)}, u32[]{:S(2)}) collective-permute-start(f32[3,32,1024]{2,1,0:T(8,128)S(1)} %pad_maximum_fusion.rest_2_), channel_id=1, source_target_pairs={{0,4},{4,0},{8,12},{12,8},{16,20},{20,16},{24,28},{28,24},{1,5},{5... | collective-permute-start | bytes 1179656 | tf_op jit(solution)/shard_map/ppermute | solution.py:360
  54.1 0.6 copy-start.15
  54.1 0.8 copy-start.8
  71.7 1.0 copy-start.2
  117.6 37.3 %copy-start = (f32[32,8,1024]{2,1,0:T(8,128)}, f32[32,8,1024]{2,1,0:T(8,128)S(1)}, u32[]{:S(2)}) copy-start(f32[32,8,1024]{2,1,0:T(8,128)S(1)} %all_to_all.21.refs_1_) | copy-start | bytes 3145732
  117.6 30.4 %all-to-all-start.1 = ((f32[32,8,1024]{2,1,0:T(8,128)}), f32[32,8,1024]{2,1,0:T(8,128)S(1)}, u32[]{:S(2)}, u32[]{:S(2)}) async-start(f32[32,8,1024]{2,1,0:T(8,128)} %bitcast.10), calls=%async_computation.1 | async-start | bytes 2097152 | tf_op jit(solution)/shard_map/all_to_all | solution.py:404
  121.3 40.5 %collective-permute-start.6 = (f32[32,1024]{1,0:T(8,128)S(1)}, f32[32,1024]{1,0:T(8,128)S(1)}, u32[]{:S(2)}, u32[]{:S(2)}) collective-permute-start(f32[32,1024]{1,0:T(8,128)S(1)} %bitcast.27), channel_id=1, source_target_pairs={{1,0},{2,1},{3,2},{4,3},{5,4},{6,5},{7,6},{8,7},{9,8},{10,9},{11,1... | collective-permute-start | bytes 393224 | tf_op jit(solution)/shard_map/ppermute | solution.py:408
  148.0 6.9 %copy-start.1 = (f32[32,8,1024]{2,1,0:T(8,128)}, f32[32,8,1024]{2,1,0:T(8,128)S(1)}, u32[]{:S(2)}) copy-start(f32[32,8,1024]{2,1,0:T(8,128)S(1)} %all-to-all-done.1.refs_0_) | copy-start | bytes 3145732
  148.1 13.8 %collective-permute-start.5 = (f32[32,1024]{1,0:T(8,128)S(1)}, f32[32,1024]{1,0:T(8,128)S(1)}, u32[]{:S(2)}, u32[]{:S(2)}) collective-permute-start(f32[32,1024]{1,0:T(8,128)S(1)} %bitcast.28), channel_id=1, source_target_pairs={{1,0},{2,1},{3,2},{4,3},{5,4},{6,5},{7,6},{8,7},{9,8},{10,9},{11,1... | collective-permute-start | bytes 393224 | tf_op jit(solution)/shard_map/ppermute | solution.py:408
  161.8 0.7 copy-start.11
  161.9 0.7 copy-start.12
  164.9 1.4 collective-permute-start.7
  167.1 3.9 %collective-permute-start.8 = (f32[64,128]{1,0:T(8,128)S(1)}, f32[64,128]{1,0:T(8,128)S(1)}, u32[]{:S(2)}, u32[]{:S(2)}) collective-permute-start(f32[64,128]{1,0:T(8,128)S(1)} %add.43), channel_id=1, source_target_pairs={{0,8},{4,12},{8,0},{12,4},{16,24},{20,28},{24,16},{28,20},{1,9},{5... | collective-permute-start | bytes 98312 | tf_op jit(solution)/shard_map/ppermute | solution.py:437
  171.0 3.9 %collective-permute-start.9 = (f32[64,128]{1,0:T(8,128)S(1)}, f32[64,128]{1,0:T(8,128)S(1)}, u32[]{:S(2)}, u32[]{:S(2)}) collective-permute-start(f32[64,128]{1,0:T(8,128)S(1)} %add.44), channel_id=1, source_target_pairs={{0,16},{4,20},{8,24},{12,28},{16,0},{20,4},{24,8},{28,12},{1,17},{... | collective-permute-start | bytes 98312 | tf_op jit(solution)/shard_map/ppermute | solution.py:437
  174.9 3.9 %collective-permute-start.10 = (f32[64,128]{1,0:T(8,128)S(1)}, f32[64,128]{1,0:T(8,128)S(1)}, u32[]{:S(2)}, u32[]{:S(2)}) collective-permute-start(f32[64,128]{1,0:T(8,128)S(1)} %add.45), channel_id=1, source_target_pairs={{0,1},{1,0},{2,3},{3,2},{4,5},{5,4},{6,7},{7,6},{8,9},{9,8},{10,11... | collective-permute-start | bytes 98312 | tf_op jit(solution)/shard_map/ppermute | solution.py:437
  178.8 5.0 %copy-start.10 = (f32[64,128]{1,0:T(8,128)}, f32[64,128]{1,0:T(8,128)S(1)}, u32[]{:S(2)}) copy-start(f32[64,128]{1,0:T(8,128)S(1)} %add.46.mine_ref) | copy-start | bytes 98308
  178.9 5.0 %collective-permute-start.11 = (f32[64,128]{1,0:T(8,128)S(1)}, f32[64,128]{1,0:T(8,128)S(1)}, u32[]{:S(2)}, u32[]{:S(2)}) collective-permute-start(f32[64,128]{1,0:T(8,128)S(1)} %add.46.mine_ref), channel_id=1, source_target_pairs={{0,2},{1,3},{2,0},{3,1},{4,6},{5,7},{6,4},{7,5},{8,10},{9,11},{10,... | collective-permute-start | bytes 98312 | tf_op jit(solution)/shard_map/ppermute | solution.py:437
  183.9 0.6 copy-start.16
  193.6 4.0 %copy-start.18 = (f32[16,8,1024]{2,1,0:T(8,128)S(1)}, f32[16,8,1024]{2,1,0:T(8,128)}, u32[]{:S(2)}) copy-start(f32[16,8,1024]{2,1,0:T(8,128)} %get-tuple-element.16) | copy-start | bytes 1572868
  193.6 4.0 %copy-start.17 = (f32[16,8,1024]{2,1,0:T(8,128)S(1)}, f32[16,8,1024]{2,1,0:T(8,128)}, u32[]{:S(2)}) copy-start(f32[16,8,1024]{2,1,0:T(8,128)} %get-tuple-element.17) | copy-start | bytes 1572868
  193.6 8.1 %copy-start.14 = (f32[64,128]{1,0:T(8,128)S(1)}, f32[64,128]{1,0:T(8,128)}, u32[]{:S(2)}) copy-start(f32[64,128]{1,0:T(8,128)} %get-tuple-element.21) | copy-start | bytes 98308
  193.6 8.3 %copy-start.9 = (f32[64,64]{1,0:T(8,128)S(1)}, f32[64,64]{1,0:T(8,128)}, u32[]{:S(2)}) copy-start(f32[64,64]{1,0:T(8,128)} %get-tuple-element.18.inv_ref) | copy-start | bytes 49156
  197.4 19.2 %collective-permute-start.14 = (f32[16,8,1024]{2,1,0:T(8,128)}, f32[16,8,1024]{2,1,0:T(8,128)S(1)}, u32[]{:S(2)}, u32[]{:S(2)}) collective-permute-start(f32[16,8,1024]{2,1,0:T(8,128)} %get-tuple-element.20), channel_id=1, source_target_pairs={{0,1},{1,0},{2,3},{3,2},{4,5},{5,4},{6,7},{7,6},{8,9},{9,8},{10,11... | collective-permute-start | bytes 1572872 | tf_op jit(solution)/shard_map/ppermute | solution.py:463
  197.6 38.2 %collective-permute-start.12 = (f32[16,8,1024]{2,1,0:T(8,128)S(1)}, f32[16,8,1024]{2,1,0:T(8,128)S(1)}, u32[]{:S(2)}, u32[]{:S(2)}) collective-permute-start(f32[16,8,1024]{2,1,0:T(8,128)S(1)} %copy-done.18), channel_id=1, source_target_pairs={{0,2},{1,3},{2,0},{3,1},{4,6},{5,7},{6,4},{7,5},{8,10},{9,11},{10,... | collective-permute-start | bytes 1572872 | tf_op jit(solution)/shard_map/ppermute | solution.py:463
  197.6 38.2 %collective-permute-start.13 = (f32[16,8,1024]{2,1,0:T(8,128)S(1)}, f32[16,8,1024]{2,1,0:T(8,128)S(1)}, u32[]{:S(2)}, u32[]{:S(2)}) collective-permute-start(f32[16,8,1024]{2,1,0:T(8,128)S(1)} %copy-done.17), channel_id=1, source_target_pairs={{0,3},{1,2},{2,1},{3,0},{4,7},{5,6},{6,5},{7,4},{8,11},{9,10},{10,... | collective-permute-start | bytes 1572872 | tf_op jit(solution)/shard_map/ppermute | solution.py:463
  216.6 0.8 copy-start.5
  235.7 0.8 copy-start.6
  236.5 0.8 copy-start.7

commit v2 on v1

--- a/solution.py
+++ b/solution.py
@@ -107,54 +107,58 @@
     return (ortho_basis, ritz_matrix)
 
 
-def filter_kernel(coef_ref, me_ref, vec_ref, *rest, slabs, first):
-    if first:
-        here_ref, beside_ref, own_ref, other_ref, out_ref, site, pot_ref, sems, flip, grid, field, state_a, state_b = rest
-    else:
-        site, out_ref, flip, grid, field, state_a, state_b = rest
+def stage(read, flip, grid, target, change, rows, strips):
+    parts, total_rows, lanes = grid.shape
+    blocks = total_rows // lanes
+    per_block = lanes // rows
+    for part in range(parts):
+        for block in range(blocks):
+            tile = jnp.concatenate(
+                [read(block * per_block + p, part * lanes) for p in range(per_block)], axis=0
+            )
+            flip[block, part * lanes : (part + 1) * lanes, :] = tile.T
+    for part in range(parts):
+        for block in range(blocks):
+            tile = flip[block, pl.ds(part, lanes, stride=parts), :]
+            grid[part, block * lanes : (block + 1) * lanes, :] = tile.T
+    for j in range(rows):
+        for part in range(parts):
+            target(j, part, change(grid[part, pl.ds(j, strips, stride=rows), :]))
+
+
+def site_kernel(coef_ref, me_ref, here_ref, beside_ref, own_ref, other_ref, site, pot_ref, sems, flip, grid):
+    rows, _, strips, lanes = site.shape
+    center = coef_ref[DEGREE + 1]
+    me = me_ref[0]
+    sources = [here_ref, beside_ref]
+    for d in range(2, strips):
+        sources.append((own_ref, other_ref)[d & 1].at[(d >> 1) - 1])
+    copies = [pltpu.make_async_copy(sources[d], pot_ref.at[me ^ d], sems.at[d]) for d in range(strips)]
+    for copy in copies:
+        copy.start()
+    for copy in copies:
+        copy.wait()
+
+    def put_site(j, part, value):
+        site[j, part] = value
+
+    stage(
+        lambda p, start: pot_ref[p, :, start : start + lanes],
+        flip,
+        grid,
+        put_site,
+        lambda level: disorder * (level * (1.0 / (POT_LEVELS - 1)) - 0.5) - center,
+        rows,
+        strips,
+    )
+
+
+def filter_kernel(coef_ref, vec_ref, site, out_ref, flip, grid, field, state_a, state_b, *, slabs):
     rows, parts, strips, lanes = field.shape
     total_rows = rows * strips
     blocks = total_rows // lanes
     per_block = lanes // rows
     slab_rows = rows // slabs
-    center = coef_ref[DEGREE + 1]
-
-    def stage(read, target, change):
-        for part in range(parts):
-            for block in range(blocks):
-                tile = jnp.concatenate(
-                    [read(block * per_block + p, part * lanes) for p in range(per_block)], axis=0
-                )
-                flip[block, part * lanes : (part + 1) * lanes, :] = tile.T
-        for part in range(parts):
-            for block in range(blocks):
-                tile = flip[block, pl.ds(part, lanes, stride=parts), :]
-                grid[part, block * lanes : (block + 1) * lanes, :] = tile.T
-
-        for j in range(rows):
-            for part in range(parts):
-                target(j, part, change(grid[part, pl.ds(j, strips, stride=rows), :]))
-
-    def put_site(j, part, value):
-        site[j, part] = value
-
-    if first:
-        me = me_ref[0]
-        sources = [here_ref, beside_ref]
-        for d in range(2, strips):
-            sources.append((own_ref, other_ref)[d & 1].at[(d >> 1) - 1])
-        copies = [
-            pltpu.make_async_copy(sources[d], pot_ref.at[me ^ d], sems.at[d]) for d in range(strips)
-        ]
-        for copy in copies:
-            copy.start()
-        for copy in copies:
-            copy.wait()
-        stage(
-            lambda p, start: pot_ref[p, :, start : start + lanes],
-            put_site,
-            lambda level: disorder * (level * (1.0 / (POT_LEVELS - 1)) - 0.5) - center,
-        )
     top = coef_ref[DEGREE]
 
     def put_field(j, part, value):
@@ -162,7 +166,15 @@
         state_a[j + 1, part] = top * value
         state_b[j + 1, part] = jnp.zeros_like(value)
 
-    stage(lambda p, start: vec_ref[p, :, start : start + lanes], put_field, lambda value: value)
+    stage(
+        lambda p, start: vec_ref[p, :, start : start + lanes],
+        flip,
+        grid,
+        put_field,
+        lambda value: value,
+        rows,
+        strips,
+    )
 
     def wrap(state):
         for part in range(parts):
@@ -238,7 +250,7 @@
 
 def gram_kernel(*refs, chunks):
     slab_refs = refs[:chunks]
-    pot_ref, out_ref, lines_ref = refs[chunks:]
+    place_ref, pot_ref, out_ref, lines_ref = refs[chunks:]
     slab_rows, total, columns = lines_ref.shape
     acc = jnp.zeros(out_ref.shape, jnp.float32)
     for chunk in range(chunks):
@@ -246,9 +258,10 @@
             here = slice(group * SUBLANES, (group + 1) * SUBLANES)
             start = (group * chunks + chunk) * SUBLANES
             lines_ref[:, start : start + SUBLANES, :] = jnp.swapaxes(slab_refs[chunk][here], 0, 1)
+    levels = pot_ref[pl.ds(pl.multiple_of(place_ref[0] * slab_rows, SUBLANES), slab_rows), :]
     for j in range(slab_rows):
         here = lines_ref[j]
-        level = pot_ref[j : j + 1, :]
+        level = levels[j : j + 1, :]
         pot = disorder * (level * (1.0 / (POT_LEVELS - 1)) - 0.5)
         image = pot * here - (pltpu.roll(here, 1, 1) + pltpu.roll(here, columns - 1, 1))
         if j < slab_rows - 1:
@@ -259,15 +272,13 @@
 
 def edge_kernel(*refs, chunks):
     next_refs = refs[:chunks]
-    sums_ref, last_ref, out_ref = refs[chunks:]
-    total = sums_ref.shape[0]
+    last_ref, out_ref = refs[chunks:]
+    total = out_ref.shape[0]
     parts = []
     for group in range(total // (chunks * SUBLANES)):
         for chunk in range(chunks):
             parts.append(next_refs[chunk][group * SUBLANES : (group + 1) * SUBLANES, :])
-    below = jnp.concatenate(parts, axis=0)
-    both = jnp.concatenate([jnp.zeros_like(below), below], axis=0)
-    out_ref[...] = sums_ref[...] - 2.0 * outer(last_ref[0], both)
+    out_ref[...] = -2.0 * outer(last_ref[0], jnp.concatenate(parts, axis=0))
 
 
 def eliminate(sums):
@@ -326,19 +337,6 @@
     products(inv_ref, lines_ref, rest[-1], rest[:-1], place_ref[0], scale, targets, half)
 
 
-def place_kernel(place_ref, *refs, targets):
-    out_ref, sems = refs[-2:]
-    slab_rows = refs[0].shape[1]
-    copies = []
-    for n, d in enumerate(targets):
-        start = pl.multiple_of((place_ref[0] ^ d) * slab_rows, SUBLANES)
-        copies.append(pltpu.make_async_copy(refs[n], out_ref.at[:, pl.ds(start, slab_rows), :], sems.at[n]))
-    for copy in copies:
-        copy.start()
-    for copy in copies:
-        copy.wait()
-
-
 def whole_shards(start_vectors, potential, bounds):
     vec_local, rows, columns = start_vectors.shape
     strips = lax.axis_size("strip")
@@ -360,13 +358,19 @@
         return lax.ppermute(value, "strip", [(i, i ^ bit) for i in range(strips)])
 
     inner = []
-    for chunk in range(vecs):
-        part = start_vectors[chunk * strips : (chunk + 1) * strips]
+
+    def spread(vectors, chunk):
+        part = vectors[chunk * strips : (chunk + 1) * strips]
         inner.append(lax.all_to_all(part, "strip", split_axis=0, concat_axis=0, tiled=True))
+
+    spread(start_vectors, 0)
     beside = swap(level, 1)
     pieces = [swap(level, bit) for bit in range(2, strips, 2)]
     own_pots = jnp.stack(pieces)
     other_pots = swap(own_pots, 1)
+    later, _ = lax.optimization_barrier((start_vectors, own_pots))
+    for chunk in range(1, vecs):
+        spread(later, chunk)
 
     parts = columns // LANES
     lattice = (rows, parts, strips, LANES)
@@ -375,67 +379,71 @@
     vmem = pl.BlockSpec(memory_space=pltpu.VMEM)
     hbm = pl.BlockSpec(memory_space=pl.ANY)
     slab_shape = jax.ShapeDtypeStruct((groups, strips, slab_rows, columns), jnp.float32)
-    site = None
+    staging = [
+        pltpu.VMEM((strips * rows // LANES, columns, LANES), jnp.float32),
+        pltpu.VMEM((parts, strips * rows, LANES), jnp.float32),
+    ]
+    site = pl.pallas_call(
+        site_kernel,
+        in_specs=[smem, smem] + [hbm] * 4,
+        out_specs=vmem,
+        out_shape=jax.ShapeDtypeStruct(lattice, jnp.float32),
+        scratch_shapes=[
+            pltpu.VMEM((strips, rows, columns), jnp.float32),
+            pltpu.SemaphoreType.DMA((strips,)),
+        ]
+        + staging,
+        name="site",
+    )(terms, me[None], level, beside, own_pots, other_pots)
     slabs, nexts = [], []
     ring = [((i + 1) % devices, i) for i in range(devices)]
     for chunk in range(vecs):
-        first = chunk == 0
         done = pl.pallas_call(
-            functools.partial(filter_kernel, slabs=groups, first=first),
-            in_specs=[smem, smem, vmem] + ([hbm] * 4 if first else [vmem]),
-            out_specs=[vmem, vmem] if first else [vmem],
-            out_shape=[slab_shape] + ([jax.ShapeDtypeStruct(lattice, jnp.float32)] if first else []),
-            scratch_shapes=(
-                [pltpu.VMEM((strips, rows, columns), jnp.float32), pltpu.SemaphoreType.DMA((strips,))]
-                if first
-                else []
-            )
+            functools.partial(filter_kernel, slabs=groups),
+            in_specs=[smem, vmem, vmem],
+            out_specs=vmem,
+            out_shape=slab_shape,
+            scratch_shapes=staging
             + [
-                pltpu.VMEM((strips * rows // LANES, columns, LANES), jnp.float32),
-                pltpu.VMEM((parts, strips * rows, LANES), jnp.float32),
                 pltpu.VMEM(lattice, jnp.float32),
                 pltpu.VMEM(padded, jnp.float32),
                 pltpu.VMEM(padded, jnp.float32),
             ],
             name="filter",
-        )(terms, me[None], inner[chunk], *((level, beside, own_pots, other_pots) if first else (site,)))
-        if first:
-            site = done[1]
-        slab = lax.all_to_all(
-            done[0].reshape(devices, slab_rows, columns), both, split_axis=0, concat_axis=0, tiled=True
-        )
+        )(terms, inner[chunk], site)
+        slab = lax.all_to_all(done.reshape(devices, slab_rows, columns), both, split_axis=0, concat_axis=0, tiled=True)
         slabs.append(slab)
         nexts.append(lax.ppermute(slab[:, 0], ("strip", "vec"), ring))
 
     place = lax.axis_index("vec").astype(jnp.int32)
-    own_pot = lax.dynamic_slice_in_dim(level, place * slab_rows, slab_rows, axis=0)
     lines_shape = (slab_rows, total_vecs, columns)
     sums_shape = jax.ShapeDtypeStruct((total_vecs, 2 * total_vecs), jnp.float32)
     sums, lines = pl.pallas_call(
         functools.partial(gram_kernel, chunks=vecs),
-        in_specs=[vmem] * (vecs + 1),
+        in_specs=[vmem] * vecs + [smem, vmem],
         out_specs=[vmem, vmem],
         out_shape=[sums_shape, jax.ShapeDtypeStruct(lines_shape, jnp.float32)],
         name="gram",
-    )(*slabs, own_pot)
-    sums = pl.pallas_call(
+    )(*slabs, place[None], level)
+    edge = pl.pallas_call(
         functools.partial(edge_kernel, chunks=vecs),
         grid=(1,),
-        in_specs=[vmem] * (vecs + 1)
-        + [pl.BlockSpec((1, total_vecs, columns), lambda i: (slab_rows - 1, 0, 0))],
+        in_specs=[vmem] * vecs + [pl.BlockSpec((1, total_vecs, columns), lambda i: (slab_rows - 1, 0, 0))],
         out_specs=vmem,
-        out_shape=sums_shape,
+        out_shape=jax.ShapeDtypeStruct((total_vecs, total_vecs), jnp.float32),
         name="edge",
-    )(*nexts, sums, lines)
-
-    pending = None
-    for axis, count in (("strip", strips), ("vec", groups)):
-        bit = 1
-        while bit < count:
-            if pending is not None:
-                sums = sums + pending
-            pending = lax.ppermute(sums, axis, [(i, i ^ bit) for i in range(count)])
-            bit *= 2
+    )(*nexts, lines)
+
+    def pairwise(value, order):
+        rounds = [(axis, count, 1 << n) for axis, count in order for n in range(count.bit_length() - 1)]
+        for number, (axis, count, bit) in enumerate(rounds):
+            other = lax.ppermute(value, axis, [(i, i ^ bit) for i in range(count)])
+            if number < len(rounds) - 1:
+                value = value + other
+        return value, other
+
+    sums, pending = pairwise(sums, (("strip", strips), ("vec", groups)))
+    edge = sum(pairwise(edge, (("vec", groups), ("strip", strips))))
 
     scale = math.sqrt(strips * rows * columns)
     half = groups // 2
@@ -464,26 +472,12 @@
 
     far_blocks = [across(block, d) for d, block in zip(far, far_blocks)]
     near_blocks = [across(block, d) for d, block in zip(near, near_blocks)]
-    out_shape = jax.ShapeDtypeStruct((vec_local, rows, columns), jnp.float32)
-    ortho_basis = pl.pallas_call(
-        functools.partial(place_kernel, targets=near),
-        in_specs=[smem] + [vmem] * half,
-        out_specs=hbm,
-        out_shape=out_shape,
-        scratch_shapes=[pltpu.SemaphoreType.DMA((half,))],
-        name="place_near",
-    )(place[None], *near_blocks)
-    ortho_basis = pl.pallas_call(
-        functools.partial(place_kernel, targets=far),
-        in_specs=[smem] + [vmem] * half + [hbm],
-        out_specs=hbm,
-        out_shape=out_shape,
-        scratch_shapes=[pltpu.SemaphoreType.DMA((half,))],
-        input_output_aliases={half + 1: 0},
-        name="place_far",
-    )(place[None], *far_blocks, ortho_basis)
-
-    cross_half = gram_cross[:, total_vecs:]
+    ortho_basis = jnp.zeros((vec_local, rows, columns), jnp.float32)
+    for d, block in zip(near + far, near_blocks + far_blocks):
+        start = (place ^ d) * slab_rows
+        ortho_basis = lax.dynamic_update_slice(ortho_basis, block, (0, start, 0))
+
+    cross_half = gram_cross[:, total_vecs:] + edge
     cross_sum = 0.5 * (cross_half + cross_half.T)
     half_done = jnp.dot(inverse, cross_sum, precision=lax.Precision.HIGHEST)
     ritz_matrix = float(rows) * jnp.dot(inverse, half_done.T, precision=lax.Precision.HIGHEST)

time: 243 us -> 223 us (0.918)
  the two profiles are of different devices: /device:TPU:0 before, /device:TPU:10 now
where the time goes in v2:
time: 223 us; the launch traced here: 222 us
  waiting for transfers between devices  108 us (48%)
  Pallas kernels  55.3 us (25%)
  starting transfers between devices  40.8 us (18%)
  local copies, waits for them, and re-layouts  9.25 us (4%)
  between operations  5.19 us (2%)
  other arithmetic  3.12 us (1%)
    ppermute x3, waiting for transfers between devices, across(): lax.ppermute(block, 'vec', [(i, i ^ d) for i in range(groups)])  39.1 us
    all_to_all x2, waiting for transfers between devices, whole_shards(): lax.all_to_all(done.reshape(devices, slab_rows, columns), both, split_axi...  35.3 us
    pallas_call x2, Pallas kernels, whole_shards(): pl.pallas_call(functools.partial(filter_kernel, slabs=groups), in_specs=[...  29.2 us
    ppermute x10, waiting for transfers between devices, pairwise(): other = lax.ppermute(value, axis, [(i, i ^ bit) for i in range(count)])  17.9 us
    ppermute x5, waiting for transfers between devices, swap(): return lax.ppermute(value, 'strip', [(i, i ^ bit) for i in range(strips)])  15.4 us
    all_to_all x2, starting transfers between devices, whole_shards(): lax.all_to_all(done.reshape(devices, slab_rows, columns), both, split_axi...  11.2 us
    ppermute x10, starting transfers between devices, pairwise(): other = lax.ppermute(value, axis, [(i, i ^ bit) for i in range(count)])  10.8 us
    all_to_all x2, starting transfers between devices, spread(): lax.all_to_all(part, 'strip', split_axis=0, concat_axis=0, tiled=True)  9.32 us
  transfers between devices with their start and end apart: 24, of which 15 were waited for; matrix products, arithmetic and copies ran while one was open for 3% of the time, Pallas kernels for 25%

profile of v2, /device:TPU:10, one launch (start us, length us, event | category | flops | bytes accessed | tf_op | source)
XLA Modules:
  0.0 222.3 jit_solution(10699886013395762861)
XLA Ops:
  0.6 2.3 %slice.33 = f32[8,32,1024]{2,1,0:T(8,128)} slice(f32[16,32,1024]{2,1,0:T(8,128)} %param.3), slice={[0:8], [0:32], [0:1024]} | slice | bytes 2097152 | tf_op jit(solution)/shard_map/slice | solution.py:363
  3.0 4.4 %all-to-all-start = ((f32[8,32,1024]{2,1,0:T(8,128)}), f32[8,32,1024]{2,1,0:T(8,128)S(1)}, u32[]{:S(2)}, u32[]{:S(2)}) async-start(f32[8,32,1024]{2,1,0:T(8,128)} %slice.33), calls=%async_computation | async-start | bytes 2097152 | tf_op jit(solution)/shard_map/all_to_all | solution.py:364
  7.4 0.7 convert_element_type.15.here_ref.refs_3_
  8.0 2.0 collective-permute-start.2
  10.1 1.5 collective-permute-start.3
  11.5 11.7 %collective-permute-done.1 = f32[32,1024]{1,0:T(8,128)S(1)} collective-permute-done((f32[32,1024]{1,0:T(8,128)}, f32[32,1024]{1,0:T(8,128)S(1)}, u32[]{:S(2)}, u32[]{:S(2)}) %collective-permute-start.1) | collective-permute-done | bytes 131104 | tf_op jit(solution)/shard_map/ppermute | solution.py:358
  23.2 1.3 collective-permute-done.2
  24.5 2.4 %collective-permute-done.3 = f32[32,1024]{1,0:T(8,128)S(1)} collective-permute-done((f32[32,1024]{1,0:T(8,128)}, f32[32,1024]{1,0:T(8,128)S(1)}, u32[]{:S(2)}, u32[]{:S(2)}) %collective-permute-start.3) | collective-permute-done | bytes 131104 | tf_op jit(solution)/shard_map/ppermute | solution.py:358
  27.0 1.1 slice.34
  28.1 4.9 %all-to-all-start.2 = ((f32[8,32,1024]{2,1,0:T(8,128)}), f32[8,32,1024]{2,1,0:T(8,128)S(1)}, u32[]{:S(2)}, u32[]{:S(2)}) async-start(f32[8,32,1024]{2,1,0:T(8,128)} %slice.34), calls=%async_computation.2 | async-start | bytes 2097152 | tf_op jit(solution)/shard_map/all_to_all | solution.py:364
  33.6 0.7 fusion.6
  38.7 0.7 pad_maximum_fusion.1.coef_ref
  39.4 0.6 copy-done.14
  40.2 4.3 %site.1 = f32[32,8,8,128]{3,2,1,0:T(8,128)} custom-call(f32[35]{0:T(128)} %pad_maximum_fusion.1.coef_ref, s32[1]{0:T(128)} %bitcast.6.me_ref, f32[32,1024]{1,0:T(8,128)} %convert_element_type.15.here_ref.refs_3_, f32[32,1024]{1,0:T(8,128)} %copy-done.14, f32[3,32,1024]{2,1,0:T(8,128)} %copy-done.6, f32[3,32,1024]{2,1,0:T(8,128)} %copy-done.8), custom_call_target="tpu_custom_call" | custom-call | tf_op jit(solution)/shard_map/site/pallas_call | solution.py:386
  44.4 14.6 %filter.2 = f32[4,8,8,1024]{3,2,1,0:T(8,128)} custom-call(f32[35]{0:T(128)} %pad_maximum_fusion.1.coef_ref, f32[8,32,1024]{2,1,0:T(8,128)} %copy-done.2, f32[32,8,8,128]{3,2,1,0:T(8,128)} %site.1), custom_call_target="tpu_custom_call" | custom-call | tf_op jit(solution)/shard_map/filter/pallas_call | solution.py:401
  59.0 6.0 %all-to-all-start.1 = ((f32[32,8,1024]{2,1,0:T(8,128)}), f32[32,8,1024]{2,1,0:T(8,128)S(1)}, u32[]{:S(2)}, u32[]{:S(2)}) async-start(f32[32,8,1024]{2,1,0:T(8,128)} %bitcast.27), calls=%async_computation.1 | async-start | bytes 2097152 | tf_op jit(solution)/shard_map/all_to_all | solution.py:414
  65.0 14.6 %filter.3 = f32[4,8,8,1024]{3,2,1,0:T(8,128)} custom-call(f32[35]{0:T(128)} %pad_maximum_fusion.1.coef_ref, f32[8,32,1024]{2,1,0:T(8,128)} %copy-done.3, f32[32,8,8,128]{3,2,1,0:T(8,128)} %site.1), custom_call_target="tpu_custom_call" | custom-call | tf_op jit(solution)/shard_map/filter/pallas_call | solution.py:401
  79.6 10.0 %all-to-all-done.1.refs_0_ = f32[32,8,1024]{2,1,0:T(8,128)S(1)} async-done(((f32[32,8,1024]{2,1,0:T(8,128)}), f32[32,8,1024]{2,1,0:T(8,128)S(1)}, u32[]{:S(2)}, u32[]{:S(2)}) %all-to-all-start.1) | async-done | bytes 1048608 | tf_op jit(solution)/shard_map/all_to_all | solution.py:414
  89.7 5.2 %all-to-all-start.3 = ((f32[32,8,1024]{2,1,0:T(8,128)}), f32[32,8,1024]{2,1,0:T(8,128)S(1)}, u32[]{:S(2)}, u32[]{:S(2)}) async-start(f32[32,8,1024]{2,1,0:T(8,128)} %bitcast.26), calls=%async_computation.3 | async-start | bytes 2097152 | tf_op jit(solution)/shard_map/all_to_all | solution.py:414
  95.0 0.6 collective-permute-start.13
  95.6 25.3 %all-to-all-done.3.refs_1_ = f32[32,8,1024]{2,1,0:T(8,128)S(1)} async-done(((f32[32,8,1024]{2,1,0:T(8,128)}), f32[32,8,1024]{2,1,0:T(8,128)S(1)}, u32[]{:S(2)}, u32[]{:S(2)}) %all-to-all-start.3) | async-done | bytes 1048608 | tf_op jit(solution)/shard_map/all_to_all | solution.py:414
  121.0 1.3 collective-permute-start.14
  122.2 7.0 %gram.1 = (f32[64,128]{1,0:T(8,128)}, f32[8,64,1024]{2,1,0:T(8,128)}) custom-call(f32[32,8,1024]{2,1,0:T(8,128)} %copy-done, f32[32,8,1024]{2,1,0:T(8,128)} %copy-done.1, s32[1]{0:T(128)} %bitcast.refs_2_.place_ref, f32[32,1024]{1,0:T(8,128)} %convert_element_type.15.here_ref.refs_3_), custom_call_target="tpu_custom_call" | custom-call | tf_op jit(solution)/shard_map/gram/pallas_call | solution.py:421
  129.2 1.4 collective-permute-done.5
  130.6 0.8 add.69
  132.0 3.4 %collective-permute-done.6 = f32[64,128]{1,0:T(8,128)S(1)} collective-permute-done((f32[64,128]{1,0:T(8,128)S(1)}, f32[64,128]{1,0:T(8,128)S(1)}, u32[]{:S(2)}, u32[]{:S(2)}) %collective-permute-start.6) | collective-permute-done | bytes 32800 | tf_op jit(solution)/shard_map/ppermute | solution.py:440
  135.3 1.5 collective-permute-start.7
  136.8 2.4 %collective-permute-done.7 = f32[64,128]{1,0:T(8,128)S(1)} collective-permute-done((f32[64,128]{1,0:T(8,128)S(1)}, f32[64,128]{1,0:T(8,128)S(1)}, u32[]{:S(2)}, u32[]{:S(2)}) %collective-permute-start.7) | collective-permute-done | bytes 32800 | tf_op jit(solution)/shard_map/ppermute | solution.py:440
  139.2 3.7 %collective-permute-start.8 = (f32[64,128]{1,0:T(8,128)S(1)}, f32[64,128]{1,0:T(8,128)S(1)}, u32[]{:S(2)}, u32[]{:S(2)}) collective-permute-start(f32[64,128]{1,0:T(8,128)S(1)} %add.71), channel_id=1, source_target_pairs={{0,1},{1,0},{2,3},{3,2},{4,5},{5,4},{6,7},{7,6},{8,9},{9,8},{10,11... | collective-permute-start | bytes 98312 | tf_op jit(solution)/shard_map/ppermute | solution.py:440
  143.0 0.6 copy-done.11
  143.6 2.1 edge.1
  145.7 4.1 %collective-permute-done.15 = f32[64,64]{1,0:T(8,128)S(1)} collective-permute-done((f32[64,64]{1,0:T(8,128)}, f32[64,64]{1,0:T(8,128)S(1)}, u32[]{:S(2)}, u32[]{:S(2)}) %collective-permute-start.15) | collective-permute-done | bytes 16416 | tf_op jit(solution)/shard_map/ppermute | solution.py:440
  149.8 0.8 add.77
  150.6 3.0 %collective-permute-start.9 = (f32[64,128]{1,0:T(8,128)S(1)}, f32[64,128]{1,0:T(8,128)S(1)}, u32[]{:S(2)}, u32[]{:S(2)}) collective-permute-start(f32[64,128]{1,0:T(8,128)S(1)} %add.72.mine_ref), channel_id=1, source_target_pairs={{0,2},{1,3},{2,0},{3,1},{4,6},{5,7},{6,4},{7,5},{8,10},{9,11},{10,... | collective-permute-start | bytes 98312 | tf_op jit(solution)/shard_map/ppermute | solution.py:440
  153.6 1.9 collective-permute-done.16
  155.5 1.2 collective-permute-done.17
  156.7 1.9 collective-permute-start.18
  158.7 0.6 copy-done.15
  159.3 9.1 %solve.1 = (f32[64,64]{1,0:T(8,128)}, f32[64,128]{1,0:T(8,128)}, f32[16,8,1024]{2,1,0:T(8,128)}, f32[16,8,1024]{2,1,0:T(8,128)}) custom-call(s32[1]{0:T(128)} %bitcast.refs_2_.place_ref, f32[64,128]{1,0:T(8,128)} %copy-done.10, f32[64,128]{1,0:T(8,128)} %copy-done.15, f32[8,64,1024]{2,1,0:T(8,128)} %get-tuple-element.13.lines_ref.refs_2_), custom_call_target="tpu_custom_call" | custom-call | tf_op jit(solution)/shard_map/solve/pallas_call | solution.py:453
  168.4 3.6 %near.1 = (f32[16,8,1024]{2,1,0:T(8,128)}, f32[16,8,1024]{2,1,0:T(8,128)}) custom-call(s32[1]{0:T(128)} %bitcast.refs_2_.place_ref, f32[64,64]{1,0:T(8,128)} %get-tuple-element.14.inv_ref, f32[8,64,1024]{2,1,0:T(8,128)} %get-tuple-element.13.lines_ref.refs_2_), custom_call_target="tpu_custom_call" | custom-call | tf_op jit(solution)/shard_map/near/pallas_call | solution.py:461
  172.2 3.4 %collective-permute-start.12 = (f32[16,8,1024]{2,1,0:T(8,128)}, f32[16,8,1024]{2,1,0:T(8,128)S(1)}, u32[]{:S(2)}, u32[]{:S(2)}) collective-permute-start(f32[16,8,1024]{2,1,0:T(8,128)} %get-tuple-element.18), channel_id=1, source_target_pairs={{0,3},{1,2},{2,1},{3,0},{4,7},{5,6},{6,5},{7,4},{8,11},{9,10},{10,... | collective-permute-start | bytes 1572872 | tf_op jit(solution)/shard_map/ppermute | solution.py:471
  176.1 3.5 %collective-permute-done.19 = f32[64,64]{1,0:T(8,128)S(1)} collective-permute-done((f32[64,64]{1,0:T(8,128)S(1)}, f32[64,64]{1,0:T(8,128)S(1)}, u32[]{:S(2)}, u32[]{:S(2)}) %collective-permute-start.19) | collective-permute-done | bytes 16416 | tf_op jit(solution)/shard_map/ppermute | solution.py:440
  179.9 0.8 convolution_multiply_fusion
  180.7 11.6 %collective-permute-done.10 = f32[16,8,1024]{2,1,0:T(8,128)} collective-permute-done((f32[16,8,1024]{2,1,0:T(8,128)}, f32[16,8,1024]{2,1,0:T(8,128)}, u32[]{:S(2)}, u32[]{:S(2)}) %collective-permute-start.10) | collective-permute-done | bytes 524320 | tf_op jit(solution)/shard_map/ppermute | solution.py:471
  192.3 1.1 constant_dynamic-update-slice_fusion.2
  193.4 3.1 %collective-permute-done.11 = f32[16,8,1024]{2,1,0:T(8,128)S(1)} collective-permute-done((f32[16,8,1024]{2,1,0:T(8,128)}, f32[16,8,1024]{2,1,0:T(8,128)S(1)}, u32[]{:S(2)}, u32[]{:S(2)}) %collective-permute-start.11) | collective-permute-done | bytes 524320 | tf_op jit(solution)/shard_map/ppermute | solution.py:471
  196.5 24.5 %collective-permute-done.12 = f32[16,8,1024]{2,1,0:T(8,128)S(1)} collective-permute-done((f32[16,8,1024]{2,1,0:T(8,128)}, f32[16,8,1024]{2,1,0:T(8,128)S(1)}, u32[]{:S(2)}, u32[]{:S(2)}) %collective-permute-start.12) | collective-permute-done | bytes 524320 | tf_op jit(solution)/shard_map/ppermute | solution.py:471
  221.0 1.3 copy-done.4
  (73 shorter events, 2.9 us)
Async XLA Ops:
  0.6 6.7 %copy-start.13 = (s32[32,1024]{1,0:T(8,128)S(1)}, s32[32,1024]{1,0:T(8,128)}, u32[]{:S(2)}) copy-start(s32[32,1024]{1,0:T(8,128)} %param.4) | copy-start | bytes 393220
  3.0 24.0 %copy-start.5 = (f32[16,32,1024]{2,1,0:T(8,128)S(1)}, f32[16,32,1024]{2,1,0:T(8,128)}, u32[]{:S(2)}) copy-start(f32[16,32,1024]{2,1,0:T(8,128)} %param.3) | copy-start | bytes 6291460
  3.0 25.1 %all-to-all-start = ((f32[8,32,1024]{2,1,0:T(8,128)}), f32[8,32,1024]{2,1,0:T(8,128)S(1)}, u32[]{:S(2)}, u32[]{:S(2)}) async-start(f32[8,32,1024]{2,1,0:T(8,128)} %slice.33), calls=%async_computation | async-start | bytes 2097152 | tf_op jit(solution)/shard_map/all_to_all | solution.py:364
  8.0 15.2 %collective-permute-start.1 = (f32[32,1024]{1,0:T(8,128)}, f32[32,1024]{1,0:T(8,128)S(1)}, u32[]{:S(2)}, u32[]{:S(2)}) collective-permute-start(f32[32,1024]{1,0:T(8,128)} %convert_element_type.15.here_ref.refs_3_), channel_id=1, source_target_pairs={{0,8},{4,12},{8,0},{12,4},{16,24},{20,28},{24,16},{28,20},{1,9},{5... | collective-permute-start | bytes 393224 | tf_op jit(solution)/shard_map/ppermute | solution.py:358
  8.0 16.5 %collective-permute-start.2 = (f32[32,1024]{1,0:T(8,128)}, f32[32,1024]{1,0:T(8,128)S(1)}, u32[]{:S(2)}, u32[]{:S(2)}) collective-permute-start(f32[32,1024]{1,0:T(8,128)} %convert_element_type.15.here_ref.refs_3_), channel_id=1, source_target_pairs={{0,16},{4,20},{8,24},{12,28},{16,0},{20,4},{24,8},{28,12},{1,17},{... | collective-permute-start | bytes 393224 | tf_op jit(solution)/shard_map/ppermute | solution.py:358
  10.1 16.9 %collective-permute-start.3 = (f32[32,1024]{1,0:T(8,128)}, f32[32,1024]{1,0:T(8,128)S(1)}, u32[]{:S(2)}, u32[]{:S(2)}) collective-permute-start(f32[32,1024]{1,0:T(8,128)} %convert_element_type.15.here_ref.refs_3_), channel_id=1, source_target_pairs={{0,24},{4,28},{8,16},{12,20},{16,8},{20,12},{24,0},{28,4},{1,25},{... | collective-permute-start | bytes 393224 | tf_op jit(solution)/shard_map/ppermute | solution.py:358
  27.0 6.2 %copy-start.6 = (f32[3,32,1024]{2,1,0:T(8,128)}, f32[3,32,1024]{2,1,0:T(8,128)S(1)}, u32[]{:S(2)}) copy-start(f32[3,32,1024]{2,1,0:T(8,128)S(1)} %pad_maximum_fusion.own_ref) | copy-start | bytes 1179652
  27.0 6.2 %copy-start.17 = (s32[4]{0:T(128)S(1)}, s32[4]{0:T(128)}, u32[]{:S(2)}) copy-start(s32[4]{0:T(128)} %param.5) | copy-start | bytes 52
  28.1 16.3 %copy-start.2 = (f32[8,32,1024]{2,1,0:T(8,128)}, f32[8,32,1024]{2,1,0:T(8,128)S(1)}, u32[]{:S(2)}) copy-start(f32[8,32,1024]{2,1,0:T(8,128)S(1)} %all-to-all-done.vec_ref) | copy-start | bytes 3145732
  28.1 30.9 %all-to-all-start.2 = ((f32[8,32,1024]{2,1,0:T(8,128)}), f32[8,32,1024]{2,1,0:T(8,128)S(1)}, u32[]{:S(2)}, u32[]{:S(2)}) async-start(f32[8,32,1024]{2,1,0:T(8,128)} %slice.34), calls=%async_computation.2 | async-start | bytes 2097152 | tf_op jit(solution)/shard_map/all_to_all | solution.py:364
  33.0 6.3 %collective-permute-start = (f32[32,1024]{1,0:T(8,128)}, f32[32,1024]{1,0:T(8,128)S(1)}, u32[]{:S(2)}, u32[]{:S(2)}) collective-permute-start(f32[32,1024]{1,0:T(8,128)} %convert_element_type.15.here_ref.refs_3_), channel_id=1, source_target_pairs={{0,4},{4,0},{8,12},{12,8},{16,20},{20,16},{24,28},{28,24},{1,5},{5... | collective-permute-start | bytes 393224 | tf_op jit(solution)/shard_map/ppermute | solution.py:358
  33.2 6.2 %collective-permute-start.4 = (f32[3,32,1024]{2,1,0:T(8,128)S(1)}, f32[3,32,1024]{2,1,0:T(8,128)S(1)}, u32[]{:S(2)}, u32[]{:S(2)}) collective-permute-start(f32[3,32,1024]{2,1,0:T(8,128)S(1)} %pad_maximum_fusion.own_ref), channel_id=1, source_target_pairs={{0,4},{4,0},{8,12},{12,8},{16,20},{20,16},{24,28},{28,24},{1,5},{5... | collective-permute-start | bytes 1179656 | tf_op jit(solution)/shard_map/ppermute | solution.py:358
  39.4 0.6 copy-start.14
  39.4 0.8 copy-start.8
  59.0 6.0 %copy-start.3 = (f32[8,32,1024]{2,1,0:T(8,128)}, f32[8,32,1024]{2,1,0:T(8,128)S(1)}, u32[]{:S(2)}) copy-start(f32[8,32,1024]{2,1,0:T(8,128)S(1)} %all-to-all-done.2.vec_ref) | copy-start | bytes 3145732
  59.0 30.6 %all-to-all-start.1 = ((f32[32,8,1024]{2,1,0:T(8,128)}), f32[32,8,1024]{2,1,0:T(8,128)S(1)}, u32[]{:S(2)}, u32[]{:S(2)}) async-start(f32[32,8,1024]{2,1,0:T(8,128)} %bitcast.27), calls=%async_computation.1 | async-start | bytes 2097152 | tf_op jit(solution)/shard_map/all_to_all | solution.py:414
  89.7 32.6 %copy-start = (f32[32,8,1024]{2,1,0:T(8,128)}, f32[32,8,1024]{2,1,0:T(8,128)S(1)}, u32[]{:S(2)}) copy-start(f32[32,8,1024]{2,1,0:T(8,128)S(1)} %all-to-all-done.1.refs_0_) | copy-start | bytes 3145732
  89.7 31.2 %all-to-all-start.3 = ((f32[32,8,1024]{2,1,0:T(8,128)}), f32[32,8,1024]{2,1,0:T(8,128)S(1)}, u32[]{:S(2)}, u32[]{:S(2)}) async-start(f32[32,8,1024]{2,1,0:T(8,128)} %bitcast.26), calls=%async_computation.3 | async-start | bytes 2097152 | tf_op jit(solution)/shard_map/all_to_all | solution.py:414
  95.0 48.0 %collective-permute-start.13 = (f32[32,1024]{1,0:T(8,128)S(1)}, f32[32,1024]{1,0:T(8,128)S(1)}, u32[]{:S(2)}, u32[]{:S(2)}) collective-permute-start(f32[32,1024]{1,0:T(8,128)S(1)} %bitcast.28), channel_id=1, source_target_pairs={{1,0},{2,1},{3,2},{4,3},{5,4},{6,5},{7,6},{8,7},{9,8},{10,9},{11,1... | collective-permute-start | bytes 393224 | tf_op jit(solution)/shard_map/ppermute | solution.py:416
  120.9 1.4 copy-start.1
  121.0 22.0 %collective-permute-start.14 = (f32[32,1024]{1,0:T(8,128)S(1)}, f32[32,1024]{1,0:T(8,128)S(1)}, u32[]{:S(2)}, u32[]{:S(2)}) collective-permute-start(f32[32,1024]{1,0:T(8,128)S(1)} %bitcast.29), channel_id=1, source_target_pairs={{1,0},{2,1},{3,2},{4,3},{5,4},{6,5},{7,6},{8,7},{9,8},{10,9},{11,1... | collective-permute-start | bytes 393224 | tf_op jit(solution)/shard_map/ppermute | solution.py:416
  129.2 1.4 collective-permute-start.5
  131.4 3.9 %collective-permute-start.6 = (f32[64,128]{1,0:T(8,128)S(1)}, f32[64,128]{1,0:T(8,128)S(1)}, u32[]{:S(2)}, u32[]{:S(2)}) collective-permute-start(f32[64,128]{1,0:T(8,128)S(1)} %add.69), channel_id=1, source_target_pairs={{0,8},{4,12},{8,0},{12,4},{16,24},{20,28},{24,16},{28,20},{1,9},{5... | collective-permute-start | bytes 98312 | tf_op jit(solution)/shard_map/ppermute | solution.py:440
  135.3 3.9 %collective-permute-start.7 = (f32[64,128]{1,0:T(8,128)S(1)}, f32[64,128]{1,0:T(8,128)S(1)}, u32[]{:S(2)}, u32[]{:S(2)}) collective-permute-start(f32[64,128]{1,0:T(8,128)S(1)} %add.70), channel_id=1, source_target_pairs={{0,16},{4,20},{8,24},{12,28},{16,0},{20,4},{24,8},{28,12},{1,17},{... | collective-permute-start | bytes 98312 | tf_op jit(solution)/shard_map/ppermute | solution.py:440
  139.2 11.4 %collective-permute-start.8 = (f32[64,128]{1,0:T(8,128)S(1)}, f32[64,128]{1,0:T(8,128)S(1)}, u32[]{:S(2)}, u32[]{:S(2)}) collective-permute-start(f32[64,128]{1,0:T(8,128)S(1)} %add.71), channel_id=1, source_target_pairs={{0,1},{1,0},{2,3},{3,2},{4,5},{5,4},{6,7},{7,6},{8,9},{9,8},{10,11... | collective-permute-start | bytes 98312 | tf_op jit(solution)/shard_map/ppermute | solution.py:440
  142.9 0.7 copy-start.11
  142.9 0.7 copy-start.12
  145.7 4.1 %collective-permute-start.15 = (f32[64,64]{1,0:T(8,128)}, f32[64,64]{1,0:T(8,128)S(1)}, u32[]{:S(2)}, u32[]{:S(2)}) collective-permute-start(f32[64,64]{1,0:T(8,128)} %edge.1), channel_id=1, source_target_pairs={{0,1},{1,0},{2,3},{3,2},{4,5},{5,4},{6,7},{7,6},{8,9},{9,8},{10,11... | collective-permute-start | bytes 49160 | tf_op jit(solution)/shard_map/ppermute | solution.py:440
  150.6 4.9 %collective-permute-start.16 = (f32[64,64]{1,0:T(8,128)S(1)}, f32[64,64]{1,0:T(8,128)S(1)}, u32[]{:S(2)}, u32[]{:S(2)}) collective-permute-start(f32[64,64]{1,0:T(8,128)S(1)} %add.77), channel_id=1, source_target_pairs={{0,2},{1,3},{2,0},{3,1},{4,6},{5,7},{6,4},{7,5},{8,10},{9,11},{10,... | collective-permute-start | bytes 49160 | tf_op jit(solution)/shard_map/ppermute | solution.py:440
  150.6 8.0 %copy-start.10 = (f32[64,128]{1,0:T(8,128)}, f32[64,128]{1,0:T(8,128)S(1)}, u32[]{:S(2)}) copy-start(f32[64,128]{1,0:T(8,128)S(1)} %add.72.mine_ref) | copy-start | bytes 98308
  150.6 8.0 %collective-permute-start.9 = (f32[64,128]{1,0:T(8,128)S(1)}, f32[64,128]{1,0:T(8,128)S(1)}, u32[]{:S(2)}, u32[]{:S(2)}) collective-permute-start(f32[64,128]{1,0:T(8,128)S(1)} %add.72.mine_ref), channel_id=1, source_target_pairs={{0,2},{1,3},{2,0},{3,1},{4,6},{5,7},{6,4},{7,5},{8,10},{9,11},{10,... | collective-permute-start | bytes 98312 | tf_op jit(solution)/shard_map/ppermute | solution.py:440
  155.5 1.2 collective-permute-start.17
  156.7 18.9 %collective-permute-start.18 = (f32[64,64]{1,0:T(8,128)S(1)}, f32[64,64]{1,0:T(8,128)S(1)}, u32[]{:S(2)}, u32[]{:S(2)}) collective-permute-start(f32[64,64]{1,0:T(8,128)S(1)} %add.79), channel_id=1, source_target_pairs={{0,8},{4,12},{8,0},{12,4},{16,24},{20,28},{24,16},{28,20},{1,9},{5... | collective-permute-start | bytes 49160 | tf_op jit(solution)/shard_map/ppermute | solution.py:440
  158.7 0.6 copy-start.15
  172.0 4.0 %copy-start.7 = (f32[16,8,1024]{2,1,0:T(8,128)S(1)}, f32[16,8,1024]{2,1,0:T(8,128)}, u32[]{:S(2)}) copy-start(f32[16,8,1024]{2,1,0:T(8,128)} %get-tuple-element.15) | copy-start | bytes 1572868
  172.0 7.5 %copy-start.16 = (f32[64,128]{1,0:T(8,128)S(1)}, f32[64,128]{1,0:T(8,128)}, u32[]{:S(2)}) copy-start(f32[64,128]{1,0:T(8,128)} %get-tuple-element.19) | copy-start | bytes 98308
  172.0 7.7 %copy-start.9 = (f32[64,64]{1,0:T(8,128)S(1)}, f32[64,64]{1,0:T(8,128)}, u32[]{:S(2)}) copy-start(f32[64,64]{1,0:T(8,128)} %get-tuple-element.14.inv_ref) | copy-start | bytes 49156
  172.0 20.3 %collective-permute-start.10 = (f32[16,8,1024]{2,1,0:T(8,128)}, f32[16,8,1024]{2,1,0:T(8,128)}, u32[]{:S(2)}, u32[]{:S(2)}) collective-permute-start(f32[16,8,1024]{2,1,0:T(8,128)} %get-tuple-element.16), channel_id=1, source_target_pairs={{0,1},{1,0},{2,3},{3,2},{4,5},{5,4},{6,7},{7,6},{8,9},{9,8},{10,11... | collective-permute-start | bytes 1572872 | tf_op jit(solution)/shard_map/ppermute | solution.py:471
  172.1 24.3 %collective-permute-start.11 = (f32[16,8,1024]{2,1,0:T(8,128)}, f32[16,8,1024]{2,1,0:T(8,128)S(1)}, u32[]{:S(2)}, u32[]{:S(2)}) collective-permute-start(f32[16,8,1024]{2,1,0:T(8,128)} %get-tuple-element.17), channel_id=1, source_target_pairs={{0,2},{1,3},{2,0},{3,1},{4,6},{5,7},{6,4},{7,5},{8,10},{9,11},{10,... | collective-permute-start | bytes 1572872 | tf_op jit(solution)/shard_map/ppermute | solution.py:471
  172.2 48.8 %collective-permute-start.12 = (f32[16,8,1024]{2,1,0:T(8,128)}, f32[16,8,1024]{2,1,0:T(8,128)S(1)}, u32[]{:S(2)}, u32[]{:S(2)}) collective-permute-start(f32[16,8,1024]{2,1,0:T(8,128)} %get-tuple-element.18), channel_id=1, source_target_pairs={{0,3},{1,2},{2,1},{3,0},{4,7},{5,6},{6,5},{7,4},{8,11},{9,10},{10,... | collective-permute-start | bytes 1572872 | tf_op jit(solution)/shard_map/ppermute | solution.py:471
  175.6 4.0 %collective-permute-start.19 = (f32[64,64]{1,0:T(8,128)S(1)}, f32[64,64]{1,0:T(8,128)S(1)}, u32[]{:S(2)}, u32[]{:S(2)}) collective-permute-start(f32[64,64]{1,0:T(8,128)S(1)} %add.80), channel_id=1, source_target_pairs={{0,16},{4,20},{8,24},{12,28},{16,0},{20,4},{24,8},{28,12},{1,17},{... | collective-permute-start | bytes 49160 | tf_op jit(solution)/shard_map/ppermute | solution.py:440
  221.0 1.3 copy-start.4

commit v3 on v2

--- a/solution.py
+++ b/solution.py
@@ -105,6 +105,11 @@
         lower_factor, half_done.T, lower=True
     )
     return (ortho_basis, ritz_matrix)
+
+
+def turned(group, strip, groups):
+    odd = strip % 2
+    return group + odd * (groups - 1 - 2 * group)
 
 
 def stage(read, flip, grid, target, change, rows, strips):
@@ -231,11 +236,11 @@
         for block in range(blocks):
             tile = flip[block, part * lanes : (part + 1) * lanes, :].T
             for p in range(per_block):
+                strip = block * per_block + p
                 for slab in range(slabs):
                     start = p * rows + slab * slab_rows
-                    out_ref[slab, block * per_block + p, :, part * lanes : (part + 1) * lanes] = tile[
-                        start : start + slab_rows
-                    ]
+                    group = turned(slab, strip, slabs)
+                    out_ref[group, strip, :, part * lanes : (part + 1) * lanes] = tile[start : start + slab_rows]
 
 
 def outer(left, right):
@@ -396,7 +401,8 @@
         name="site",
     )(terms, me[None], level, beside, own_pots, other_pots)
     slabs, nexts = [], []
-    ring = [((i + 1) % devices, i) for i in range(devices)]
+    holders = [p * groups + turned(s, p, groups) for p in range(strips) for s in range(groups)]
+    ring = [(holders[(g + 1) % devices], holders[g]) for g in range(devices)]
     for chunk in range(vecs):
         done = pl.pallas_call(
             functools.partial(filter_kernel, slabs=groups),
@@ -424,7 +430,7 @@
         out_specs=[vmem, vmem],
         out_shape=[sums_shape, jax.ShapeDtypeStruct(lines_shape, jnp.float32)],
         name="gram",
-    )(*slabs, place[None], level)
+    )(*slabs, turned(place, me, groups)[None], level)
     edge = pl.pallas_call(
         functools.partial(edge_kernel, chunks=vecs),
         grid=(1,),
@@ -443,7 +449,11 @@
         return value, other
 
     sums, pending = pairwise(sums, (("strip", strips), ("vec", groups)))
-    edge = sum(pairwise(edge, (("vec", groups), ("strip", strips))))
+    edge = sum(pairwise(edge, (("strip", strips),)))
+    others = []
+    for d in range(1, groups):
+        others.append(lax.ppermute(edge, "vec", [(i, i ^ d) for i in range(groups)]))
+    edge = edge + sum(others)
 
     scale = math.sqrt(strips * rows * columns)
     half = groups // 2
@@ -474,7 +484,7 @@
     near_blocks = [across(block, d) for d, block in zip(near, near_blocks)]
     ortho_basis = jnp.zeros((vec_local, rows, columns), jnp.float32)
     for d, block in zip(near + far, near_blocks + far_blocks):
-        start = (place ^ d) * slab_rows
+        start = turned(place ^ d, me, groups) * slab_rows
         ortho_basis = lax.dynamic_update_slice(ortho_basis, block, (0, start, 0))
 
     cross_half = gram_cross[:, total_vecs:] + edge

time: 223 us -> 217 us (0.973)
  the two profiles are of different devices: /device:TPU:10 before, /device:TPU:8 now
where the time goes in v3:
time: 217 us; the launch traced here: 216 us
  waiting for transfers between devices  104 us (48%)
  Pallas kernels  55.3 us (25%)
  starting transfers between devices  39 us (18%)
  local copies, waits for them, and re-layouts  9.29 us (4%)
  between operations  4.97 us (2%)
  other arithmetic  3.08 us (1%)
    all_to_all x2, waiting for transfers between devices, whole_shards(): lax.all_to_all(done.reshape(devices, slab_rows, columns), both, split_axi...  35.5 us
    ppermute x3, waiting for transfers between devices, whole_shards(): lax.ppermute(edge, 'vec', [(i, i ^ d) for i in range(groups)])  33.2 us
    pallas_call x2, Pallas kernels, whole_shards(): pl.pallas_call(functools.partial(filter_kernel, slabs=groups), in_specs=[...  29.2 us
    ppermute x5, waiting for transfers between devices, swap(): return lax.ppermute(value, 'strip', [(i, i ^ bit) for i in range(strips)])  16.9 us
    all_to_all x2, starting transfers between devices, whole_shards(): lax.all_to_all(done.reshape(devices, slab_rows, columns), both, split_axi...  10.9 us
    ppermute x8, waiting for transfers between devices, pairwise(): other = lax.ppermute(value, axis, [(i, i ^ bit) for i in range(count)])  9.76 us
    pallas_call x1, Pallas kernels, whole_shards(): pl.pallas_call(functools.partial(solve_kernel, scale=scale, targets=far,...  9.14 us
    ppermute x3, waiting for transfers between devices, across(): lax.ppermute(block, 'vec', [(i, i ^ d) for i in range(groups)])  8.46 us
  transfers between devices with their start and end apart: 25, of which 13 were waited for; matrix products, arithmetic and copies ran while one was open for 3% of the time, Pallas kernels for 26%

profile of v3, /device:TPU:8, one launch (start us, length us, event | category | flops | bytes accessed | tf_op | source)
XLA Modules:
  0.0 216.4 jit_solution(15936123831514059321)
XLA Ops:
  0.6 2.3 %slice.33 = f32[8,32,1024]{2,1,0:T(8,128)} slice(f32[16,32,1024]{2,1,0:T(8,128)} %param.3), slice={[0:8], [0:32], [0:1024]} | slice | bytes 2097152 | tf_op jit(solution)/shard_map/slice | solution.py:368
  3.0 3.9 %all-to-all-start = ((f32[8,32,1024]{2,1,0:T(8,128)}), f32[8,32,1024]{2,1,0:T(8,128)S(1)}, u32[]{:S(2)}, u32[]{:S(2)}) async-start(f32[8,32,1024]{2,1,0:T(8,128)} %slice.33), calls=%async_computation | async-start | bytes 2097152 | tf_op jit(solution)/shard_map/all_to_all | solution.py:369
  6.8 0.7 convert_element_type.15.here_ref.refs_3_
  7.5 2.0 collective-permute-start.1
  9.5 1.5 collective-permute-start.2
  11.0 13.7 %collective-permute-done.1 = f32[32,1024]{1,0:T(8,128)S(1)} collective-permute-done((f32[32,1024]{1,0:T(8,128)}, f32[32,1024]{1,0:T(8,128)S(1)}, u32[]{:S(2)}, u32[]{:S(2)}) %collective-permute-start.1) | collective-permute-done | bytes 131104 | tf_op jit(solution)/shard_map/ppermute | solution.py:363
  24.7 3.1 %collective-permute-done.3 = f32[32,1024]{1,0:T(8,128)S(1)} collective-permute-done((f32[32,1024]{1,0:T(8,128)}, f32[32,1024]{1,0:T(8,128)S(1)}, u32[]{:S(2)}, u32[]{:S(2)}) %collective-permute-start.3) | collective-permute-done | bytes 131104 | tf_op jit(solution)/shard_map/ppermute | solution.py:363
  27.9 1.1 slice.34
  29.1 3.6 %all-to-all-start.2 = ((f32[8,32,1024]{2,1,0:T(8,128)}), f32[8,32,1024]{2,1,0:T(8,128)S(1)}, u32[]{:S(2)}, u32[]{:S(2)}) async-start(f32[8,32,1024]{2,1,0:T(8,128)} %slice.34), calls=%async_computation.2 | async-start | bytes 2097152 | tf_op jit(solution)/shard_map/all_to_all | solution.py:369
  33.3 0.7 fusion.6
  38.8 0.6 copy-done.14
  39.6 4.2 %site.1 = f32[32,8,8,128]{3,2,1,0:T(8,128)} custom-call(f32[35]{0:T(128)} %pad_maximum_fusion.1.coef_ref, s32[1]{0:T(128)} %bitcast.6.me_ref, f32[32,1024]{1,0:T(8,128)} %convert_element_type.15.here_ref.refs_3_, f32[32,1024]{1,0:T(8,128)} %copy-done.14, f32[3,32,1024]{2,1,0:T(8,128)} %copy-done.6, f32[3,32,1024]{2,1,0:T(8,128)} %copy-done.8), custom_call_target="tpu_custom_call" | custom-call | tf_op jit(solution)/shard_map/site/pallas_call | solution.py:391
  43.8 14.6 %filter.2 = f32[4,8,8,1024]{3,2,1,0:T(8,128)} custom-call(f32[35]{0:T(128)} %pad_maximum_fusion.1.coef_ref, f32[8,32,1024]{2,1,0:T(8,128)} %copy-done.2, f32[32,8,8,128]{3,2,1,0:T(8,128)} %site.1), custom_call_target="tpu_custom_call" | custom-call | tf_op jit(solution)/shard_map/filter/pallas_call | solution.py:407
  58.4 6.4 %all-to-all-start.1 = ((f32[32,8,1024]{2,1,0:T(8,128)}), f32[32,8,1024]{2,1,0:T(8,128)S(1)}, u32[]{:S(2)}, u32[]{:S(2)}) async-start(f32[32,8,1024]{2,1,0:T(8,128)} %bitcast.28), calls=%async_computation.1 | async-start | bytes 2097152 | tf_op jit(solution)/shard_map/all_to_all | solution.py:420
  64.8 14.6 %filter.3 = f32[4,8,8,1024]{3,2,1,0:T(8,128)} custom-call(f32[35]{0:T(128)} %pad_maximum_fusion.1.coef_ref, f32[8,32,1024]{2,1,0:T(8,128)} %copy-done.3, f32[32,8,8,128]{3,2,1,0:T(8,128)} %site.1), custom_call_target="tpu_custom_call" | custom-call | tf_op jit(solution)/shard_map/filter/pallas_call | solution.py:407
  79.5 10.7 %all-to-all-done.1.refs_0_ = f32[32,8,1024]{2,1,0:T(8,128)S(1)} async-done(((f32[32,8,1024]{2,1,0:T(8,128)}), f32[32,8,1024]{2,1,0:T(8,128)S(1)}, u32[]{:S(2)}, u32[]{:S(2)}) %all-to-all-start.1) | async-done | bytes 1048608 | tf_op jit(solution)/shard_map/all_to_all | solution.py:420
  90.1 4.5 %all-to-all-start.3 = ((f32[32,8,1024]{2,1,0:T(8,128)}), f32[32,8,1024]{2,1,0:T(8,128)S(1)}, u32[]{:S(2)}, u32[]{:S(2)}) async-start(f32[32,8,1024]{2,1,0:T(8,128)} %bitcast.27), calls=%async_computation.3 | async-start | bytes 2097152 | tf_op jit(solution)/shard_map/all_to_all | solution.py:420
  95.1 24.9 %all-to-all-done.3.refs_1_ = f32[32,8,1024]{2,1,0:T(8,128)S(1)} async-done(((f32[32,8,1024]{2,1,0:T(8,128)}), f32[32,8,1024]{2,1,0:T(8,128)S(1)}, u32[]{:S(2)}, u32[]{:S(2)}) %all-to-all-start.3) | async-done | bytes 1048608 | tf_op jit(solution)/shard_map/all_to_all | solution.py:420
  120.1 1.4 collective-permute-start.14
  121.5 7.0 %gram.1 = (f32[64,128]{1,0:T(8,128)}, f32[8,64,1024]{2,1,0:T(8,128)}) custom-call(f32[32,8,1024]{2,1,0:T(8,128)} %copy-done, f32[32,8,1024]{2,1,0:T(8,128)} %copy-done.1, s32[1]{0:T(128)} %bitcast.12.refs_2_, f32[32,1024]{1,0:T(8,128)} %convert_element_type.15.here_ref.refs_3_), custom_call_target="tpu_custom_call" | custom-call | tf_op jit(solution)/shard_map/gram/pallas_call | solution.py:427
  128.4 1.4 collective-permute-done.5
  129.9 0.8 add.95
  130.6 1.5 collective-permute-start.6
  132.1 2.4 %collective-permute-done.6 = f32[64,128]{1,0:T(8,128)S(1)} collective-permute-done((f32[64,128]{1,0:T(8,128)S(1)}, f32[64,128]{1,0:T(8,128)S(1)}, u32[]{:S(2)}, u32[]{:S(2)}) %collective-permute-start.6) | collective-permute-done | bytes 32800 | tf_op jit(solution)/shard_map/ppermute | solution.py:446
  134.5 1.5 collective-permute-start.7
  136.0 2.4 %collective-permute-done.7 = f32[64,128]{1,0:T(8,128)S(1)} collective-permute-done((f32[64,128]{1,0:T(8,128)S(1)}, f32[64,128]{1,0:T(8,128)S(1)}, u32[]{:S(2)}, u32[]{:S(2)}) %collective-permute-start.7) | collective-permute-done | bytes 32800 | tf_op jit(solution)/shard_map/ppermute | solution.py:446
  138.5 1.4 collective-permute-start.8
  140.6 2.1 edge.1
  142.7 0.9 collective-permute-start.9
  144.1 0.8 add.106
  144.9 0.9 collective-permute-start.16
  145.8 3.0 %collective-permute-done.16 = f32[64,64]{1,0:T(8,128)S(1)} collective-permute-done((f32[64,64]{1,0:T(8,128)S(1)}, f32[64,64]{1,0:T(8,128)S(1)}, u32[]{:S(2)}, u32[]{:S(2)}) %collective-permute-start.16) | collective-permute-done | bytes 16416 | tf_op jit(solution)/shard_map/ppermute | solution.py:446
  148.8 1.0 collective-permute-start.17
  150.4 9.1 %solve.1 = (f32[64,64]{1,0:T(8,128)}, f32[64,128]{1,0:T(8,128)}, f32[16,8,1024]{2,1,0:T(8,128)}, f32[16,8,1024]{2,1,0:T(8,128)}) custom-call(s32[1]{0:T(128)} %bitcast.place_ref, f32[64,128]{1,0:T(8,128)} %copy-done.10, f32[64,128]{1,0:T(8,128)} %copy-done.15, f32[8,64,1024]{2,1,0:T(8,128)} %get-tuple-element.13.lines_ref.refs_2_), custom_call_target="tpu_custom_call" | custom-call | tf_op jit(solution)/shard_map/solve/pallas_call | solution.py:463
  159.5 3.7 %near.1 = (f32[16,8,1024]{2,1,0:T(8,128)}, f32[16,8,1024]{2,1,0:T(8,128)}) custom-call(s32[1]{0:T(128)} %bitcast.place_ref, f32[64,64]{1,0:T(8,128)} %get-tuple-element.14.inv_ref, f32[8,64,1024]{2,1,0:T(8,128)} %get-tuple-element.13.lines_ref.refs_2_), custom_call_target="tpu_custom_call" | custom-call | tf_op jit(solution)/shard_map/near/pallas_call | solution.py:471
  163.2 1.1 collective-permute-start.10
  164.3 1.7 collective-permute-start.11
  166.0 1.1 collective-permute-start.18
  167.1 1.2 collective-permute-start.19
  168.3 1.3 collective-permute-start.20
  169.9 18.9 %collective-permute-done.18 = f32[64,64]{1,0:T(8,128)S(1)} collective-permute-done((f32[64,64]{1,0:T(8,128)S(1)}, f32[64,64]{1,0:T(8,128)S(1)}, u32[]{:S(2)}, u32[]{:S(2)}) %collective-permute-start.18) | collective-permute-done | bytes 16416 | tf_op jit(solution)/shard_map/ppermute | solution.py:455
  188.8 1.2 collective-permute-start.12
  190.0 12.5 %collective-permute-done.19 = f32[64,64]{1,0:T(8,128)S(1)} collective-permute-done((f32[64,64]{1,0:T(8,128)S(1)}, f32[64,64]{1,0:T(8,128)S(1)}, u32[]{:S(2)}, u32[]{:S(2)}) %collective-permute-start.19) | collective-permute-done | bytes 16416 | tf_op jit(solution)/shard_map/ppermute | solution.py:455
  202.5 1.7 collective-permute-done.20
  204.6 0.8 convolution_multiply_fusion
  205.5 8.5 %collective-permute-done.12 = f32[16,8,1024]{2,1,0:T(8,128)} collective-permute-done((f32[16,8,1024]{2,1,0:T(8,128)}, f32[16,8,1024]{2,1,0:T(8,128)}, u32[]{:S(2)}, u32[]{:S(2)}) %collective-permute-start.12) | collective-permute-done | bytes 524320 | tf_op jit(solution)/shard_map/ppermute | solution.py:481
  213.9 1.1 constant_dynamic-update-slice_fusion
  215.0 1.3 copy-done.4
  (74 shorter events, 4.6 us)
Async XLA Ops:
  0.6 6.2 %copy-start.13 = (s32[32,1024]{1,0:T(8,128)S(1)}, s32[32,1024]{1,0:T(8,128)}, u32[]{:S(2)}) copy-start(s32[32,1024]{1,0:T(8,128)} %param.4) | copy-start | bytes 393220
  3.0 24.9 %copy-start.5 = (f32[16,32,1024]{2,1,0:T(8,128)S(1)}, f32[16,32,1024]{2,1,0:T(8,128)}, u32[]{:S(2)}) copy-start(f32[16,32,1024]{2,1,0:T(8,128)} %param.3) | copy-start | bytes 6291460
  3.0 26.1 %all-to-all-start = ((f32[8,32,1024]{2,1,0:T(8,128)}), f32[8,32,1024]{2,1,0:T(8,128)S(1)}, u32[]{:S(2)}, u32[]{:S(2)}) async-start(f32[8,32,1024]{2,1,0:T(8,128)} %slice.33), calls=%async_computation | async-start | bytes 2097152 | tf_op jit(solution)/shard_map/all_to_all | solution.py:369
  7.5 17.2 %collective-permute-start.1 = (f32[32,1024]{1,0:T(8,128)}, f32[32,1024]{1,0:T(8,128)S(1)}, u32[]{:S(2)}, u32[]{:S(2)}) collective-permute-start(f32[32,1024]{1,0:T(8,128)} %convert_element_type.15.here_ref.refs_3_), channel_id=1, source_target_pairs={{0,8},{4,12},{8,0},{12,4},{16,24},{20,28},{24,16},{28,20},{1,9},{5... | collective-permute-start | bytes 393224 | tf_op jit(solution)/shard_map/ppermute | solution.py:363
  9.5 15.2 %collective-permute-start.2 = (f32[32,1024]{1,0:T(8,128)}, f32[32,1024]{1,0:T(8,128)S(1)}, u32[]{:S(2)}, u32[]{:S(2)}) collective-permute-start(f32[32,1024]{1,0:T(8,128)} %convert_element_type.15.here_ref.refs_3_), channel_id=1, source_target_pairs={{0,16},{4,20},{8,24},{12,28},{16,0},{20,4},{24,8},{28,12},{1,17},{... | collective-permute-start | bytes 393224 | tf_op jit(solution)/shard_map/ppermute | solution.py:363
  11.0 16.9 %collective-permute-start.3 = (f32[32,1024]{1,0:T(8,128)}, f32[32,1024]{1,0:T(8,128)S(1)}, u32[]{:S(2)}, u32[]{:S(2)}) collective-permute-start(f32[32,1024]{1,0:T(8,128)} %convert_element_type.15.here_ref.refs_3_), channel_id=1, source_target_pairs={{0,24},{4,28},{8,16},{12,20},{16,8},{20,12},{24,0},{28,4},{1,25},{... | collective-permute-start | bytes 393224 | tf_op jit(solution)/shard_map/ppermute | solution.py:363
  27.9 5.1 %copy-start.6 = (f32[3,32,1024]{2,1,0:T(8,128)}, f32[3,32,1024]{2,1,0:T(8,128)S(1)}, u32[]{:S(2)}) copy-start(f32[3,32,1024]{2,1,0:T(8,128)S(1)} %pad_maximum_fusion.own_ref) | copy-start | bytes 1179652
  27.9 5.1 %copy-start.17 = (s32[4]{0:T(128)S(1)}, s32[4]{0:T(128)}, u32[]{:S(2)}) copy-start(s32[4]{0:T(128)} %param.5) | copy-start | bytes 52
  29.1 14.8 %copy-start.2 = (f32[8,32,1024]{2,1,0:T(8,128)}, f32[8,32,1024]{2,1,0:T(8,128)S(1)}, u32[]{:S(2)}) copy-start(f32[8,32,1024]{2,1,0:T(8,128)S(1)} %all-to-all-done.vec_ref) | copy-start | bytes 3145732
  29.1 29.4 %all-to-all-start.2 = ((f32[8,32,1024]{2,1,0:T(8,128)}), f32[8,32,1024]{2,1,0:T(8,128)S(1)}, u32[]{:S(2)}, u32[]{:S(2)}) async-start(f32[8,32,1024]{2,1,0:T(8,128)} %slice.34), calls=%async_computation.2 | async-start | bytes 2097152 | tf_op jit(solution)/shard_map/all_to_all | solution.py:369
  32.6 6.1 %collective-permute-start = (f32[32,1024]{1,0:T(8,128)}, f32[32,1024]{1,0:T(8,128)S(1)}, u32[]{:S(2)}, u32[]{:S(2)}) collective-permute-start(f32[32,1024]{1,0:T(8,128)} %convert_element_type.15.here_ref.refs_3_), channel_id=1, source_target_pairs={{0,4},{4,0},{8,12},{12,8},{16,20},{20,16},{24,28},{28,24},{1,5},{5... | collective-permute-start | bytes 393224 | tf_op jit(solution)/shard_map/ppermute | solution.py:363
  33.0 5.7 %collective-permute-start.4 = (f32[3,32,1024]{2,1,0:T(8,128)S(1)}, f32[3,32,1024]{2,1,0:T(8,128)S(1)}, u32[]{:S(2)}, u32[]{:S(2)}) collective-permute-start(f32[3,32,1024]{2,1,0:T(8,128)S(1)} %pad_maximum_fusion.own_ref), channel_id=1, source_target_pairs={{0,4},{4,0},{8,12},{12,8},{16,20},{20,16},{24,28},{28,24},{1,5},{5... | collective-permute-start | bytes 1179656 | tf_op jit(solution)/shard_map/ppermute | solution.py:363
  38.8 0.7 copy-start.14
  38.8 0.8 copy-start.8
  58.4 6.4 %copy-start.3 = (f32[8,32,1024]{2,1,0:T(8,128)}, f32[8,32,1024]{2,1,0:T(8,128)S(1)}, u32[]{:S(2)}) copy-start(f32[8,32,1024]{2,1,0:T(8,128)S(1)} %all-to-all-done.2.vec_ref) | copy-start | bytes 3145732
  58.4 31.7 %all-to-all-start.1 = ((f32[32,8,1024]{2,1,0:T(8,128)}), f32[32,8,1024]{2,1,0:T(8,128)S(1)}, u32[]{:S(2)}, u32[]{:S(2)}) async-start(f32[32,8,1024]{2,1,0:T(8,128)} %bitcast.28), calls=%async_computation.1 | async-start | bytes 2097152 | tf_op jit(solution)/shard_map/all_to_all | solution.py:420
  90.1 31.4 %copy-start = (f32[32,8,1024]{2,1,0:T(8,128)}, f32[32,8,1024]{2,1,0:T(8,128)S(1)}, u32[]{:S(2)}) copy-start(f32[32,8,1024]{2,1,0:T(8,128)S(1)} %all-to-all-done.1.refs_0_) | copy-start | bytes 3145732
  90.1 29.8 %all-to-all-start.3 = ((f32[32,8,1024]{2,1,0:T(8,128)}), f32[32,8,1024]{2,1,0:T(8,128)S(1)}, u32[]{:S(2)}, u32[]{:S(2)}) async-start(f32[32,8,1024]{2,1,0:T(8,128)} %bitcast.27), calls=%async_computation.3 | async-start | bytes 2097152 | tf_op jit(solution)/shard_map/all_to_all | solution.py:420
  94.8 45.1 %collective-permute-start.13 = (f32[32,1024]{1,0:T(8,128)S(1)}, f32[32,1024]{1,0:T(8,128)S(1)}, u32[]{:S(2)}, u32[]{:S(2)}) collective-permute-start(f32[32,1024]{1,0:T(8,128)S(1)} %bitcast.29), channel_id=1, source_target_pairs={{1,0},{2,1},{3,2},{7,3},{6,7},{5,6},{4,5},{8,4},{9,8},{10,9},{11,1... | collective-permute-start | bytes 393224 | tf_op jit(solution)/shard_map/ppermute | solution.py:422
  120.0 1.5 copy-start.1
  120.1 19.8 %collective-permute-start.14 = (f32[32,1024]{1,0:T(8,128)S(1)}, f32[32,1024]{1,0:T(8,128)S(1)}, u32[]{:S(2)}, u32[]{:S(2)}) collective-permute-start(f32[32,1024]{1,0:T(8,128)S(1)} %bitcast.30), channel_id=1, source_target_pairs={{1,0},{2,1},{3,2},{7,3},{6,7},{5,6},{4,5},{8,4},{9,8},{10,9},{11,1... | collective-permute-start | bytes 393224 | tf_op jit(solution)/shard_map/ppermute | solution.py:422
  128.4 1.4 collective-permute-start.5
  130.6 3.9 %collective-permute-start.6 = (f32[64,128]{1,0:T(8,128)S(1)}, f32[64,128]{1,0:T(8,128)S(1)}, u32[]{:S(2)}, u32[]{:S(2)}) collective-permute-start(f32[64,128]{1,0:T(8,128)S(1)} %add.95), channel_id=1, source_target_pairs={{0,8},{4,12},{8,0},{12,4},{16,24},{20,28},{24,16},{28,20},{1,9},{5... | collective-permute-start | bytes 98312 | tf_op jit(solution)/shard_map/ppermute | solution.py:446
  134.5 3.9 %collective-permute-start.7 = (f32[64,128]{1,0:T(8,128)S(1)}, f32[64,128]{1,0:T(8,128)S(1)}, u32[]{:S(2)}, u32[]{:S(2)}) collective-permute-start(f32[64,128]{1,0:T(8,128)S(1)} %add.96), channel_id=1, source_target_pairs={{0,16},{4,20},{8,24},{12,28},{16,0},{20,4},{24,8},{28,12},{1,17},{... | collective-permute-start | bytes 98312 | tf_op jit(solution)/shard_map/ppermute | solution.py:446
  138.5 4.2 %collective-permute-start.8 = (f32[64,128]{1,0:T(8,128)S(1)}, f32[64,128]{1,0:T(8,128)S(1)}, u32[]{:S(2)}, u32[]{:S(2)}) collective-permute-start(f32[64,128]{1,0:T(8,128)S(1)} %add.97), channel_id=1, source_target_pairs={{0,1},{1,0},{2,3},{3,2},{4,5},{5,4},{6,7},{7,6},{8,9},{9,8},{10,11... | collective-permute-start | bytes 98312 | tf_op jit(solution)/shard_map/ppermute | solution.py:446
  139.9 0.6 copy-start.11
  139.9 0.7 copy-start.12
  142.7 1.4 collective-permute-start.15
  142.7 7.1 %copy-start.10 = (f32[64,128]{1,0:T(8,128)}, f32[64,128]{1,0:T(8,128)S(1)}, u32[]{:S(2)}) copy-start(f32[64,128]{1,0:T(8,128)S(1)} %add.98.mine_ref) | copy-start | bytes 98308
  142.7 7.1 %collective-permute-start.9 = (f32[64,128]{1,0:T(8,128)S(1)}, f32[64,128]{1,0:T(8,128)S(1)}, u32[]{:S(2)}, u32[]{:S(2)}) collective-permute-start(f32[64,128]{1,0:T(8,128)S(1)} %add.98.mine_ref), channel_id=1, source_target_pairs={{0,2},{1,3},{2,0},{3,1},{4,6},{5,7},{6,4},{7,5},{8,10},{9,11},{10,... | collective-permute-start | bytes 98312 | tf_op jit(solution)/shard_map/ppermute | solution.py:446
  144.9 3.9 %collective-permute-start.16 = (f32[64,64]{1,0:T(8,128)S(1)}, f32[64,64]{1,0:T(8,128)S(1)}, u32[]{:S(2)}, u32[]{:S(2)}) collective-permute-start(f32[64,64]{1,0:T(8,128)S(1)} %add.106), channel_id=1, source_target_pairs={{0,8},{4,12},{8,0},{12,4},{16,24},{20,28},{24,16},{28,20},{1,9},{5... | collective-permute-start | bytes 49160 | tf_op jit(solution)/shard_map/ppermute | solution.py:446
  148.8 17.2 %collective-permute-start.17 = (f32[64,64]{1,0:T(8,128)S(1)}, f32[64,64]{1,0:T(8,128)S(1)}, u32[]{:S(2)}, u32[]{:S(2)}) collective-permute-start(f32[64,64]{1,0:T(8,128)S(1)} %add.107), channel_id=1, source_target_pairs={{0,16},{4,20},{8,24},{12,28},{16,0},{20,4},{24,8},{28,12},{1,17},{... | collective-permute-start | bytes 49160 | tf_op jit(solution)/shard_map/ppermute | solution.py:446
  149.8 0.6 copy-start.15
  163.2 6.6 %copy-start.7 = (f32[16,8,1024]{2,1,0:T(8,128)S(1)}, f32[16,8,1024]{2,1,0:T(8,128)}, u32[]{:S(2)}) copy-start(f32[16,8,1024]{2,1,0:T(8,128)} %get-tuple-element.15) | copy-start | bytes 1572868
  163.2 41.0 %copy-start.16 = (f32[64,128]{1,0:T(8,128)S(1)}, f32[64,128]{1,0:T(8,128)}, u32[]{:S(2)}) copy-start(f32[64,128]{1,0:T(8,128)} %get-tuple-element.19) | copy-start | bytes 98308
  163.2 41.2 %copy-start.9 = (f32[64,64]{1,0:T(8,128)S(1)}, f32[64,64]{1,0:T(8,128)}, u32[]{:S(2)}) copy-start(f32[64,64]{1,0:T(8,128)} %get-tuple-element.14.inv_ref) | copy-start | bytes 49156
  163.2 42.2 %collective-permute-start.10 = (f32[16,8,1024]{2,1,0:T(8,128)}, f32[16,8,1024]{2,1,0:T(8,128)S(1)}, u32[]{:S(2)}, u32[]{:S(2)}) collective-permute-start(f32[16,8,1024]{2,1,0:T(8,128)} %get-tuple-element.16), channel_id=1, source_target_pairs={{0,1},{1,0},{2,3},{3,2},{4,5},{5,4},{6,7},{7,6},{8,9},{9,8},{10,11... | collective-permute-start | bytes 1572872 | tf_op jit(solution)/shard_map/ppermute | solution.py:481
  164.3 41.1 %collective-permute-start.11 = (f32[16,8,1024]{2,1,0:T(8,128)}, f32[16,8,1024]{2,1,0:T(8,128)S(1)}, u32[]{:S(2)}, u32[]{:S(2)}) collective-permute-start(f32[16,8,1024]{2,1,0:T(8,128)} %get-tuple-element.17), channel_id=1, source_target_pairs={{0,2},{1,3},{2,0},{3,1},{4,6},{5,7},{6,4},{7,5},{8,10},{9,11},{10,... | collective-permute-start | bytes 1572872 | tf_op jit(solution)/shard_map/ppermute | solution.py:481
  166.0 22.8 %collective-permute-start.18 = (f32[64,64]{1,0:T(8,128)S(1)}, f32[64,64]{1,0:T(8,128)S(1)}, u32[]{:S(2)}, u32[]{:S(2)}) collective-permute-start(f32[64,64]{1,0:T(8,128)S(1)} %add.108), channel_id=1, source_target_pairs={{0,1},{1,0},{2,3},{3,2},{4,5},{5,4},{6,7},{7,6},{8,9},{9,8},{10,11... | collective-permute-start | bytes 49160 | tf_op jit(solution)/shard_map/ppermute | solution.py:455
  167.1 35.4 %collective-permute-start.19 = (f32[64,64]{1,0:T(8,128)S(1)}, f32[64,64]{1,0:T(8,128)S(1)}, u32[]{:S(2)}, u32[]{:S(2)}) collective-permute-start(f32[64,64]{1,0:T(8,128)S(1)} %add.108), channel_id=1, source_target_pairs={{0,2},{1,3},{2,0},{3,1},{4,6},{5,7},{6,4},{7,5},{8,10},{9,11},{10,... | collective-permute-start | bytes 49160 | tf_op jit(solution)/shard_map/ppermute | solution.py:455
  168.3 35.9 %collective-permute-start.20 = (f32[64,64]{1,0:T(8,128)S(1)}, f32[64,64]{1,0:T(8,128)S(1)}, u32[]{:S(2)}, u32[]{:S(2)}) collective-permute-start(f32[64,64]{1,0:T(8,128)S(1)} %add.108), channel_id=1, source_target_pairs={{0,3},{1,2},{2,1},{3,0},{4,7},{5,6},{6,5},{7,4},{8,11},{9,10},{10,... | collective-permute-start | bytes 49160 | tf_op jit(solution)/shard_map/ppermute | solution.py:455
  188.8 25.2 %collective-permute-start.12 = (f32[16,8,1024]{2,1,0:T(8,128)}, f32[16,8,1024]{2,1,0:T(8,128)}, u32[]{:S(2)}, u32[]{:S(2)}) collective-permute-start(f32[16,8,1024]{2,1,0:T(8,128)} %get-tuple-element.18), channel_id=1, source_target_pairs={{0,3},{1,2},{2,1},{3,0},{4,7},{5,6},{6,5},{7,4},{8,11},{9,10},{10,... | collective-permute-start | bytes 1572872 | tf_op jit(solution)/shard_map/ppermute | solution.py:481
  215.0 1.3 copy-start.4

commit v4 on v3

--- a/solution.py
+++ b/solution.py
@@ -255,35 +255,38 @@
 
 def gram_kernel(*refs, chunks):
     slab_refs = refs[:chunks]
-    place_ref, pot_ref, out_ref, lines_ref = refs[chunks:]
-    slab_rows, total, columns = lines_ref.shape
+    place_ref, pot_ref, out_ref, first_ref, low_ref, high_ref = refs[chunks:]
+    slab_rows, total, width = low_ref.shape
+    columns = slab_refs[0].shape[2]
     acc = jnp.zeros(out_ref.shape, jnp.float32)
     for chunk in range(chunks):
         for group in range(total // (chunks * SUBLANES)):
             here = slice(group * SUBLANES, (group + 1) * SUBLANES)
             start = (group * chunks + chunk) * SUBLANES
-            lines_ref[:, start : start + SUBLANES, :] = jnp.swapaxes(slab_refs[chunk][here], 0, 1)
+            there = slice(start, start + SUBLANES)
+            value = jnp.swapaxes(slab_refs[chunk][here], 0, 1)
+            low_ref[:, there, :] = value[:, :, :width]
+            high_ref[:, there, :] = value[:, :, width:]
+            first_ref[there, :] = value[0]
+
+    def line(j):
+        return jnp.concatenate([low_ref[j], high_ref[j]], axis=1)
+
     levels = pot_ref[pl.ds(pl.multiple_of(place_ref[0] * slab_rows, SUBLANES), slab_rows), :]
     for j in range(slab_rows):
-        here = lines_ref[j]
+        here = line(j)
         level = levels[j : j + 1, :]
         pot = disorder * (level * (1.0 / (POT_LEVELS - 1)) - 0.5)
         image = pot * here - (pltpu.roll(here, 1, 1) + pltpu.roll(here, columns - 1, 1))
         if j < slab_rows - 1:
-            image = image - 2.0 * lines_ref[j + 1]
+            image = image - 2.0 * line(j + 1)
         acc = acc + outer(here, jnp.concatenate([here, image], axis=0))
     out_ref[...] = acc
 
 
-def edge_kernel(*refs, chunks):
-    next_refs = refs[:chunks]
-    last_ref, out_ref = refs[chunks:]
-    total = out_ref.shape[0]
-    parts = []
-    for group in range(total // (chunks * SUBLANES)):
-        for chunk in range(chunks):
-            parts.append(next_refs[chunk][group * SUBLANES : (group + 1) * SUBLANES, :])
-    out_ref[...] = -2.0 * outer(last_ref[0], jnp.concatenate(parts, axis=0))
+def edge_kernel(next_ref, low_ref, high_ref, out_ref):
+    last = jnp.concatenate([low_ref[0], high_ref[0]], axis=1)
+    out_ref[...] = -2.0 * outer(last, next_ref[...])
 
 
 def eliminate(sums):
@@ -315,31 +318,38 @@
     return jnp.concatenate(result, axis=0)[:, total:]
 
 
-def products(inv_ref, lines_ref, done_ref, out_refs, place, scale, targets, half):
-    slab_rows = lines_ref.shape[0]
-    vec_local = out_refs[0].shape[0]
+def products(inv_ref, sources, done_ref, place, scale, targets, half, vec_local):
     first = ((place ^ targets[0]) // half) * half
     weights = scale * inv_ref[pl.ds(pl.multiple_of(first * vec_local, SUBLANES), half * vec_local), :]
-    for j in range(slab_rows):
-        done_ref[j] = jnp.dot(
-            weights, lines_ref[j], precision=lax.Precision.HIGHEST, preferred_element_type=jnp.float32
-        )
-    for d, out_ref in zip(targets, out_refs):
-        start = ((place ^ d) - first) * vec_local
-        for vec in range(0, vec_local, SUBLANES):
-            rows = pl.ds(pl.multiple_of(start + vec, SUBLANES), SUBLANES)
-            out_ref[vec : vec + SUBLANES] = jnp.swapaxes(done_ref[:, rows, :], 0, 1)
-
-
-def solve_kernel(place_ref, mine_ref, other_ref, lines_ref, inv_ref, sums_ref, *rest, scale, targets, half):
+    for lines_ref, out_refs, at in sources:
+        slab_rows, _, width = lines_ref.shape
+        for j in range(slab_rows):
+            done_ref[j] = jnp.dot(
+                weights, lines_ref[j], precision=lax.Precision.HIGHEST, preferred_element_type=jnp.float32
+            )
+        for d, out_ref in zip(targets, out_refs):
+            start = ((place ^ d) - first) * vec_local
+            for vec in range(0, vec_local, SUBLANES):
+                rows = pl.ds(pl.multiple_of(start + vec, SUBLANES), SUBLANES)
+                out_ref[vec : vec + SUBLANES, :, at : at + width] = jnp.swapaxes(done_ref[:, rows, :], 0, 1)
+
+
+def solve_kernel(place_ref, mine_ref, other_ref, low_ref, high_ref, inv_ref, sums_ref, *rest, **static):
     sums = mine_ref[...] + other_ref[...]
     sums_ref[...] = sums
     inv_ref[...] = eliminate(sums)
-    products(inv_ref, lines_ref, rest[-1], rest[:-1], place_ref[0], scale, targets, half)
-
-
-def near_kernel(place_ref, inv_ref, lines_ref, *rest, scale, targets, half):
-    products(inv_ref, lines_ref, rest[-1], rest[:-1], place_ref[0], scale, targets, half)
+    half = static["half"]
+    sources = [(low_ref, rest[:half], 0), (high_ref, rest[half : 2 * half], 0)]
+    products(inv_ref, sources, rest[-1], place_ref[0], **static)
+
+
+def near_kernel(place_ref, inv_ref, low_ref, high_ref, *rest, **static):
+    sources = [(low_ref, rest[:-1], 0), (high_ref, rest[:-1], low_ref.shape[2])]
+    products(inv_ref, sources, rest[-1], place_ref[0], **static)
+
+
+def extra_kernel(place_ref, inv_ref, lines_ref, *rest, **static):
+    products(inv_ref, [(lines_ref, rest[:-1], 0)], rest[-1], place_ref[0], **static)
 
 
 def whole_shards(start_vectors, potential, bounds):
@@ -400,7 +410,7 @@
         + staging,
         name="site",
     )(terms, me[None], level, beside, own_pots, other_pots)
-    slabs, nexts = [], []
+    slabs = []
     holders = [p * groups + turned(s, p, groups) for p in range(strips) for s in range(groups)]
     ring = [(holders[(g + 1) % devices], holders[g]) for g in range(devices)]
     for chunk in range(vecs):
@@ -419,26 +429,36 @@
         )(terms, inner[chunk], site)
         slab = lax.all_to_all(done.reshape(devices, slab_rows, columns), both, split_axis=0, concat_axis=0, tiled=True)
         slabs.append(slab)
-        nexts.append(lax.ppermute(slab[:, 0], ("strip", "vec"), ring))
 
     place = lax.axis_index("vec").astype(jnp.int32)
-    lines_shape = (slab_rows, total_vecs, columns)
+    width = columns // 2
+    lines_shape = jax.ShapeDtypeStruct((slab_rows, total_vecs, width), jnp.float32)
     sums_shape = jax.ShapeDtypeStruct((total_vecs, 2 * total_vecs), jnp.float32)
-    sums, lines = pl.pallas_call(
+    sums, first_row, low, high = pl.pallas_call(
         functools.partial(gram_kernel, chunks=vecs),
         in_specs=[vmem] * vecs + [smem, vmem],
-        out_specs=[vmem, vmem],
-        out_shape=[sums_shape, jax.ShapeDtypeStruct(lines_shape, jnp.float32)],
+        out_specs=[vmem] * 4,
+        out_shape=[
+            sums_shape,
+            jax.ShapeDtypeStruct((total_vecs, columns), jnp.float32),
+            lines_shape,
+            lines_shape,
+        ],
         name="gram",
     )(*slabs, turned(place, me, groups)[None], level)
+    next_row = lax.ppermute(first_row, ("strip", "vec"), ring)
+    half = groups // 2
+    middle = (half - 1, half)
+    raw = lax.ppermute(high, "vec", [middle, middle[::-1]])
+    last_row = pl.BlockSpec((1, total_vecs, width), lambda i: (slab_rows - 1, 0, 0))
     edge = pl.pallas_call(
-        functools.partial(edge_kernel, chunks=vecs),
+        edge_kernel,
         grid=(1,),
-        in_specs=[vmem] * vecs + [pl.BlockSpec((1, total_vecs, columns), lambda i: (slab_rows - 1, 0, 0))],
+        in_specs=[vmem, last_row, last_row],
         out_specs=vmem,
         out_shape=jax.ShapeDtypeStruct((total_vecs, total_vecs), jnp.float32),
         name="edge",
-    )(*nexts, lines)
+    )(next_row, low, high)
 
     def pairwise(value, order):
         rounds = [(axis, count, 1 << n) for axis, count in order for n in range(count.bit_length() - 1)]
@@ -448,44 +468,66 @@
                 value = value + other
         return value, other
 
-    sums, pending = pairwise(sums, (("strip", strips), ("vec", groups)))
-    edge = sum(pairwise(edge, (("strip", strips),)))
+    sums, pending = pairwise(sums, (("vec", groups), ("strip", strips)))
+    mine, other = pairwise(edge, (("strip", strips),))
+    edge = mine + other
     others = []
     for d in range(1, groups):
         others.append(lax.ppermute(edge, "vec", [(i, i ^ d) for i in range(groups)]))
     edge = edge + sum(others)
 
-    scale = math.sqrt(strips * rows * columns)
-    half = groups // 2
+    static = dict(scale=math.sqrt(strips * rows * columns), half=half, vec_local=vec_local)
     far, near = tuple(range(half, groups)), tuple(range(half))
     piece = jax.ShapeDtypeStruct((vec_local, slab_rows, columns), jnp.float32)
-    products_scratch = [pltpu.VMEM((slab_rows, half * vec_local, columns), jnp.float32)]
-    inverse, gram_cross, *far_blocks = pl.pallas_call(
-        functools.partial(solve_kernel, scale=scale, targets=far, half=half),
-        in_specs=[smem, vmem, vmem, vmem],
-        out_specs=[vmem] * (2 + half),
-        out_shape=[jax.ShapeDtypeStruct((total_vecs, total_vecs), jnp.float32), sums_shape] + [piece] * half,
+    part_piece = jax.ShapeDtypeStruct((vec_local, slab_rows, width), jnp.float32)
+    products_scratch = [pltpu.VMEM((slab_rows, half * vec_local, width), jnp.float32)]
+    inverse, gram_cross, *blocks = pl.pallas_call(
+        functools.partial(solve_kernel, targets=far, **static),
+        in_specs=[smem] + [vmem] * 4,
+        out_specs=[vmem] * (2 + 2 * half),
+        out_shape=[jax.ShapeDtypeStruct((total_vecs, total_vecs), jnp.float32), sums_shape]
+        + [part_piece] * (2 * half),
         scratch_shapes=products_scratch,
         name="solve",
-    )(place[None], sums, pending, lines)
-    near_blocks = pl.pallas_call(
-        functools.partial(near_kernel, scale=scale, targets=near, half=half),
-        in_specs=[smem, vmem, vmem],
+    )(place[None], sums, pending, low, high)
+    own_block, beside_block = pl.pallas_call(
+        functools.partial(near_kernel, targets=near, **static),
+        in_specs=[smem] + [vmem] * 3,
         out_specs=[vmem] * half,
         out_shape=[piece] * half,
         scratch_shapes=products_scratch,
         name="near",
-    )(place[None], inverse, lines)
-
-    def across(block, d):
-        return lax.ppermute(block, "vec", [(i, i ^ d) for i in range(groups)]) if d else block
-
-    far_blocks = [across(block, d) for d, block in zip(far, far_blocks)]
-    near_blocks = [across(block, d) for d, block in zip(near, near_blocks)]
+    )(place[None], inverse, low, high)
+    own_extra, beside_extra = pl.pallas_call(
+        functools.partial(extra_kernel, targets=near, **static),
+        in_specs=[smem] + [vmem] * 2,
+        out_specs=[vmem] * half,
+        out_shape=[part_piece] * half,
+        scratch_shapes=products_scratch,
+        name="extra",
+    )(place[None], inverse, raw)
+
+    def across(block, d, sources=range(groups)):
+        return lax.ppermute(block, "vec", [(i, i ^ d) for i in sources])
+
+    outer_groups = [i for i in range(groups) if i not in middle]
+    far_high = [across(block, d, outer_groups) for d, block in zip(far, blocks[half:])]
+    far_low = [across(block, d) for d, block in zip(far, blocks[:half])]
+    beside_block = across(beside_block, 1)
+    beside_extra = across(beside_extra, 1, middle)
+    far_high = [far_high[0] + beside_extra, far_high[1] + own_extra]
+
     ortho_basis = jnp.zeros((vec_local, rows, columns), jnp.float32)
-    for d, block in zip(near + far, near_blocks + far_blocks):
+    for d, block, at in (
+        (0, own_block, 0),
+        (1, beside_block, 0),
+        (2, far_low[0], 0),
+        (3, far_low[1], 0),
+        (2, far_high[0], width),
+        (3, far_high[1], width),
+    ):
         start = turned(place ^ d, me, groups) * slab_rows
-        ortho_basis = lax.dynamic_update_slice(ortho_basis, block, (0, start, 0))
+        ortho_basis = lax.dynamic_update_slice(ortho_basis, block, (0, start, at))
 
     cross_half = gram_cross[:, total_vecs:] + edge
     cross_sum = 0.5 * (cross_half + cross_half.T)
@@ -503,7 +545,7 @@
         and columns % (LANES * SUBLANES) == 0
         and LANES % rows == 0
         and strips * rows % LANES == 0
-        and groups >= 2
+        and groups == 4
         and devices & (devices - 1) == 0
         and vec_local % SUBLANES == 0
         and 2 * vec_local * groups == LANES

time: 217 us -> 238 us (1.097)
  the two profiles are of different devices: /device:TPU:8 before, /device:TPU:0 now
where the time goes in v4:
time: 238 us; the launch traced here: 236 us
  waiting for transfers between devices  105 us (44%)
  Pallas kernels  57.6 us (24%)
  starting transfers between devices  50.3 us (21%)
  local copies, waits for them, and re-layouts  11 us (5%)
  between operations  5.28 us (2%)
  other arithmetic  5.04 us (2%)
    all_to_all x2, waiting for transfers between devices, whole_shards(): lax.all_to_all(done.reshape(devices, slab_rows, columns), both, split_axi...  37.6 us
    pallas_call x2, Pallas kernels, whole_shards(): pl.pallas_call(functools.partial(filter_kernel, slabs=groups), in_specs=[...  29.2 us
    ppermute x8, waiting for transfers between devices, pairwise(): other = lax.ppermute(value, axis, [(i, i ^ bit) for i in range(count)])  27.4 us
    ppermute x5, waiting for transfers between devices, swap(): return lax.ppermute(value, 'strip', [(i, i ^ bit) for i in range(strips)])  16.9 us
    ppermute x6, waiting for transfers between devices, across(): return lax.ppermute(block, 'vec', [(i, i ^ d) for i in sources])  13.5 us
    ppermute x6, starting transfers between devices, across(): return lax.ppermute(block, 'vec', [(i, i ^ d) for i in sources])  11.8 us
    all_to_all x2, starting transfers between devices, whole_shards(): lax.all_to_all(done.reshape(devices, slab_rows, columns), both, split_axi...  9.99 us
    ppermute x3, waiting for transfers between devices, whole_shards(): lax.ppermute(edge, 'vec', [(i, i ^ d) for i in range(groups)])  9.95 us
  transfers between devices with their start and end apart: 28, of which 12 were waited for; matrix products, arithmetic and copies ran while one was open for 4% of the time, Pallas kernels for 22%

profile of v4, /device:TPU:0, one launch (start us, length us, event | category | flops | bytes accessed | tf_op | source)
XLA Modules:
  0.0 235.5 jit_solution(13375210771240488160)
XLA Ops:
  0.6 2.3 slice.27
  3.0 5.3 %all-to-all-start = ((f32[8,32,1024]{2,1,0:T(8,128)}), f32[8,32,1024]{2,1,0:T(8,128)S(1)}, u32[]{:S(2)}, u32[]{:S(2)}) async-start(f32[8,32,1024]{2,1,0:T(8,128)} %slice.27), calls=%async_computation | async-start | bytes 2097152 | tf_op jit(solution)/shard_map/all_to_all | solution.py:379
  9.0 2.0 collective-permute-start.1
  11.0 1.5 collective-permute-start.2
  12.5 13.8 %collective-permute-done.1 = f32[32,1024]{1,0:T(8,128)S(1)} collective-permute-done((f32[32,1024]{1,0:T(8,128)}, f32[32,1024]{1,0:T(8,128)S(1)}, u32[]{:S(2)}, u32[]{:S(2)}) %collective-permute-start.1) | collective-permute-done | bytes 131104 | tf_op jit(solution)/shard_map/ppermute | solution.py:373
  26.2 3.1 %collective-permute-done.3 = f32[32,1024]{1,0:T(8,128)S(1)} collective-permute-done((f32[32,1024]{1,0:T(8,128)}, f32[32,1024]{1,0:T(8,128)S(1)}, u32[]{:S(2)}, u32[]{:S(2)}) %collective-permute-start.3) | collective-permute-done | bytes 131104 | tf_op jit(solution)/shard_map/ppermute | solution.py:373
  29.4 1.1 slice.28
  30.5 3.6 %all-to-all-start.2 = ((f32[8,32,1024]{2,1,0:T(8,128)}), f32[8,32,1024]{2,1,0:T(8,128)S(1)}, u32[]{:S(2)}, u32[]{:S(2)}) async-start(f32[8,32,1024]{2,1,0:T(8,128)} %slice.28), calls=%async_computation.2 | async-start | bytes 2097152 | tf_op jit(solution)/shard_map/all_to_all | solution.py:379
  41.3 4.2 %site.1 = f32[32,8,8,128]{3,2,1,0:T(8,128)} custom-call(f32[35]{0:T(128)} %pad_maximum_fusion.1.coef_ref, s32[1]{0:T(128)} %bitcast.6.me_ref, f32[32,1024]{1,0:T(8,128)} %convert_element_type.15.here_ref.refs_3_, f32[32,1024]{1,0:T(8,128)} %copy-done.15, f32[3,32,1024]{2,1,0:T(8,128)} %copy-done.6, f32[3,32,1024]{2,1,0:T(8,128)} %copy-done.10), custom_call_target="tpu_custom_call" | custom-call | tf_op jit(solution)/shard_map/site/pallas_call | solution.py:401
  45.5 14.6 %filter.2 = f32[4,8,8,1024]{3,2,1,0:T(8,128)} custom-call(f32[35]{0:T(128)} %pad_maximum_fusion.1.coef_ref, f32[8,32,1024]{2,1,0:T(8,128)} %copy-done.2, f32[32,8,8,128]{3,2,1,0:T(8,128)} %site.1), custom_call_target="tpu_custom_call" | custom-call | tf_op jit(solution)/shard_map/filter/pallas_call | solution.py:417
  60.1 6.2 %all-to-all-start.1 = ((f32[32,8,1024]{2,1,0:T(8,128)}), f32[32,8,1024]{2,1,0:T(8,128)S(1)}, u32[]{:S(2)}, u32[]{:S(2)}) async-start(f32[32,8,1024]{2,1,0:T(8,128)} %bitcast.22), calls=%async_computation.1 | async-start | bytes 2097152 | tf_op jit(solution)/shard_map/all_to_all | solution.py:430
  66.4 14.6 %filter.3 = f32[4,8,8,1024]{3,2,1,0:T(8,128)} custom-call(f32[35]{0:T(128)} %pad_maximum_fusion.1.coef_ref, f32[8,32,1024]{2,1,0:T(8,128)} %copy-done.3, f32[32,8,8,128]{3,2,1,0:T(8,128)} %site.1), custom_call_target="tpu_custom_call" | custom-call | tf_op jit(solution)/shard_map/filter/pallas_call | solution.py:417
  81.0 11.6 %all-to-all-done.1.refs_0_ = f32[32,8,1024]{2,1,0:T(8,128)S(1)} async-done(((f32[32,8,1024]{2,1,0:T(8,128)}), f32[32,8,1024]{2,1,0:T(8,128)S(1)}, u32[]{:S(2)}, u32[]{:S(2)}) %all-to-all-start.1) | async-done | bytes 1048608 | tf_op jit(solution)/shard_map/all_to_all | solution.py:430
  92.5 3.8 %all-to-all-start.3 = ((f32[32,8,1024]{2,1,0:T(8,128)}), f32[32,8,1024]{2,1,0:T(8,128)S(1)}, u32[]{:S(2)}, u32[]{:S(2)}) async-start(f32[32,8,1024]{2,1,0:T(8,128)} %bitcast.21), calls=%async_computation.3 | async-start | bytes 2097152 | tf_op jit(solution)/shard_map/all_to_all | solution.py:430
  96.4 26.0 %all-to-all-done.3.refs_1_ = f32[32,8,1024]{2,1,0:T(8,128)S(1)} async-done(((f32[32,8,1024]{2,1,0:T(8,128)}), f32[32,8,1024]{2,1,0:T(8,128)S(1)}, u32[]{:S(2)}, u32[]{:S(2)}) %all-to-all-start.3) | async-done | bytes 1048608 | tf_op jit(solution)/shard_map/all_to_all | solution.py:430
  122.4 1.0 copy-done.1
  123.4 7.0 %gram.1 = (f32[64,128]{1,0:T(8,128)}, f32[64,1024]{1,0:T(8,128)}, f32[8,64,512]{2,1,0:T(8,128)}, f32[8,64,512]{2,1,0:T(8,128)}) custom-call(f32[32,8,1024]{2,1,0:T(8,128)} %copy-done, f32[32,8,1024]{2,1,0:T(8,128)} %copy-done.1, s32[1]{0:T(128)} %bitcast.12.refs_2_, f32[32,1024]{1,0:T(8,128)} %convert_element_type.15.here_ref.refs_3_), custom_call_target="tpu_custom_call" | custom-call | tf_op jit(solution)/shard_map/gram/pallas_call | solution.py:437
  130.3 1.4 collective-permute-start.17
  132.5 2.7 %collective-permute-start.5 = (f32[64,128]{1,0:T(8,128)}, f32[64,128]{1,0:T(8,128)S(1)}, u32[]{:S(2)}, u32[]{:S(2)}) collective-permute-start(f32[64,128]{1,0:T(8,128)} %get-tuple-element.18), channel_id=1, source_target_pairs={{0,1},{1,0},{2,3},{3,2},{4,5},{5,4},{6,7},{7,6},{8,9},{9,8},{10,11... | collective-permute-start | bytes 98312 | tf_op jit(solution)/shard_map/ppermute | solution.py:466
  135.2 2.4 %collective-permute-done.5 = f32[64,128]{1,0:T(8,128)S(1)} collective-permute-done((f32[64,128]{1,0:T(8,128)}, f32[64,128]{1,0:T(8,128)S(1)}, u32[]{:S(2)}, u32[]{:S(2)}) %collective-permute-start.5) | collective-permute-done | bytes 32800 | tf_op jit(solution)/shard_map/ppermute | solution.py:466
  138.4 2.3 collective-permute-start.6
  140.7 20.4 %collective-permute-done.6 = f32[64,128]{1,0:T(8,128)S(1)} collective-permute-done((f32[64,128]{1,0:T(8,128)S(1)}, f32[64,128]{1,0:T(8,128)S(1)}, u32[]{:S(2)}, u32[]{:S(2)}) %collective-permute-start.6) | collective-permute-done | bytes 32800 | tf_op jit(solution)/shard_map/ppermute | solution.py:466
  161.1 1.2 collective-permute-done.7
  162.3 0.8 collective-permute-start.8
  163.8 2.0 edge.1
  166.2 1.3 collective-permute-start.9
  167.5 0.8 add.120
  168.3 0.9 collective-permute-start.19
  169.2 3.0 %collective-permute-done.19 = f32[64,64]{1,0:T(8,128)S(1)} collective-permute-done((f32[64,64]{1,0:T(8,128)S(1)}, f32[64,64]{1,0:T(8,128)S(1)}, u32[]{:S(2)}, u32[]{:S(2)}) %collective-permute-start.19) | collective-permute-done | bytes 16416 | tf_op jit(solution)/shard_map/ppermute | solution.py:466
  172.2 0.8 collective-permute-start.20
  173.6 8.9 %solve.1 = (f32[64,64]{1,0:T(8,128)}, f32[64,128]{1,0:T(8,128)}, f32[16,8,512]{2,1,0:T(8,128)}, f32[16,8,512]{2,1,0:T(8,128)}, f32[16,8,512]{2,1,0:T(8,128)}, /*index=5*/f32[16,8,512]{2,1,0:T(8,128)}) custom-call(s32[1]{0:T(128)} %bitcast.place_ref, f32[64,128]{1,0:T(8,128)} %copy-done.13, f32[64,128]{1,0:T(8,128)} %copy-done.16, ...), custom_call_target="tpu_custom_call" | custom-call | tf_op jit(solution)/shard_map/solve/pallas_call | solution.py:484
  182.5 3.6 %near.1 = (f32[16,8,1024]{2,1,0:T(8,128)}, f32[16,8,1024]{2,1,0:T(8,128)}) custom-call(s32[1]{0:T(128)} %bitcast.place_ref, f32[64,64]{1,0:T(8,128)} %get-tuple-element.21.inv_ref, f32[8,64,512]{2,1,0:T(8,128)} %get-tuple-element.19.low_ref, f32[8,64,512]{2,1,0:T(8,128)} %get-tuple-element.20.high_ref), custom_call_target="tpu_custom_call" | custom-call | tf_op jit(solution)/shard_map/near/pallas_call | solution.py:493
  186.3 2.1 collective-permute-start.21
  188.5 2.3 collective-permute-start.23
  191.1 9.9 %collective-permute-done.21 = f32[64,64]{1,0:T(8,128)S(1)} collective-permute-done((f32[64,64]{1,0:T(8,128)S(1)}, f32[64,64]{1,0:T(8,128)S(1)}, u32[]{:S(2)}, u32[]{:S(2)}) %collective-permute-start.21) | collective-permute-done | bytes 16416 | tf_op jit(solution)/shard_map/ppermute | solution.py:476
  201.0 1.9 collective-permute-start.12
  203.0 4.0 %collective-permute-start.13 = (f32[16,8,512]{2,1,0:T(8,128)}, f32[16,8,512]{2,1,0:T(8,128)}, u32[]{:S(2)}, u32[]{:S(2)}) collective-permute-start(f32[16,8,512]{2,1,0:T(8,128)} %get-tuple-element.26), channel_id=1, source_target_pairs={{0,2},{3,1},{4,6},{7,5},{8,10},{11,9},{12,14},{15,13},{16,18},{19,... | collective-permute-start | bytes 786440 | tf_op jit(solution)/shard_map/ppermute | solution.py:511
  207.3 0.8 convolution_multiply_fusion
  208.1 4.4 %collective-permute-start.16 = (f32[16,8,512]{2,1,0:T(8,128)}, f32[16,8,512]{2,1,0:T(8,128)}, u32[]{:S(2)}, u32[]{:S(2)}) collective-permute-start(f32[16,8,512]{2,1,0:T(8,128)} %get-tuple-element.28), channel_id=1, source_target_pairs={{0,3},{3,0},{4,7},{7,4},{8,11},{11,8},{12,15},{15,12},{16,19},{19,... | collective-permute-start | bytes 786440 | tf_op jit(solution)/shard_map/ppermute | solution.py:511
  212.6 2.6 %extra.1 = (f32[16,8,512]{2,1,0:T(8,128)}, f32[16,8,512]{2,1,0:T(8,128)}) custom-call(s32[1]{0:T(128)} %bitcast.place_ref, f32[64,64]{1,0:T(8,128)} %get-tuple-element.21.inv_ref, f32[8,64,512]{2,1,0:T(8,128)} %copy-done.7), custom_call_target="tpu_custom_call" | custom-call | tf_op jit(solution)/shard_map/extra/pallas_call | solution.py:501
  215.2 1.4 collective-permute-start.15
  216.6 1.1 constant_dynamic-update-slice_fusion.2
  217.7 11.7 %collective-permute-done.11 = f32[16,8,512]{2,1,0:T(8,128)S(1)} collective-permute-done((f32[16,8,512]{2,1,0:T(8,128)}, f32[16,8,512]{2,1,0:T(8,128)S(1)}, u32[]{:S(2)}, u32[]{:S(2)}) %collective-permute-start.11) | collective-permute-done | bytes 262176 | tf_op jit(solution)/shard_map/ppermute | solution.py:511
  229.5 1.0 constant_dynamic-update-slice_fusion
  230.5 1.7 collective-permute-done.15
  232.2 1.0 add_dynamic-update-slice_fusion.1
  233.2 1.0 add_dynamic-update-slice_fusion
  234.2 1.3 copy-done.4
  (81 shorter events, 7.7 us)
Async XLA Ops:
  0.6 7.7 %copy-start.14 = (s32[32,1024]{1,0:T(8,128)S(1)}, s32[32,1024]{1,0:T(8,128)}, u32[]{:S(2)}) copy-start(s32[32,1024]{1,0:T(8,128)} %param.4) | copy-start | bytes 393220
  3.0 26.4 %copy-start.5 = (f32[16,32,1024]{2,1,0:T(8,128)S(1)}, f32[16,32,1024]{2,1,0:T(8,128)}, u32[]{:S(2)}) copy-start(f32[16,32,1024]{2,1,0:T(8,128)} %param.3) | copy-start | bytes 6291460
  3.0 27.5 %all-to-all-start = ((f32[8,32,1024]{2,1,0:T(8,128)}), f32[8,32,1024]{2,1,0:T(8,128)S(1)}, u32[]{:S(2)}, u32[]{:S(2)}) async-start(f32[8,32,1024]{2,1,0:T(8,128)} %slice.27), calls=%async_computation | async-start | bytes 2097152 | tf_op jit(solution)/shard_map/all_to_all | solution.py:379
  9.0 17.2 %collective-permute-start.1 = (f32[32,1024]{1,0:T(8,128)}, f32[32,1024]{1,0:T(8,128)S(1)}, u32[]{:S(2)}, u32[]{:S(2)}) collective-permute-start(f32[32,1024]{1,0:T(8,128)} %convert_element_type.15.here_ref.refs_3_), channel_id=1, source_target_pairs={{0,8},{4,12},{8,0},{12,4},{16,24},{20,28},{24,16},{28,20},{1,9},{5... | collective-permute-start | bytes 393224 | tf_op jit(solution)/shard_map/ppermute | solution.py:373
  11.0 15.2 %collective-permute-start.2 = (f32[32,1024]{1,0:T(8,128)}, f32[32,1024]{1,0:T(8,128)S(1)}, u32[]{:S(2)}, u32[]{:S(2)}) collective-permute-start(f32[32,1024]{1,0:T(8,128)} %convert_element_type.15.here_ref.refs_3_), channel_id=1, source_target_pairs={{0,16},{4,20},{8,24},{12,28},{16,0},{20,4},{24,8},{28,12},{1,17},{... | collective-permute-start | bytes 393224 | tf_op jit(solution)/shard_map/ppermute | solution.py:373
  12.5 16.9 %collective-permute-start.3 = (f32[32,1024]{1,0:T(8,128)}, f32[32,1024]{1,0:T(8,128)S(1)}, u32[]{:S(2)}, u32[]{:S(2)}) collective-permute-start(f32[32,1024]{1,0:T(8,128)} %convert_element_type.15.here_ref.refs_3_), channel_id=1, source_target_pairs={{0,24},{4,28},{8,16},{12,20},{16,8},{20,12},{24,0},{28,4},{1,25},{... | collective-permute-start | bytes 393224 | tf_op jit(solution)/shard_map/ppermute | solution.py:373
  29.4 5.1 %copy-start.6 = (f32[3,32,1024]{2,1,0:T(8,128)}, f32[3,32,1024]{2,1,0:T(8,128)S(1)}, u32[]{:S(2)}) copy-start(f32[3,32,1024]{2,1,0:T(8,128)S(1)} %pad_maximum_fusion.own_ref) | copy-start | bytes 1179652
  29.4 5.1 %copy-start.18 = (s32[4]{0:T(128)S(1)}, s32[4]{0:T(128)}, u32[]{:S(2)}) copy-start(s32[4]{0:T(128)} %param.5) | copy-start | bytes 52
  30.5 15.0 %copy-start.2 = (f32[8,32,1024]{2,1,0:T(8,128)}, f32[8,32,1024]{2,1,0:T(8,128)S(1)}, u32[]{:S(2)}) copy-start(f32[8,32,1024]{2,1,0:T(8,128)S(1)} %all-to-all-done.vec_ref) | copy-start | bytes 3145732
  30.5 29.6 %all-to-all-start.2 = ((f32[8,32,1024]{2,1,0:T(8,128)}), f32[8,32,1024]{2,1,0:T(8,128)S(1)}, u32[]{:S(2)}, u32[]{:S(2)}) async-start(f32[8,32,1024]{2,1,0:T(8,128)} %slice.28), calls=%async_computation.2 | async-start | bytes 2097152 | tf_op jit(solution)/shard_map/all_to_all | solution.py:379
  34.1 6.4 %collective-permute-start = (f32[32,1024]{1,0:T(8,128)}, f32[32,1024]{1,0:T(8,128)S(1)}, u32[]{:S(2)}, u32[]{:S(2)}) collective-permute-start(f32[32,1024]{1,0:T(8,128)} %convert_element_type.15.here_ref.refs_3_), channel_id=1, source_target_pairs={{0,4},{4,0},{8,12},{12,8},{16,20},{20,16},{24,28},{28,24},{1,5},{5... | collective-permute-start | bytes 393224 | tf_op jit(solution)/shard_map/ppermute | solution.py:373
  34.5 6.0 %collective-permute-start.4 = (f32[3,32,1024]{2,1,0:T(8,128)S(1)}, f32[3,32,1024]{2,1,0:T(8,128)S(1)}, u32[]{:S(2)}, u32[]{:S(2)}) collective-permute-start(f32[3,32,1024]{2,1,0:T(8,128)S(1)} %pad_maximum_fusion.own_ref), channel_id=1, source_target_pairs={{0,4},{4,0},{8,12},{12,8},{16,20},{20,16},{24,28},{28,24},{1,5},{5... | collective-permute-start | bytes 1179656 | tf_op jit(solution)/shard_map/ppermute | solution.py:373
  40.5 0.6 copy-start.15
  40.5 0.8 copy-start.10
  60.1 6.2 %copy-start.3 = (f32[8,32,1024]{2,1,0:T(8,128)}, f32[8,32,1024]{2,1,0:T(8,128)S(1)}, u32[]{:S(2)}) copy-start(f32[8,32,1024]{2,1,0:T(8,128)S(1)} %all-to-all-done.2.vec_ref) | copy-start | bytes 3145732
  60.1 32.4 %all-to-all-start.1 = ((f32[32,8,1024]{2,1,0:T(8,128)}), f32[32,8,1024]{2,1,0:T(8,128)S(1)}, u32[]{:S(2)}, u32[]{:S(2)}) async-start(f32[32,8,1024]{2,1,0:T(8,128)} %bitcast.22), calls=%async_computation.1 | async-start | bytes 2097152 | tf_op jit(solution)/shard_map/all_to_all | solution.py:430
  92.5 29.8 %copy-start = (f32[32,8,1024]{2,1,0:T(8,128)}, f32[32,8,1024]{2,1,0:T(8,128)S(1)}, u32[]{:S(2)}) copy-start(f32[32,8,1024]{2,1,0:T(8,128)S(1)} %all-to-all-done.1.refs_0_) | copy-start | bytes 3145732
  92.5 29.8 %all-to-all-start.3 = ((f32[32,8,1024]{2,1,0:T(8,128)}), f32[32,8,1024]{2,1,0:T(8,128)S(1)}, u32[]{:S(2)}, u32[]{:S(2)}) async-start(f32[32,8,1024]{2,1,0:T(8,128)} %bitcast.21), calls=%async_computation.3 | async-start | bytes 2097152 | tf_op jit(solution)/shard_map/all_to_all | solution.py:430
  122.4 1.0 copy-start.1
  130.3 32.8 %collective-permute-start.17 = (f32[64,1024]{1,0:T(8,128)}, f32[64,1024]{1,0:T(8,128)S(1)}, u32[]{:S(2)}, u32[]{:S(2)}) collective-permute-start(f32[64,1024]{1,0:T(8,128)} %get-tuple-element.31), channel_id=1, source_target_pairs={{1,0},{2,1},{3,2},{7,3},{6,7},{5,6},{4,5},{8,4},{9,8},{10,9},{11,1... | collective-permute-start | bytes 786440 | tf_op jit(solution)/shard_map/ppermute | solution.py:449
  131.8 76.3 %collective-permute-start.14 = (f32[8,64,512]{2,1,0:T(8,128)}, f32[8,64,512]{2,1,0:T(8,128)S(1)}, u32[]{:S(2)}, u32[]{:S(2)}) collective-permute-start(f32[8,64,512]{2,1,0:T(8,128)} %get-tuple-element.20.high_ref), channel_id=1, source_target_pairs={{1,2},{2,1},{5,6},{6,5},{9,10},{10,9},{13,14},{14,13},{17,18},{18,... | collective-permute-start | bytes 3145736 | tf_op jit(solution)/shard_map/ppermute | solution.py:452
  132.5 5.1 %collective-permute-start.5 = (f32[64,128]{1,0:T(8,128)}, f32[64,128]{1,0:T(8,128)S(1)}, u32[]{:S(2)}, u32[]{:S(2)}) collective-permute-start(f32[64,128]{1,0:T(8,128)} %get-tuple-element.18), channel_id=1, source_target_pairs={{0,1},{1,0},{2,3},{3,2},{4,5},{5,4},{6,7},{7,6},{8,9},{9,8},{10,11... | collective-permute-start | bytes 98312 | tf_op jit(solution)/shard_map/ppermute | solution.py:466
  138.4 22.7 %collective-permute-start.6 = (f32[64,128]{1,0:T(8,128)S(1)}, f32[64,128]{1,0:T(8,128)S(1)}, u32[]{:S(2)}, u32[]{:S(2)}) collective-permute-start(f32[64,128]{1,0:T(8,128)S(1)} %add.107), channel_id=1, source_target_pairs={{0,2},{1,3},{2,0},{3,1},{4,6},{5,7},{6,4},{7,5},{8,10},{9,11},{10,... | collective-permute-start | bytes 98312 | tf_op jit(solution)/shard_map/ppermute | solution.py:466
  161.1 1.2 collective-permute-start.7
  162.3 3.9 %collective-permute-start.8 = (f32[64,128]{1,0:T(8,128)S(1)}, f32[64,128]{1,0:T(8,128)S(1)}, u32[]{:S(2)}, u32[]{:S(2)}) collective-permute-start(f32[64,128]{1,0:T(8,128)S(1)} %add.109), channel_id=1, source_target_pairs={{0,8},{4,12},{8,0},{12,4},{16,24},{20,28},{24,16},{28,20},{1,9},{5... | collective-permute-start | bytes 98312 | tf_op jit(solution)/shard_map/ppermute | solution.py:466
  163.1 0.7 copy-start.11
  165.8 1.7 collective-permute-start.18
  166.2 6.8 %copy-start.13 = (f32[64,128]{1,0:T(8,128)}, f32[64,128]{1,0:T(8,128)S(1)}, u32[]{:S(2)}) copy-start(f32[64,128]{1,0:T(8,128)S(1)} %add.110.mine_ref) | copy-start | bytes 98308
  166.2 6.8 %collective-permute-start.9 = (f32[64,128]{1,0:T(8,128)S(1)}, f32[64,128]{1,0:T(8,128)S(1)}, u32[]{:S(2)}, u32[]{:S(2)}) collective-permute-start(f32[64,128]{1,0:T(8,128)S(1)} %add.110.mine_ref), channel_id=1, source_target_pairs={{0,16},{4,20},{8,24},{12,28},{16,0},{20,4},{24,8},{28,12},{1,17},{... | collective-permute-start | bytes 98312 | tf_op jit(solution)/shard_map/ppermute | solution.py:466
  168.3 3.9 %collective-permute-start.19 = (f32[64,64]{1,0:T(8,128)S(1)}, f32[64,64]{1,0:T(8,128)S(1)}, u32[]{:S(2)}, u32[]{:S(2)}) collective-permute-start(f32[64,64]{1,0:T(8,128)S(1)} %add.120), channel_id=1, source_target_pairs={{0,8},{4,12},{8,0},{12,4},{16,24},{20,28},{24,16},{28,20},{1,9},{5... | collective-permute-start | bytes 49160 | tf_op jit(solution)/shard_map/ppermute | solution.py:466
  172.2 14.0 %collective-permute-start.20 = (f32[64,64]{1,0:T(8,128)S(1)}, f32[64,64]{1,0:T(8,128)S(1)}, u32[]{:S(2)}, u32[]{:S(2)}) collective-permute-start(f32[64,64]{1,0:T(8,128)S(1)} %add.121), channel_id=1, source_target_pairs={{0,16},{4,20},{8,24},{12,28},{16,0},{20,4},{24,8},{28,12},{1,17},{... | collective-permute-start | bytes 49160 | tf_op jit(solution)/shard_map/ppermute | solution.py:466
  173.0 0.6 copy-start.16
  186.2 4.9 %copy-start.9 = (f32[16,8,1024]{2,1,0:T(8,128)S(1)}, f32[16,8,1024]{2,1,0:T(8,128)}, u32[]{:S(2)}) copy-start(f32[16,8,1024]{2,1,0:T(8,128)} %get-tuple-element.22) | copy-start | bytes 1572868
  186.2 20.8 %copy-start.17 = (f32[64,128]{1,0:T(8,128)S(1)}, f32[64,128]{1,0:T(8,128)}, u32[]{:S(2)}) copy-start(f32[64,128]{1,0:T(8,128)} %get-tuple-element.30) | copy-start | bytes 98308
  186.2 20.9 %copy-start.8 = (f32[64,64]{1,0:T(8,128)S(1)}, f32[64,64]{1,0:T(8,128)}, u32[]{:S(2)}) copy-start(f32[64,64]{1,0:T(8,128)} %get-tuple-element.21.inv_ref) | copy-start | bytes 49156
  186.2 29.0 %collective-permute-start.10 = (f32[16,8,1024]{2,1,0:T(8,128)}, f32[16,8,1024]{2,1,0:T(8,128)}, u32[]{:S(2)}, u32[]{:S(2)}) collective-permute-start(f32[16,8,1024]{2,1,0:T(8,128)} %get-tuple-element.23), channel_id=1, source_target_pairs={{0,1},{1,0},{2,3},{3,2},{4,5},{5,4},{6,7},{7,6},{8,9},{9,8},{10,11... | collective-permute-start | bytes 1572872 | tf_op jit(solution)/shard_map/ppermute | solution.py:511
  186.3 14.8 %collective-permute-start.21 = (f32[64,64]{1,0:T(8,128)S(1)}, f32[64,64]{1,0:T(8,128)S(1)}, u32[]{:S(2)}, u32[]{:S(2)}) collective-permute-start(f32[64,64]{1,0:T(8,128)S(1)} %add.122), channel_id=1, source_target_pairs={{0,1},{1,0},{2,3},{3,2},{4,5},{5,4},{6,7},{7,6},{8,9},{9,8},{10,11... | collective-permute-start | bytes 49160 | tf_op jit(solution)/shard_map/ppermute | solution.py:476
  188.3 12.7 %collective-permute-start.22 = (f32[64,64]{1,0:T(8,128)S(1)}, f32[64,64]{1,0:T(8,128)S(1)}, u32[]{:S(2)}, u32[]{:S(2)}) collective-permute-start(f32[64,64]{1,0:T(8,128)S(1)} %add.122), channel_id=1, source_target_pairs={{0,2},{1,3},{2,0},{3,1},{4,6},{5,7},{6,4},{7,5},{8,10},{9,11},{10,... | collective-permute-start | bytes 49160 | tf_op jit(solution)/shard_map/ppermute | solution.py:476
  188.5 14.5 %collective-permute-start.23 = (f32[64,64]{1,0:T(8,128)S(1)}, f32[64,64]{1,0:T(8,128)S(1)}, u32[]{:S(2)}, u32[]{:S(2)}) collective-permute-start(f32[64,64]{1,0:T(8,128)S(1)} %add.122), channel_id=1, source_target_pairs={{0,3},{1,2},{2,1},{3,0},{4,7},{5,6},{6,5},{7,4},{8,11},{9,10},{10,... | collective-permute-start | bytes 49160 | tf_op jit(solution)/shard_map/ppermute | solution.py:476
  201.0 28.4 %collective-permute-start.11 = (f32[16,8,512]{2,1,0:T(8,128)}, f32[16,8,512]{2,1,0:T(8,128)S(1)}, u32[]{:S(2)}, u32[]{:S(2)}) collective-permute-start(f32[16,8,512]{2,1,0:T(8,128)} %get-tuple-element.24), channel_id=1, source_target_pairs={{0,2},{1,3},{2,0},{3,1},{4,6},{5,7},{6,4},{7,5},{8,10},{9,11},{10,... | collective-permute-start | bytes 786440 | tf_op jit(solution)/shard_map/ppermute | solution.py:511
  201.0 28.5 %collective-permute-start.12 = (f32[16,8,512]{2,1,0:T(8,128)}, f32[16,8,512]{2,1,0:T(8,128)}, u32[]{:S(2)}, u32[]{:S(2)}) collective-permute-start(f32[16,8,512]{2,1,0:T(8,128)} %get-tuple-element.25), channel_id=1, source_target_pairs={{0,3},{1,2},{2,1},{3,0},{4,7},{5,6},{6,5},{7,4},{8,11},{9,10},{10,... | collective-permute-start | bytes 786440 | tf_op jit(solution)/shard_map/ppermute | solution.py:511
  203.0 27.5 %collective-permute-start.13 = (f32[16,8,512]{2,1,0:T(8,128)}, f32[16,8,512]{2,1,0:T(8,128)}, u32[]{:S(2)}, u32[]{:S(2)}) collective-permute-start(f32[16,8,512]{2,1,0:T(8,128)} %get-tuple-element.26), channel_id=1, source_target_pairs={{0,2},{3,1},{4,6},{7,5},{8,10},{11,9},{12,14},{15,13},{16,18},{19,... | collective-permute-start | bytes 786440 | tf_op jit(solution)/shard_map/ppermute | solution.py:511
  208.1 4.5 %copy-start.7 = (f32[8,64,512]{2,1,0:T(8,128)}, f32[8,64,512]{2,1,0:T(8,128)S(1)}, u32[]{:S(2)}) copy-start(f32[8,64,512]{2,1,0:T(8,128)S(1)} %collective-permute-done.14.lines_ref) | copy-start | bytes 3145732
  208.1 25.1 %collective-permute-start.16 = (f32[16,8,512]{2,1,0:T(8,128)}, f32[16,8,512]{2,1,0:T(8,128)}, u32[]{:S(2)}, u32[]{:S(2)}) collective-permute-start(f32[16,8,512]{2,1,0:T(8,128)} %get-tuple-element.28), channel_id=1, source_target_pairs={{0,3},{3,0},{4,7},{7,4},{8,11},{11,8},{12,15},{15,12},{16,19},{19,... | collective-permute-start | bytes 786440 | tf_op jit(solution)/shard_map/ppermute | solution.py:511
  215.2 18.0 %copy-start.12 = (f32[16,8,512]{2,1,0:T(8,128)S(1)}, f32[16,8,512]{2,1,0:T(8,128)}, u32[]{:S(2)}) copy-start(f32[16,8,512]{2,1,0:T(8,128)} %get-tuple-element.29) | copy-start | bytes 786436
  215.2 17.0 %collective-permute-start.15 = (f32[16,8,512]{2,1,0:T(8,128)}, f32[16,8,512]{2,1,0:T(8,128)S(1)}, u32[]{:S(2)}, u32[]{:S(2)}) collective-permute-start(f32[16,8,512]{2,1,0:T(8,128)} %get-tuple-element.27), channel_id=1, source_target_pairs={{1,0},{2,3},{5,4},{6,7},{9,8},{10,11},{13,12},{14,15},{17,16},{18,... | collective-permute-start | bytes 786440 | tf_op jit(solution)/shard_map/ppermute | solution.py:511
  234.2 1.3 copy-start.4

commit v5 on v4

--- a/solution.py
+++ b/solution.py
@@ -324,14 +324,16 @@
     for lines_ref, out_refs, at in sources:
         slab_rows, _, width = lines_ref.shape
         for j in range(slab_rows):
-            done_ref[j] = jnp.dot(
+            done_ref[j, :, :width] = jnp.dot(
                 weights, lines_ref[j], precision=lax.Precision.HIGHEST, preferred_element_type=jnp.float32
             )
         for d, out_ref in zip(targets, out_refs):
             start = ((place ^ d) - first) * vec_local
             for vec in range(0, vec_local, SUBLANES):
                 rows = pl.ds(pl.multiple_of(start + vec, SUBLANES), SUBLANES)
-                out_ref[vec : vec + SUBLANES, :, at : at + width] = jnp.swapaxes(done_ref[:, rows, :], 0, 1)
+                out_ref[vec : vec + SUBLANES, :, at : at + width] = jnp.swapaxes(
+                    done_ref[:, rows, :width], 0, 1
+                )
 
 
 def solve_kernel(place_ref, mine_ref, other_ref, low_ref, high_ref, inv_ref, sums_ref, *rest, **static):
@@ -431,8 +433,9 @@
         slabs.append(slab)
 
     place = lax.axis_index("vec").astype(jnp.int32)
-    width = columns // 2
-    lines_shape = jax.ShapeDtypeStruct((slab_rows, total_vecs, width), jnp.float32)
+    width = columns - columns // 4
+    low_shape = jax.ShapeDtypeStruct((slab_rows, total_vecs, width), jnp.float32)
+    high_shape = jax.ShapeDtypeStruct((slab_rows, total_vecs, columns - width), jnp.float32)
     sums_shape = jax.ShapeDtypeStruct((total_vecs, 2 * total_vecs), jnp.float32)
     sums, first_row, low, high = pl.pallas_call(
         functools.partial(gram_kernel, chunks=vecs),
@@ -441,8 +444,8 @@
         out_shape=[
             sums_shape,
             jax.ShapeDtypeStruct((total_vecs, columns), jnp.float32),
-            lines_shape,
-            lines_shape,
+            low_shape,
+            high_shape,
         ],
         name="gram",
     )(*slabs, turned(place, me, groups)[None], level)
@@ -450,11 +453,14 @@
     half = groups // 2
     middle = (half - 1, half)
     raw = lax.ppermute(high, "vec", [middle, middle[::-1]])
-    last_row = pl.BlockSpec((1, total_vecs, width), lambda i: (slab_rows - 1, 0, 0))
+    last_low, last_high = (
+        pl.BlockSpec((1, total_vecs, part.shape[2]), lambda i: (slab_rows - 1, 0, 0))
+        for part in (low_shape, high_shape)
+    )
     edge = pl.pallas_call(
         edge_kernel,
         grid=(1,),
-        in_specs=[vmem, last_row, last_row],
+        in_specs=[vmem, last_low, last_high],
         out_specs=vmem,
         out_shape=jax.ShapeDtypeStruct((total_vecs, total_vecs), jnp.float32),
         name="edge",
@@ -479,14 +485,16 @@
     static = dict(scale=math.sqrt(strips * rows * columns), half=half, vec_local=vec_local)
     far, near = tuple(range(half, groups)), tuple(range(half))
     piece = jax.ShapeDtypeStruct((vec_local, slab_rows, columns), jnp.float32)
-    part_piece = jax.ShapeDtypeStruct((vec_local, slab_rows, width), jnp.float32)
+    low_piece = jax.ShapeDtypeStruct((vec_local, slab_rows, width), jnp.float32)
+    high_piece = jax.ShapeDtypeStruct((vec_local, slab_rows, columns - width), jnp.float32)
     products_scratch = [pltpu.VMEM((slab_rows, half * vec_local, width), jnp.float32)]
     inverse, gram_cross, *blocks = pl.pallas_call(
         functools.partial(solve_kernel, targets=far, **static),
         in_specs=[smem] + [vmem] * 4,
         out_specs=[vmem] * (2 + 2 * half),
         out_shape=[jax.ShapeDtypeStruct((total_vecs, total_vecs), jnp.float32), sums_shape]
-        + [part_piece] * (2 * half),
+        + [low_piece] * half
+        + [high_piece] * half,
         scratch_shapes=products_scratch,
         name="solve",
     )(place[None], sums, pending, low, high)
@@ -502,7 +510,7 @@
         functools.partial(extra_kernel, targets=near, **static),
         in_specs=[smem] + [vmem] * 2,
         out_specs=[vmem] * half,
-        out_shape=[part_piece] * half,
+        out_shape=[high_piece] * half,
         scratch_shapes=products_scratch,
         name="extra",
     )(place[None], inverse, raw)

time: 238 us -> 227 us (0.954)
  the two profiles are of different devices: /device:TPU:0 before, /device:TPU:9 now
where the time goes in v5:
time: 227 us; the launch traced here: 226 us
  waiting for transfers between devices  101 us (44%)
  Pallas kernels  57.1 us (25%)
  starting transfers between devices  46.5 us (20%)
  local copies, waits for them, and re-layouts  12.1 us (5%)
  between operations  5.22 us (2%)
  other arithmetic  3.07 us (1%)
    all_to_all x2, waiting for transfers between devices, whole_shards(): lax.all_to_all(done.reshape(devices, slab_rows, columns), both, split_axi...  35.9 us
    pallas_call x2, Pallas kernels, whole_shards(): pl.pallas_call(functools.partial(filter_kernel, slabs=groups), in_specs=[...  29.2 us
    ppermute x6, waiting for transfers between devices, across(): return lax.ppermute(block, 'vec', [(i, i ^ d) for i in sources])  26.4 us
    ppermute x5, waiting for transfers between devices, swap(): return lax.ppermute(value, 'strip', [(i, i ^ bit) for i in range(strips)])  16.8 us
    ppermute x8, waiting for transfers between devices, pairwise(): other = lax.ppermute(value, axis, [(i, i ^ bit) for i in range(count)])  12.2 us
    ppermute x6, starting transfers between devices, across(): return lax.ppermute(block, 'vec', [(i, i ^ d) for i in sources])  11.5 us
    all_to_all x2, starting transfers between devices, whole_shards(): lax.all_to_all(done.reshape(devices, slab_rows, columns), both, split_axi...  10.7 us
    ppermute x3, waiting for transfers between devices, whole_shards(): lax.ppermute(edge, 'vec', [(i, i ^ d) for i in range(groups)])  9.33 us
  transfers between devices with their start and end apart: 28, of which 11 were waited for; matrix products, arithmetic and copies ran while one was open for 4% of the time, Pallas kernels for 22%

profile of v5, /device:TPU:9, one launch (start us, length us, event | category | flops | bytes accessed | tf_op | source)
XLA Modules:
  0.0 225.5 jit_solution(6500841267762206785)
XLA Ops:
  0.6 2.3 %slice.27 = f32[8,32,1024]{2,1,0:T(8,128)} slice(f32[16,32,1024]{2,1,0:T(8,128)} %param.3), slice={[0:8], [0:32], [0:1024]} | slice | bytes 2097152 | tf_op jit(solution)/shard_map/slice | solution.py:380
  3.0 4.5 %all-to-all-start = ((f32[8,32,1024]{2,1,0:T(8,128)}), f32[8,32,1024]{2,1,0:T(8,128)S(1)}, u32[]{:S(2)}, u32[]{:S(2)}) async-start(f32[8,32,1024]{2,1,0:T(8,128)} %slice.27), calls=%async_computation | async-start | bytes 2097152 | tf_op jit(solution)/shard_map/all_to_all | solution.py:381
  8.2 1.4 collective-permute-start.1
  9.5 1.2 collective-permute-start.2
  10.8 13.1 %collective-permute-done.1 = f32[32,1024]{1,0:T(8,128)S(1)} collective-permute-done((f32[32,1024]{1,0:T(8,128)}, f32[32,1024]{1,0:T(8,128)S(1)}, u32[]{:S(2)}, u32[]{:S(2)}) %collective-permute-start.1) | collective-permute-done | bytes 131104 | tf_op jit(solution)/shard_map/ppermute | solution.py:375
  23.9 3.7 %collective-permute-done.3 = f32[32,1024]{1,0:T(8,128)S(1)} collective-permute-done((f32[32,1024]{1,0:T(8,128)}, f32[32,1024]{1,0:T(8,128)S(1)}, u32[]{:S(2)}, u32[]{:S(2)}) %collective-permute-start.3) | collective-permute-done | bytes 131104 | tf_op jit(solution)/shard_map/ppermute | solution.py:375
  27.6 1.1 slice.28
  28.8 4.4 %all-to-all-start.2 = ((f32[8,32,1024]{2,1,0:T(8,128)}), f32[8,32,1024]{2,1,0:T(8,128)S(1)}, u32[]{:S(2)}, u32[]{:S(2)}) async-start(f32[8,32,1024]{2,1,0:T(8,128)} %slice.28), calls=%async_computation.2 | async-start | bytes 2097152 | tf_op jit(solution)/shard_map/all_to_all | solution.py:381
  40.2 4.2 %site.1 = f32[32,8,8,128]{3,2,1,0:T(8,128)} custom-call(f32[35]{0:T(128)} %pad_maximum_fusion.1.coef_ref, s32[1]{0:T(128)} %bitcast.6.me_ref, f32[32,1024]{1,0:T(8,128)} %convert_element_type.15.here_ref.refs_3_, f32[32,1024]{1,0:T(8,128)} %copy-done.16, f32[3,32,1024]{2,1,0:T(8,128)} %copy-done.7, f32[3,32,1024]{2,1,0:T(8,128)} %copy-done.11), custom_call_target="tpu_custom_call" | custom-call | tf_op jit(solution)/shard_map/site/pallas_call | solution.py:403
  44.4 14.6 %filter.2 = f32[4,8,8,1024]{3,2,1,0:T(8,128)} custom-call(f32[35]{0:T(128)} %pad_maximum_fusion.1.coef_ref, f32[8,32,1024]{2,1,0:T(8,128)} %copy-done.3, f32[32,8,8,128]{3,2,1,0:T(8,128)} %site.1), custom_call_target="tpu_custom_call" | custom-call | tf_op jit(solution)/shard_map/filter/pallas_call | solution.py:419
  59.0 6.2 %all-to-all-start.1 = ((f32[32,8,1024]{2,1,0:T(8,128)}), f32[32,8,1024]{2,1,0:T(8,128)S(1)}, u32[]{:S(2)}, u32[]{:S(2)}) async-start(f32[32,8,1024]{2,1,0:T(8,128)} %bitcast.22), calls=%async_computation.1 | async-start | bytes 2097152 | tf_op jit(solution)/shard_map/all_to_all | solution.py:432
  65.2 14.6 %filter.3 = f32[4,8,8,1024]{3,2,1,0:T(8,128)} custom-call(f32[35]{0:T(128)} %pad_maximum_fusion.1.coef_ref, f32[8,32,1024]{2,1,0:T(8,128)} %copy-done.4, f32[32,8,8,128]{3,2,1,0:T(8,128)} %site.1), custom_call_target="tpu_custom_call" | custom-call | tf_op jit(solution)/shard_map/filter/pallas_call | solution.py:419
  79.8 10.7 %all-to-all-done.1.refs_0_ = f32[32,8,1024]{2,1,0:T(8,128)S(1)} async-done(((f32[32,8,1024]{2,1,0:T(8,128)}), f32[32,8,1024]{2,1,0:T(8,128)S(1)}, u32[]{:S(2)}, u32[]{:S(2)}) %all-to-all-start.1) | async-done | bytes 1048608 | tf_op jit(solution)/shard_map/all_to_all | solution.py:432
  90.5 4.5 %all-to-all-start.3 = ((f32[32,8,1024]{2,1,0:T(8,128)}), f32[32,8,1024]{2,1,0:T(8,128)S(1)}, u32[]{:S(2)}, u32[]{:S(2)}) async-start(f32[32,8,1024]{2,1,0:T(8,128)} %bitcast.21), calls=%async_computation.3 | async-start | bytes 2097152 | tf_op jit(solution)/shard_map/all_to_all | solution.py:432
  95.1 25.3 %all-to-all-done.3.refs_1_ = f32[32,8,1024]{2,1,0:T(8,128)S(1)} async-done(((f32[32,8,1024]{2,1,0:T(8,128)}), f32[32,8,1024]{2,1,0:T(8,128)S(1)}, u32[]{:S(2)}, u32[]{:S(2)}) %all-to-all-start.3) | async-done | bytes 1048608 | tf_op jit(solution)/shard_map/all_to_all | solution.py:432
  120.3 1.0 copy-done.2
  121.3 7.0 %gram.1 = (f32[64,128]{1,0:T(8,128)}, f32[64,1024]{1,0:T(8,128)}, f32[8,64,768]{2,1,0:T(8,128)}, f32[8,64,256]{2,1,0:T(8,128)}) custom-call(f32[32,8,1024]{2,1,0:T(8,128)} %copy-done.1, f32[32,8,1024]{2,1,0:T(8,128)} %copy-done.2, s32[1]{0:T(128)} %bitcast.12.refs_2_, f32[32,1024]{1,0:T(8,128)} %convert_element_type.15.here_ref.refs_3_), custom_call_target="tpu_custom_call" | custom-call | tf_op jit(solution)/shard_map/gram/pallas_call | solution.py:440
  128.3 0.8 collective-permute-start.17
  129.7 5.0 %collective-permute-done.5 = f32[64,128]{1,0:T(8,128)S(1)} collective-permute-done((f32[64,128]{1,0:T(8,128)}, f32[64,128]{1,0:T(8,128)S(1)}, u32[]{:S(2)}, u32[]{:S(2)}) %collective-permute-start.5) | collective-permute-done | bytes 32800 | tf_op jit(solution)/shard_map/ppermute | solution.py:472
  134.7 0.8 add.107
  135.7 3.8 %collective-permute-done.6 = f32[64,128]{1,0:T(8,128)S(1)} collective-permute-done((f32[64,128]{1,0:T(8,128)S(1)}, f32[64,128]{1,0:T(8,128)S(1)}, u32[]{:S(2)}, u32[]{:S(2)}) %collective-permute-start.6) | collective-permute-done | bytes 32800 | tf_op jit(solution)/shard_map/ppermute | solution.py:472
  140.2 0.9 collective-permute-done.7
  141.1 1.0 collective-permute-start.8
  142.1 0.7 copy-done.12
  142.8 2.0 edge.1
  145.5 1.2 collective-permute-start.9
  146.7 0.8 add.120
  147.7 2.5 %collective-permute-done.19 = f32[64,64]{1,0:T(8,128)S(1)} collective-permute-done((f32[64,64]{1,0:T(8,128)S(1)}, f32[64,64]{1,0:T(8,128)S(1)}, u32[]{:S(2)}, u32[]{:S(2)}) %collective-permute-start.19) | collective-permute-done | bytes 16416 | tf_op jit(solution)/shard_map/ppermute | solution.py:472
  150.2 1.0 collective-permute-start.20
  151.2 2.8 %collective-permute-start.14 = (f32[8,64,256]{2,1,0:T(8,128)S(1)}, f32[8,64,256]{2,1,0:T(8,128)S(1)}, u32[]{:S(2)}, u32[]{:S(2)}) collective-permute-start(f32[8,64,256]{2,1,0:T(8,128)S(1)} %copy-done), channel_id=1, source_target_pairs={{1,2},{2,1},{5,6},{6,5},{9,10},{10,9},{13,14},{14,13},{17,18},{18,... | collective-permute-start | bytes 1572872 | tf_op jit(solution)/shard_map/ppermute | solution.py:455
  154.7 8.9 %solve.1 = (f32[64,64]{1,0:T(8,128)}, f32[64,128]{1,0:T(8,128)}, f32[16,8,768]{2,1,0:T(8,128)}, f32[16,8,768]{2,1,0:T(8,128)}, f32[16,8,256]{2,1,0:T(8,128)}, /*index=5*/f32[16,8,256]{2,1,0:T(8,128)}) custom-call(s32[1]{0:T(128)} %bitcast.place_ref, f32[64,128]{1,0:T(8,128)} %copy-done.13, f32[64,128]{1,0:T(8,128)} %copy-done.17, ...), custom_call_target="tpu_custom_call" | custom-call | tf_op jit(solution)/shard_map/solve/pallas_call | solution.py:491
  163.6 3.6 %near.1 = (f32[16,8,1024]{2,1,0:T(8,128)}, f32[16,8,1024]{2,1,0:T(8,128)}) custom-call(s32[1]{0:T(128)} %bitcast.place_ref, f32[64,64]{1,0:T(8,128)} %get-tuple-element.21.inv_ref, f32[8,64,768]{2,1,0:T(8,128)} %get-tuple-element.19.low_ref, f32[8,64,256]{2,1,0:T(8,128)} %get-tuple-element.20.high_ref), custom_call_target="tpu_custom_call" | custom-call | tf_op jit(solution)/shard_map/near/pallas_call | solution.py:501
  167.3 1.5 collective-permute-start.21
  169.1 0.9 collective-permute-start.23
  170.4 9.3 %collective-permute-done.21 = f32[64,64]{1,0:T(8,128)S(1)} collective-permute-done((f32[64,64]{1,0:T(8,128)S(1)}, f32[64,64]{1,0:T(8,128)S(1)}, u32[]{:S(2)}, u32[]{:S(2)}) %collective-permute-start.21) | collective-permute-done | bytes 16416 | tf_op jit(solution)/shard_map/ppermute | solution.py:482
  179.7 1.2 collective-permute-start.11
  180.9 0.9 collective-permute-start.12
  181.9 1.3 collective-permute-start.13
  183.5 0.8 convolution_multiply_fusion
  184.3 0.7 collective-permute-start.16
  185.1 2.1 extra.1
  187.2 7.3 %collective-permute-start.15 = (f32[16,8,256]{2,1,0:T(8,128)}, f32[16,8,256]{2,1,0:T(8,128)S(1)}, u32[]{:S(2)}, u32[]{:S(2)}) collective-permute-start(f32[16,8,256]{2,1,0:T(8,128)} %get-tuple-element.27), channel_id=1, source_target_pairs={{1,0},{2,3},{5,4},{6,7},{9,8},{10,11},{13,12},{14,15},{17,16},{18,... | collective-permute-start | bytes 393224 | tf_op jit(solution)/shard_map/ppermute | solution.py:519
  194.6 1.1 constant_dynamic-update-slice_fusion.2
  195.7 17.4 %collective-permute-done.11 = f32[16,8,768]{2,1,0:T(8,128)} collective-permute-done((f32[16,8,768]{2,1,0:T(8,128)}, f32[16,8,768]{2,1,0:T(8,128)}, u32[]{:S(2)}, u32[]{:S(2)}) %collective-permute-start.11) | collective-permute-done | bytes 393248 | tf_op jit(solution)/shard_map/ppermute | solution.py:519
  213.1 1.0 constant_dynamic-update-slice_fusion.1
  214.1 8.9 %collective-permute-done.12 = f32[16,8,768]{2,1,0:T(8,128)} collective-permute-done((f32[16,8,768]{2,1,0:T(8,128)}, f32[16,8,768]{2,1,0:T(8,128)}, u32[]{:S(2)}, u32[]{:S(2)}) %collective-permute-start.12) | collective-permute-done | bytes 393248 | tf_op jit(solution)/shard_map/ppermute | solution.py:519
  223.1 1.0 constant_dynamic-update-slice_fusion
  224.2 1.3 copy-done.5
  (85 shorter events, 7.8 us)
Async XLA Ops:
  0.6 6.9 %copy-start.14 = (s32[32,1024]{1,0:T(8,128)S(1)}, s32[32,1024]{1,0:T(8,128)}, u32[]{:S(2)}) copy-start(s32[32,1024]{1,0:T(8,128)} %param.4) | copy-start | bytes 393220
  3.0 24.6 %copy-start.6 = (f32[16,32,1024]{2,1,0:T(8,128)S(1)}, f32[16,32,1024]{2,1,0:T(8,128)}, u32[]{:S(2)}) copy-start(f32[16,32,1024]{2,1,0:T(8,128)} %param.3) | copy-start | bytes 6291460
  3.0 25.8 %all-to-all-start = ((f32[8,32,1024]{2,1,0:T(8,128)}), f32[8,32,1024]{2,1,0:T(8,128)S(1)}, u32[]{:S(2)}, u32[]{:S(2)}) async-start(f32[8,32,1024]{2,1,0:T(8,128)} %slice.27), calls=%async_computation | async-start | bytes 2097152 | tf_op jit(solution)/shard_map/all_to_all | solution.py:381
  8.2 15.7 %collective-permute-start.1 = (f32[32,1024]{1,0:T(8,128)}, f32[32,1024]{1,0:T(8,128)S(1)}, u32[]{:S(2)}, u32[]{:S(2)}) collective-permute-start(f32[32,1024]{1,0:T(8,128)} %convert_element_type.15.here_ref.refs_3_), channel_id=1, source_target_pairs={{0,8},{4,12},{8,0},{12,4},{16,24},{20,28},{24,16},{28,20},{1,9},{5... | collective-permute-start | bytes 393224 | tf_op jit(solution)/shard_map/ppermute | solution.py:375
  9.5 14.4 %collective-permute-start.2 = (f32[32,1024]{1,0:T(8,128)}, f32[32,1024]{1,0:T(8,128)S(1)}, u32[]{:S(2)}, u32[]{:S(2)}) collective-permute-start(f32[32,1024]{1,0:T(8,128)} %convert_element_type.15.here_ref.refs_3_), channel_id=1, source_target_pairs={{0,16},{4,20},{8,24},{12,28},{16,0},{20,4},{24,8},{28,12},{1,17},{... | collective-permute-start | bytes 393224 | tf_op jit(solution)/shard_map/ppermute | solution.py:375
  10.7 16.9 %collective-permute-start.3 = (f32[32,1024]{1,0:T(8,128)}, f32[32,1024]{1,0:T(8,128)S(1)}, u32[]{:S(2)}, u32[]{:S(2)}) collective-permute-start(f32[32,1024]{1,0:T(8,128)} %convert_element_type.15.here_ref.refs_3_), channel_id=1, source_target_pairs={{0,24},{4,28},{8,16},{12,20},{16,8},{20,12},{24,0},{28,4},{1,25},{... | collective-permute-start | bytes 393224 | tf_op jit(solution)/shard_map/ppermute | solution.py:375
  27.6 5.8 %copy-start.7 = (f32[3,32,1024]{2,1,0:T(8,128)}, f32[3,32,1024]{2,1,0:T(8,128)S(1)}, u32[]{:S(2)}) copy-start(f32[3,32,1024]{2,1,0:T(8,128)S(1)} %pad_maximum_fusion.own_ref) | copy-start | bytes 1179652
  27.6 5.7 %copy-start.20 = (s32[4]{0:T(128)S(1)}, s32[4]{0:T(128)}, u32[]{:S(2)}) copy-start(s32[4]{0:T(128)} %param.5) | copy-start | bytes 52
  28.8 15.7 %copy-start.3 = (f32[8,32,1024]{2,1,0:T(8,128)}, f32[8,32,1024]{2,1,0:T(8,128)S(1)}, u32[]{:S(2)}) copy-start(f32[8,32,1024]{2,1,0:T(8,128)S(1)} %all-to-all-done.vec_ref) | copy-start | bytes 3145732
  28.8 30.3 %all-to-all-start.2 = ((f32[8,32,1024]{2,1,0:T(8,128)}), f32[8,32,1024]{2,1,0:T(8,128)S(1)}, u32[]{:S(2)}, u32[]{:S(2)}) async-start(f32[8,32,1024]{2,1,0:T(8,128)} %slice.28), calls=%async_computation.2 | async-start | bytes 2097152 | tf_op jit(solution)/shard_map/all_to_all | solution.py:381
  33.2 6.2 %collective-permute-start = (f32[32,1024]{1,0:T(8,128)}, f32[32,1024]{1,0:T(8,128)S(1)}, u32[]{:S(2)}, u32[]{:S(2)}) collective-permute-start(f32[32,1024]{1,0:T(8,128)} %convert_element_type.15.here_ref.refs_3_), channel_id=1, source_target_pairs={{0,4},{4,0},{8,12},{12,8},{16,20},{20,16},{24,28},{28,24},{1,5},{5... | collective-permute-start | bytes 393224 | tf_op jit(solution)/shard_map/ppermute | solution.py:375
  33.4 6.0 %collective-permute-start.4 = (f32[3,32,1024]{2,1,0:T(8,128)S(1)}, f32[3,32,1024]{2,1,0:T(8,128)S(1)}, u32[]{:S(2)}, u32[]{:S(2)}) collective-permute-start(f32[3,32,1024]{2,1,0:T(8,128)S(1)} %pad_maximum_fusion.own_ref), channel_id=1, source_target_pairs={{0,4},{4,0},{8,12},{12,8},{16,20},{20,16},{24,28},{28,24},{1,5},{5... | collective-permute-start | bytes 1179656 | tf_op jit(solution)/shard_map/ppermute | solution.py:375
  39.4 0.6 copy-start.16
  39.4 0.8 copy-start.11
  59.0 6.2 %copy-start.4 = (f32[8,32,1024]{2,1,0:T(8,128)}, f32[8,32,1024]{2,1,0:T(8,128)S(1)}, u32[]{:S(2)}) copy-start(f32[8,32,1024]{2,1,0:T(8,128)S(1)} %all-to-all-done.2.vec_ref) | copy-start | bytes 3145732
  59.0 31.5 %all-to-all-start.1 = ((f32[32,8,1024]{2,1,0:T(8,128)}), f32[32,8,1024]{2,1,0:T(8,128)S(1)}, u32[]{:S(2)}, u32[]{:S(2)}) async-start(f32[32,8,1024]{2,1,0:T(8,128)} %bitcast.22), calls=%async_computation.1 | async-start | bytes 2097152 | tf_op jit(solution)/shard_map/all_to_all | solution.py:432
  90.5 29.8 %copy-start.1 = (f32[32,8,1024]{2,1,0:T(8,128)}, f32[32,8,1024]{2,1,0:T(8,128)S(1)}, u32[]{:S(2)}) copy-start(f32[32,8,1024]{2,1,0:T(8,128)S(1)} %all-to-all-done.1.refs_0_) | copy-start | bytes 3145732
  90.5 29.8 %all-to-all-start.3 = ((f32[32,8,1024]{2,1,0:T(8,128)}), f32[32,8,1024]{2,1,0:T(8,128)S(1)}, u32[]{:S(2)}, u32[]{:S(2)}) async-start(f32[32,8,1024]{2,1,0:T(8,128)} %bitcast.21), calls=%async_computation.3 | async-start | bytes 2097152 | tf_op jit(solution)/shard_map/all_to_all | solution.py:432
  120.3 1.0 copy-start.2
  128.3 22.9 %copy-start = (f32[8,64,256]{2,1,0:T(8,128)S(1)}, f32[8,64,256]{2,1,0:T(8,128)}, u32[]{:S(2)}) copy-start(f32[8,64,256]{2,1,0:T(8,128)} %get-tuple-element.20.high_ref) | copy-start | bytes 1572868
  128.3 13.8 %collective-permute-start.17 = (f32[64,1024]{1,0:T(8,128)}, f32[64,1024]{1,0:T(8,128)S(1)}, u32[]{:S(2)}, u32[]{:S(2)}) collective-permute-start(f32[64,1024]{1,0:T(8,128)} %get-tuple-element.31), channel_id=1, source_target_pairs={{1,0},{2,1},{3,2},{7,3},{6,7},{5,6},{4,5},{8,4},{9,8},{10,9},{11,1... | collective-permute-start | bytes 786440 | tf_op jit(solution)/shard_map/ppermute | solution.py:452
  129.1 5.6 %collective-permute-start.5 = (f32[64,128]{1,0:T(8,128)}, f32[64,128]{1,0:T(8,128)S(1)}, u32[]{:S(2)}, u32[]{:S(2)}) collective-permute-start(f32[64,128]{1,0:T(8,128)} %get-tuple-element.18), channel_id=1, source_target_pairs={{0,1},{1,0},{2,3},{3,2},{4,5},{5,4},{6,7},{7,6},{8,9},{9,8},{10,11... | collective-permute-start | bytes 98312 | tf_op jit(solution)/shard_map/ppermute | solution.py:472
  135.5 4.1 %collective-permute-start.6 = (f32[64,128]{1,0:T(8,128)S(1)}, f32[64,128]{1,0:T(8,128)S(1)}, u32[]{:S(2)}, u32[]{:S(2)}) collective-permute-start(f32[64,128]{1,0:T(8,128)S(1)} %add.107), channel_id=1, source_target_pairs={{0,2},{1,3},{2,0},{3,1},{4,6},{5,7},{6,4},{7,5},{8,10},{9,11},{10,... | collective-permute-start | bytes 98312 | tf_op jit(solution)/shard_map/ppermute | solution.py:472
  139.6 1.5 collective-permute-start.7
  141.1 4.4 %collective-permute-start.8 = (f32[64,128]{1,0:T(8,128)S(1)}, f32[64,128]{1,0:T(8,128)S(1)}, u32[]{:S(2)}, u32[]{:S(2)}) collective-permute-start(f32[64,128]{1,0:T(8,128)S(1)} %add.109), channel_id=1, source_target_pairs={{0,8},{4,12},{8,0},{12,4},{16,24},{20,28},{24,16},{28,20},{1,9},{5... | collective-permute-start | bytes 98312 | tf_op jit(solution)/shard_map/ppermute | solution.py:472
  142.1 0.7 copy-start.12
  144.8 1.9 collective-permute-start.18
  145.5 8.6 %copy-start.13 = (f32[64,128]{1,0:T(8,128)}, f32[64,128]{1,0:T(8,128)S(1)}, u32[]{:S(2)}) copy-start(f32[64,128]{1,0:T(8,128)S(1)} %add.110.mine_ref) | copy-start | bytes 98308
  145.5 8.6 %collective-permute-start.9 = (f32[64,128]{1,0:T(8,128)S(1)}, f32[64,128]{1,0:T(8,128)S(1)}, u32[]{:S(2)}, u32[]{:S(2)}) collective-permute-start(f32[64,128]{1,0:T(8,128)S(1)} %add.110.mine_ref), channel_id=1, source_target_pairs={{0,16},{4,20},{8,24},{12,28},{16,0},{20,4},{24,8},{28,12},{1,17},{... | collective-permute-start | bytes 98312 | tf_op jit(solution)/shard_map/ppermute | solution.py:472
  147.5 2.8 %collective-permute-start.19 = (f32[64,64]{1,0:T(8,128)S(1)}, f32[64,64]{1,0:T(8,128)S(1)}, u32[]{:S(2)}, u32[]{:S(2)}) collective-permute-start(f32[64,64]{1,0:T(8,128)S(1)} %add.120), channel_id=1, source_target_pairs={{0,8},{4,12},{8,0},{12,4},{16,24},{20,28},{24,16},{28,20},{1,9},{5... | collective-permute-start | bytes 49160 | tf_op jit(solution)/shard_map/ppermute | solution.py:472
  150.2 17.0 %collective-permute-start.20 = (f32[64,64]{1,0:T(8,128)S(1)}, f32[64,64]{1,0:T(8,128)S(1)}, u32[]{:S(2)}, u32[]{:S(2)}) collective-permute-start(f32[64,64]{1,0:T(8,128)S(1)} %add.121), channel_id=1, source_target_pairs={{0,16},{4,20},{8,24},{12,28},{16,0},{20,4},{24,8},{28,12},{1,17},{... | collective-permute-start | bytes 49160 | tf_op jit(solution)/shard_map/ppermute | solution.py:472
  151.2 33.1 %collective-permute-start.14 = (f32[8,64,256]{2,1,0:T(8,128)S(1)}, f32[8,64,256]{2,1,0:T(8,128)S(1)}, u32[]{:S(2)}, u32[]{:S(2)}) collective-permute-start(f32[8,64,256]{2,1,0:T(8,128)S(1)} %copy-done), channel_id=1, source_target_pairs={{1,2},{2,1},{5,6},{6,5},{9,10},{10,9},{13,14},{14,13},{17,18},{18,... | collective-permute-start | bytes 1572872 | tf_op jit(solution)/shard_map/ppermute | solution.py:455
  167.2 3.1 %copy-start.10 = (f32[16,8,1024]{2,1,0:T(8,128)S(1)}, f32[16,8,1024]{2,1,0:T(8,128)}, u32[]{:S(2)}) copy-start(f32[16,8,1024]{2,1,0:T(8,128)} %get-tuple-element.22) | copy-start | bytes 1572868
  167.2 16.0 %copy-start.18 = (f32[64,128]{1,0:T(8,128)S(1)}, f32[64,128]{1,0:T(8,128)}, u32[]{:S(2)}) copy-start(f32[64,128]{1,0:T(8,128)} %get-tuple-element.30) | copy-start | bytes 98308
  167.2 16.2 %copy-start.8 = (f32[64,64]{1,0:T(8,128)S(1)}, f32[64,64]{1,0:T(8,128)}, u32[]{:S(2)}) copy-start(f32[64,64]{1,0:T(8,128)} %get-tuple-element.21.inv_ref) | copy-start | bytes 49156
  167.2 17.1 %copy-start.19 = (f32[16,8,256]{2,1,0:T(8,128)S(1)}, f32[16,8,256]{2,1,0:T(8,128)}, u32[]{:S(2)}) copy-start(f32[16,8,256]{2,1,0:T(8,128)} %get-tuple-element.28) | copy-start | bytes 393220
  167.2 20.1 %collective-permute-start.10 = (f32[16,8,1024]{2,1,0:T(8,128)}, f32[16,8,1024]{2,1,0:T(8,128)}, u32[]{:S(2)}, u32[]{:S(2)}) collective-permute-start(f32[16,8,1024]{2,1,0:T(8,128)} %get-tuple-element.23), channel_id=1, source_target_pairs={{0,1},{1,0},{2,3},{3,2},{4,5},{5,4},{6,7},{7,6},{8,9},{9,8},{10,11... | collective-permute-start | bytes 1572872 | tf_op jit(solution)/shard_map/ppermute | solution.py:519
  167.3 12.4 %collective-permute-start.21 = (f32[64,64]{1,0:T(8,128)S(1)}, f32[64,64]{1,0:T(8,128)S(1)}, u32[]{:S(2)}, u32[]{:S(2)}) collective-permute-start(f32[64,64]{1,0:T(8,128)S(1)} %add.122), channel_id=1, source_target_pairs={{0,1},{1,0},{2,3},{3,2},{4,5},{5,4},{6,7},{7,6},{8,9},{9,8},{10,11... | collective-permute-start | bytes 49160 | tf_op jit(solution)/shard_map/ppermute | solution.py:482
  168.8 12.1 %collective-permute-start.22 = (f32[64,64]{1,0:T(8,128)S(1)}, f32[64,64]{1,0:T(8,128)S(1)}, u32[]{:S(2)}, u32[]{:S(2)}) collective-permute-start(f32[64,64]{1,0:T(8,128)S(1)} %add.122), channel_id=1, source_target_pairs={{0,2},{1,3},{2,0},{3,1},{4,6},{5,7},{6,4},{7,5},{8,10},{9,11},{10,... | collective-permute-start | bytes 49160 | tf_op jit(solution)/shard_map/ppermute | solution.py:482
  169.1 12.8 %collective-permute-start.23 = (f32[64,64]{1,0:T(8,128)S(1)}, f32[64,64]{1,0:T(8,128)S(1)}, u32[]{:S(2)}, u32[]{:S(2)}) collective-permute-start(f32[64,64]{1,0:T(8,128)S(1)} %add.122), channel_id=1, source_target_pairs={{0,3},{1,2},{2,1},{3,0},{4,7},{5,6},{6,5},{7,4},{8,11},{9,10},{10,... | collective-permute-start | bytes 49160 | tf_op jit(solution)/shard_map/ppermute | solution.py:482
  179.7 33.4 %collective-permute-start.11 = (f32[16,8,768]{2,1,0:T(8,128)}, f32[16,8,768]{2,1,0:T(8,128)}, u32[]{:S(2)}, u32[]{:S(2)}) collective-permute-start(f32[16,8,768]{2,1,0:T(8,128)} %get-tuple-element.24), channel_id=1, source_target_pairs={{0,2},{1,3},{2,0},{3,1},{4,6},{5,7},{6,4},{7,5},{8,10},{9,11},{10,... | collective-permute-start | bytes 1179656 | tf_op jit(solution)/shard_map/ppermute | solution.py:519
  180.9 42.2 %collective-permute-start.12 = (f32[16,8,768]{2,1,0:T(8,128)}, f32[16,8,768]{2,1,0:T(8,128)}, u32[]{:S(2)}, u32[]{:S(2)}) collective-permute-start(f32[16,8,768]{2,1,0:T(8,128)} %get-tuple-element.25), channel_id=1, source_target_pairs={{0,3},{1,2},{2,1},{3,0},{4,7},{5,6},{6,5},{7,4},{8,11},{9,10},{10,... | collective-permute-start | bytes 1179656 | tf_op jit(solution)/shard_map/ppermute | solution.py:519
  181.9 42.2 %collective-permute-start.13 = (f32[16,8,256]{2,1,0:T(8,128)}, f32[16,8,256]{2,1,0:T(8,128)S(1)}, u32[]{:S(2)}, u32[]{:S(2)}) collective-permute-start(f32[16,8,256]{2,1,0:T(8,128)} %get-tuple-element.26), channel_id=1, source_target_pairs={{0,2},{3,1},{4,6},{7,5},{8,10},{11,9},{12,14},{15,13},{16,18},{19,... | collective-permute-start | bytes 393224 | tf_op jit(solution)/shard_map/ppermute | solution.py:519
  184.3 0.8 copy-start.9
  184.3 39.8 %collective-permute-start.16 = (f32[16,8,256]{2,1,0:T(8,128)S(1)}, f32[16,8,256]{2,1,0:T(8,128)S(1)}, u32[]{:S(2)}, u32[]{:S(2)}) collective-permute-start(f32[16,8,256]{2,1,0:T(8,128)S(1)} %copy-done.19), channel_id=1, source_target_pairs={{0,3},{3,0},{4,7},{7,4},{8,11},{11,8},{12,15},{15,12},{16,19},{19,... | collective-permute-start | bytes 393224 | tf_op jit(solution)/shard_map/ppermute | solution.py:519
  187.2 36.9 %copy-start.15 = (f32[16,8,256]{2,1,0:T(8,128)S(1)}, f32[16,8,256]{2,1,0:T(8,128)}, u32[]{:S(2)}) copy-start(f32[16,8,256]{2,1,0:T(8,128)} %get-tuple-element.29) | copy-start | bytes 393220
  187.2 36.9 %collective-permute-start.15 = (f32[16,8,256]{2,1,0:T(8,128)}, f32[16,8,256]{2,1,0:T(8,128)S(1)}, u32[]{:S(2)}, u32[]{:S(2)}) collective-permute-start(f32[16,8,256]{2,1,0:T(8,128)} %get-tuple-element.27), channel_id=1, source_target_pairs={{1,0},{2,3},{5,4},{6,7},{9,8},{10,11},{13,12},{14,15},{17,16},{18,... | collective-permute-start | bytes 393224 | tf_op jit(solution)/shard_map/ppermute | solution.py:519
  224.2 1.3 copy-start.5
  (1 other events, 0.6 us)

commit v6 on v5

--- a/solution.py
+++ b/solution.py
@@ -298,17 +298,31 @@
     for block in range(blocks):
         unit = (lane == sublane + (total + block * SUBLANES)).astype(jnp.float32)
         work.append(jnp.where(lane < total, sums[block * SUBLANES : (block + 1) * SUBLANES], unit))
-    for k in range(total):
+    for k in range(0, total, 2):
         home, inside = k // SUBLANES, k % SUBLANES
-        columns = [
-            jnp.broadcast_to(work[block][:, k : k + 1], (SUBLANES, width)) for block in range(home, blocks)
-        ]
-        pivot = columns[0][inside : inside + 1, :]
-        row = work[home][inside : inside + 1, :] / pivot
-        row = jnp.broadcast_to(row, (SUBLANES, width))
-        columns[0] = jnp.where(sublane > inside, columns[0], 0.0)
+
+        def column(k):
+            return [
+                jnp.broadcast_to(work[block][:, k : k + 1], (SUBLANES, width)) for block in range(home, blocks)
+            ]
+
+        one, two = column(k), column(k + 1)
+        upper, lower = slice(inside, inside + 1), slice(inside + 1, inside + 2)
+        inverse = 1.0 / one[0][upper]
+        shared = two[0][upper] * inverse
+        ratio = one[0][lower] * inverse
+        row_one = work[home][upper]
+        row_two = work[home][lower] - ratio * row_one
+        row_two = row_two * (1.0 / (two[0][lower] - ratio * two[0][upper]))
+        row_one = jnp.broadcast_to(row_one * inverse, (SUBLANES, width))
+        row_two = jnp.broadcast_to(row_two, (SUBLANES, width))
         for block in range(home, blocks):
-            work[block] = work[block] - columns[block - home] * row
+            first = one[block - home]
+            second = two[block - home] - first * shared
+            if block == home:
+                first = jnp.where(sublane > inside, first, 0.0)
+                second = jnp.where(sublane > inside + 1, second, 0.0)
+            work[block] = work[block] - (first * row_one + second * row_two)
     result = []
     for block in range(blocks):
         pivots = jnp.sum(
@@ -321,11 +335,13 @@
 def products(inv_ref, sources, done_ref, place, scale, targets, half, vec_local):
     first = ((place ^ targets[0]) // half) * half
     weights = scale * inv_ref[pl.ds(pl.multiple_of(first * vec_local, SUBLANES), half * vec_local), :]
-    for lines_ref, out_refs, at in sources:
-        slab_rows, _, width = lines_ref.shape
-        for j in range(slab_rows):
+    for lines_ref, begin, width, out_refs, at in sources:
+        for j in range(lines_ref.shape[0]):
             done_ref[j, :, :width] = jnp.dot(
-                weights, lines_ref[j], precision=lax.Precision.HIGHEST, preferred_element_type=jnp.float32
+                weights,
+                lines_ref[j, :, begin : begin + width],
+                precision=lax.Precision.HIGHEST,
+                preferred_element_type=jnp.float32,
             )
         for d, out_ref in zip(targets, out_refs):
             start = ((place ^ d) - first) * vec_local
@@ -336,22 +352,31 @@
                 )
 
 
-def solve_kernel(place_ref, mine_ref, other_ref, low_ref, high_ref, inv_ref, sums_ref, *rest, **static):
+def solve_kernel(place_ref, mine_ref, other_ref, low_ref, inv_ref, sums_ref, *rest, **static):
     sums = mine_ref[...] + other_ref[...]
     sums_ref[...] = sums
     inv_ref[...] = eliminate(sums)
-    half = static["half"]
-    sources = [(low_ref, rest[:half], 0), (high_ref, rest[half : 2 * half], 0)]
+    head = rest[0].shape[2]
+    products(inv_ref, [(low_ref, 0, head, rest[:-1], 0)], rest[-1], place_ref[0], **static)
+
+
+def rest_kernel(place_ref, inv_ref, low_ref, high_ref, *rest, **static):
+    half, tail = static["half"], rest[0].shape[2]
+    sources = [
+        (low_ref, low_ref.shape[2] - tail, tail, rest[:half], 0),
+        (high_ref, 0, high_ref.shape[2], rest[half : 2 * half], 0),
+    ]
     products(inv_ref, sources, rest[-1], place_ref[0], **static)
 
 
 def near_kernel(place_ref, inv_ref, low_ref, high_ref, *rest, **static):
-    sources = [(low_ref, rest[:-1], 0), (high_ref, rest[:-1], low_ref.shape[2])]
+    low, high = low_ref.shape[2], high_ref.shape[2]
+    sources = [(low_ref, 0, low, rest[:-1], 0), (high_ref, 0, high, rest[:-1], low)]
     products(inv_ref, sources, rest[-1], place_ref[0], **static)
 
 
 def extra_kernel(place_ref, inv_ref, lines_ref, *rest, **static):
-    products(inv_ref, [(lines_ref, rest[:-1], 0)], rest[-1], place_ref[0], **static)
+    products(inv_ref, [(lines_ref, 0, lines_ref.shape[2], rest[:-1], 0)], rest[-1], place_ref[0], **static)
 
 
 def whole_shards(start_vectors, potential, bounds):
@@ -485,19 +510,28 @@
     static = dict(scale=math.sqrt(strips * rows * columns), half=half, vec_local=vec_local)
     far, near = tuple(range(half, groups)), tuple(range(half))
     piece = jax.ShapeDtypeStruct((vec_local, slab_rows, columns), jnp.float32)
-    low_piece = jax.ShapeDtypeStruct((vec_local, slab_rows, width), jnp.float32)
+    head = columns // 4
+    head_piece = jax.ShapeDtypeStruct((vec_local, slab_rows, head), jnp.float32)
+    tail_piece = jax.ShapeDtypeStruct((vec_local, slab_rows, width - head), jnp.float32)
     high_piece = jax.ShapeDtypeStruct((vec_local, slab_rows, columns - width), jnp.float32)
     products_scratch = [pltpu.VMEM((slab_rows, half * vec_local, width), jnp.float32)]
-    inverse, gram_cross, *blocks = pl.pallas_call(
+    inverse, gram_cross, *heads = pl.pallas_call(
         functools.partial(solve_kernel, targets=far, **static),
-        in_specs=[smem] + [vmem] * 4,
-        out_specs=[vmem] * (2 + 2 * half),
+        in_specs=[smem] + [vmem] * 3,
+        out_specs=[vmem] * (2 + half),
         out_shape=[jax.ShapeDtypeStruct((total_vecs, total_vecs), jnp.float32), sums_shape]
-        + [low_piece] * half
-        + [high_piece] * half,
+        + [head_piece] * half,
         scratch_shapes=products_scratch,
         name="solve",
-    )(place[None], sums, pending, low, high)
+    )(place[None], sums, pending, low)
+    blocks = pl.pallas_call(
+        functools.partial(rest_kernel, targets=far, **static),
+        in_specs=[smem] + [vmem] * 3,
+        out_specs=[vmem] * (2 * half),
+        out_shape=[tail_piece] * half + [high_piece] * half,
+        scratch_shapes=products_scratch,
+        name="rest",
+    )(place[None], inverse, low, high)
     own_block, beside_block = pl.pallas_call(
         functools.partial(near_kernel, targets=near, **static),
         in_specs=[smem] + [vmem] * 3,
@@ -520,7 +554,8 @@
 
     outer_groups = [i for i in range(groups) if i not in middle]
     far_high = [across(block, d, outer_groups) for d, block in zip(far, blocks[half:])]
-    far_low = [across(block, d) for d, block in zip(far, blocks[:half])]
+    far_head = [across(block, d) for d, block in zip(far, heads)]
+    far_tail = [across(block, d) for d, block in zip(far, blocks[:half])]
     beside_block = across(beside_block, 1)
     beside_extra = across(beside_extra, 1, middle)
     far_high = [far_high[0] + beside_extra, far_high[1] + own_extra]
@@ -529,8 +564,10 @@
     for d, block, at in (
         (0, own_block, 0),
         (1, beside_block, 0),
-        (2, far_low[0], 0),
-        (3, far_low[1], 0),
+        (2, far_head[0], 0),
+        (3, far_head[1], 0),
+        (2, far_tail[0], head),
+        (3, far_tail[1], head),
         (2, far_high[0], width),
         (3, far_high[1], width),
     ):

time: 227 us -> 219 us (0.965)
  the two profiles are of different devices: /device:TPU:9 before, /device:TPU:0 now
where the time goes in v6:
time: 219 us; the launch traced here: 217 us
  waiting for transfers between devices  84.3 us (38%)
  Pallas kernels  57.2 us (26%)
  starting transfers between devices  54 us (25%)
  local copies, waits for them, and re-layouts  11.6 us (5%)
  between operations  5.11 us (2%)
  other arithmetic  3.98 us (2%)
    all_to_all x2, waiting for transfers between devices, whole_shards(): lax.all_to_all(done.reshape(devices, slab_rows, columns), both, split_axi...  37.6 us
    pallas_call x2, Pallas kernels, whole_shards(): pl.pallas_call(functools.partial(filter_kernel, slabs=groups), in_specs=[...  29.2 us
    ppermute x8, waiting for transfers between devices, across(): return lax.ppermute(block, 'vec', [(i, i ^ d) for i in sources])  17.9 us
    ppermute x8, starting transfers between devices, across(): return lax.ppermute(block, 'vec', [(i, i ^ d) for i in sources])  17.5 us
    ppermute x5, waiting for transfers between devices, swap(): return lax.ppermute(value, 'strip', [(i, i ^ bit) for i in range(strips)])  16 us
    ppermute x8, waiting for transfers between devices, pairwise(): other = lax.ppermute(value, axis, [(i, i ^ bit) for i in range(count)])  12.9 us
    all_to_all x2, starting transfers between devices, whole_shards(): lax.all_to_all(done.reshape(devices, slab_rows, columns), both, split_axi...  9.99 us
    all_to_all x2, starting transfers between devices, spread(): lax.all_to_all(part, 'strip', split_axis=0, concat_axis=0, tiled=True)  8.89 us
  transfers between devices with their start and end apart: 30, of which 11 were waited for; matrix products, arithmetic and copies ran while one was open for 4% of the time, Pallas kernels for 23%

profile of v6, /device:TPU:0, one launch (start us, length us, event | category | flops | bytes accessed | tf_op | source)
XLA Modules:
  0.0 217.2 jit_solution(8399521974948034031)
XLA Ops:
  0.6 2.3 %slice.27 = f32[8,32,1024]{2,1,0:T(8,128)} slice(f32[16,32,1024]{2,1,0:T(8,128)} %param.3), slice={[0:8], [0:32], [0:1024]} | slice | bytes 2097152 | tf_op jit(solution)/shard_map/slice | solution.py:405
  3.0 5.3 %all-to-all-start = ((f32[8,32,1024]{2,1,0:T(8,128)}), f32[8,32,1024]{2,1,0:T(8,128)S(1)}, u32[]{:S(2)}, u32[]{:S(2)}) async-start(f32[8,32,1024]{2,1,0:T(8,128)} %slice.27), calls=%async_computation | async-start | bytes 2097152 | tf_op jit(solution)/shard_map/all_to_all | solution.py:406
  9.0 2.9 %collective-permute-start.3 = (f32[32,1024]{1,0:T(8,128)}, f32[32,1024]{1,0:T(8,128)S(1)}, u32[]{:S(2)}, u32[]{:S(2)}) collective-permute-start(f32[32,1024]{1,0:T(8,128)} %convert_element_type.15.here_ref.refs_3_), channel_id=1, source_target_pairs={{0,24},{4,28},{8,16},{12,20},{16,8},{20,12},{24,0},{28,4},{1,25},{... | collective-permute-start | bytes 393224 | tf_op jit(solution)/shard_map/ppermute | solution.py:400
  12.5 14.6 %collective-permute-done.3 = f32[32,1024]{1,0:T(8,128)S(1)} collective-permute-done((f32[32,1024]{1,0:T(8,128)}, f32[32,1024]{1,0:T(8,128)S(1)}, u32[]{:S(2)}, u32[]{:S(2)}) %collective-permute-start.3) | collective-permute-done | bytes 131104 | tf_op jit(solution)/shard_map/ppermute | solution.py:400
  27.1 1.2 collective-permute-done.2
  28.5 1.1 slice.28
  29.6 3.6 %all-to-all-start.2 = ((f32[8,32,1024]{2,1,0:T(8,128)}), f32[8,32,1024]{2,1,0:T(8,128)S(1)}, u32[]{:S(2)}, u32[]{:S(2)}) async-start(f32[8,32,1024]{2,1,0:T(8,128)} %slice.28), calls=%async_computation.2 | async-start | bytes 2097152 | tf_op jit(solution)/shard_map/all_to_all | solution.py:406
  40.2 4.2 %site.1 = f32[32,8,8,128]{3,2,1,0:T(8,128)} custom-call(f32[35]{0:T(128)} %pad_maximum_fusion.1.coef_ref, s32[1]{0:T(128)} %bitcast.6.me_ref, f32[32,1024]{1,0:T(8,128)} %convert_element_type.15.here_ref.refs_3_, f32[32,1024]{1,0:T(8,128)} %copy-done.16, f32[3,32,1024]{2,1,0:T(8,128)} %copy-done.7, f32[3,32,1024]{2,1,0:T(8,128)} %copy-done.11), custom_call_target="tpu_custom_call" | custom-call | tf_op jit(solution)/shard_map/site/pallas_call | solution.py:428
  44.4 14.6 %filter.2 = f32[4,8,8,1024]{3,2,1,0:T(8,128)} custom-call(f32[35]{0:T(128)} %pad_maximum_fusion.1.coef_ref, f32[8,32,1024]{2,1,0:T(8,128)} %copy-done.3, f32[32,8,8,128]{3,2,1,0:T(8,128)} %site.1), custom_call_target="tpu_custom_call" | custom-call | tf_op jit(solution)/shard_map/filter/pallas_call | solution.py:444
  59.1 6.2 %all-to-all-start.1 = ((f32[32,8,1024]{2,1,0:T(8,128)}), f32[32,8,1024]{2,1,0:T(8,128)S(1)}, u32[]{:S(2)}, u32[]{:S(2)}) async-start(f32[32,8,1024]{2,1,0:T(8,128)} %bitcast.22), calls=%async_computation.1 | async-start | bytes 2097152 | tf_op jit(solution)/shard_map/all_to_all | solution.py:457
  65.3 14.6 %filter.3 = f32[4,8,8,1024]{3,2,1,0:T(8,128)} custom-call(f32[35]{0:T(128)} %pad_maximum_fusion.1.coef_ref, f32[8,32,1024]{2,1,0:T(8,128)} %copy-done.4, f32[32,8,8,128]{3,2,1,0:T(8,128)} %site.1), custom_call_target="tpu_custom_call" | custom-call | tf_op jit(solution)/shard_map/filter/pallas_call | solution.py:444
  79.9 11.6 %all-to-all-done.1.refs_0_ = f32[32,8,1024]{2,1,0:T(8,128)S(1)} async-done(((f32[32,8,1024]{2,1,0:T(8,128)}), f32[32,8,1024]{2,1,0:T(8,128)S(1)}, u32[]{:S(2)}, u32[]{:S(2)}) %all-to-all-start.1) | async-done | bytes 1048608 | tf_op jit(solution)/shard_map/all_to_all | solution.py:457
  91.5 3.8 %all-to-all-start.3 = ((f32[32,8,1024]{2,1,0:T(8,128)}), f32[32,8,1024]{2,1,0:T(8,128)S(1)}, u32[]{:S(2)}, u32[]{:S(2)}) async-start(f32[32,8,1024]{2,1,0:T(8,128)} %bitcast.21), calls=%async_computation.3 | async-start | bytes 2097152 | tf_op jit(solution)/shard_map/all_to_all | solution.py:457
  95.3 26.0 %all-to-all-done.3.refs_1_ = f32[32,8,1024]{2,1,0:T(8,128)S(1)} async-done(((f32[32,8,1024]{2,1,0:T(8,128)}), f32[32,8,1024]{2,1,0:T(8,128)S(1)}, u32[]{:S(2)}, u32[]{:S(2)}) %all-to-all-start.3) | async-done | bytes 1048608 | tf_op jit(solution)/shard_map/all_to_all | solution.py:457
  121.3 1.0 copy-done.2
  122.3 7.0 %gram.1 = (f32[64,128]{1,0:T(8,128)}, f32[64,1024]{1,0:T(8,128)}, f32[8,64,768]{2,1,0:T(8,128)}, f32[8,64,256]{2,1,0:T(8,128)}) custom-call(f32[32,8,1024]{2,1,0:T(8,128)} %copy-done.1, f32[32,8,1024]{2,1,0:T(8,128)} %copy-done.2, s32[1]{0:T(128)} %bitcast.12.refs_2_, f32[32,1024]{1,0:T(8,128)} %convert_element_type.15.here_ref.refs_3_), custom_call_target="tpu_custom_call" | custom-call | tf_op jit(solution)/shard_map/gram/pallas_call | solution.py:465
  129.3 1.4 collective-permute-start.19
  131.3 5.0 %collective-permute-done.5 = f32[64,128]{1,0:T(8,128)S(1)} collective-permute-done((f32[64,128]{1,0:T(8,128)}, f32[64,128]{1,0:T(8,128)S(1)}, u32[]{:S(2)}, u32[]{:S(2)}) %collective-permute-start.5) | collective-permute-done | bytes 32800 | tf_op jit(solution)/shard_map/ppermute | solution.py:497
  136.3 0.8 add.113
  137.0 0.9 collective-permute-start.6
  137.9 3.9 %collective-permute-done.6 = f32[64,128]{1,0:T(8,128)S(1)} collective-permute-done((f32[64,128]{1,0:T(8,128)S(1)}, f32[64,128]{1,0:T(8,128)S(1)}, u32[]{:S(2)}, u32[]{:S(2)}) %collective-permute-start.6) | collective-permute-done | bytes 32800 | tf_op jit(solution)/shard_map/ppermute | solution.py:497
  141.9 1.2 collective-permute-done.7
  143.1 1.5 collective-permute-start.8
  145.2 2.0 edge.1
  147.3 1.5 collective-permute-start.9
  149.6 1.2 collective-permute-start.21
  150.7 2.8 %collective-permute-done.21 = f32[64,64]{1,0:T(8,128)S(1)} collective-permute-done((f32[64,64]{1,0:T(8,128)S(1)}, f32[64,64]{1,0:T(8,128)S(1)}, u32[]{:S(2)}, u32[]{:S(2)}) %collective-permute-start.21) | collective-permute-done | bytes 16416 | tf_op jit(solution)/shard_map/ppermute | solution.py:497
  153.5 1.3 collective-permute-start.22
  156.1 5.9 %solve.1 = (f32[64,64]{1,0:T(8,128)}, f32[64,128]{1,0:T(8,128)}, f32[16,8,256]{2,1,0:T(8,128)}, f32[16,8,256]{2,1,0:T(8,128)}) custom-call(s32[1]{0:T(128)} %bitcast.place_ref, f32[64,128]{1,0:T(8,128)} %copy-done.13, f32[64,128]{1,0:T(8,128)} %copy-done.17, f32[8,64,768]{2,1,0:T(8,128)} %get-tuple-element.21.low_ref), custom_call_target="tpu_custom_call" | custom-call | tf_op jit(solution)/shard_map/solve/pallas_call | solution.py:518
  162.0 2.3 %collective-permute-start.11 = (f32[16,8,256]{2,1,0:T(8,128)}, f32[16,8,256]{2,1,0:T(8,128)S(1)}, u32[]{:S(2)}, u32[]{:S(2)}) collective-permute-start(f32[16,8,256]{2,1,0:T(8,128)} %get-tuple-element.26), channel_id=1, source_target_pairs={{0,2},{1,3},{2,0},{3,1},{4,6},{5,7},{6,4},{7,5},{8,10},{9,11},{10,... | collective-permute-start | bytes 393224 | tf_op jit(solution)/shard_map/ppermute | solution.py:553
  164.3 3.6 %near.1 = (f32[16,8,1024]{2,1,0:T(8,128)}, f32[16,8,1024]{2,1,0:T(8,128)}) custom-call(s32[1]{0:T(128)} %bitcast.place_ref, f32[64,64]{1,0:T(8,128)} %get-tuple-element.22.inv_ref, f32[8,64,768]{2,1,0:T(8,128)} %get-tuple-element.21.low_ref, f32[8,64,256]{2,1,0:T(8,128)} %get-tuple-element.23.high_ref), custom_call_target="tpu_custom_call" | custom-call | tf_op jit(solution)/shard_map/near/pallas_call | solution.py:535
  167.9 2.2 %collective-permute-start.25 = (f32[64,64]{1,0:T(8,128)S(1)}, f32[64,64]{1,0:T(8,128)S(1)}, u32[]{:S(2)}, u32[]{:S(2)}) collective-permute-start(f32[64,64]{1,0:T(8,128)S(1)} %add.128), channel_id=1, source_target_pairs={{0,3},{1,2},{2,1},{3,0},{4,7},{5,6},{6,5},{7,4},{8,11},{9,10},{10,... | collective-permute-start | bytes 49160 | tf_op jit(solution)/shard_map/ppermute | solution.py:507
  170.1 2.3 %collective-permute-start.23 = (f32[64,64]{1,0:T(8,128)S(1)}, f32[64,64]{1,0:T(8,128)}, u32[]{:S(2)}, u32[]{:S(2)}) collective-permute-start(f32[64,64]{1,0:T(8,128)S(1)} %add.128), channel_id=1, source_target_pairs={{0,1},{1,0},{2,3},{3,2},{4,5},{5,4},{6,7},{7,6},{8,9},{9,8},{10,11... | collective-permute-start | bytes 49160 | tf_op jit(solution)/shard_map/ppermute | solution.py:507
  172.7 3.1 %rest.1 = (f32[16,8,512]{2,1,0:T(8,128)}, f32[16,8,512]{2,1,0:T(8,128)}, f32[16,8,256]{2,1,0:T(8,128)}, f32[16,8,256]{2,1,0:T(8,128)}) custom-call(s32[1]{0:T(128)} %bitcast.place_ref, f32[64,64]{1,0:T(8,128)} %get-tuple-element.22.inv_ref, f32[8,64,768]{2,1,0:T(8,128)} %get-tuple-element.21.low_ref, f32[8,64,256]{2,1,0:T(8,128)} %get-tuple-element.23.high_ref), custom_call_target="tpu_custom_call" | custom-call | tf_op jit(solution)/shard_map/rest/pallas_call | solution.py:527
  175.8 2.2 %collective-permute-start.12 = (f32[16,8,256]{2,1,0:T(8,128)}, f32[16,8,256]{2,1,0:T(8,128)}, u32[]{:S(2)}, u32[]{:S(2)}) collective-permute-start(f32[16,8,256]{2,1,0:T(8,128)} %get-tuple-element.27), channel_id=1, source_target_pairs={{0,3},{1,2},{2,1},{3,0},{4,7},{5,6},{6,5},{7,4},{8,11},{9,10},{10,... | collective-permute-start | bytes 393224 | tf_op jit(solution)/shard_map/ppermute | solution.py:553
  178.6 2.7 %collective-permute-start.15 = (f32[16,8,256]{2,1,0:T(8,128)}, f32[16,8,256]{2,1,0:T(8,128)S(1)}, u32[]{:S(2)}, u32[]{:S(2)}) collective-permute-start(f32[16,8,256]{2,1,0:T(8,128)} %get-tuple-element.30), channel_id=1, source_target_pairs={{0,2},{3,1},{4,6},{7,5},{8,10},{11,9},{12,14},{15,13},{16,18},{19,... | collective-permute-start | bytes 393224 | tf_op jit(solution)/shard_map/ppermute | solution.py:553
  181.4 0.9 add_add_fusion
  182.6 0.8 convolution_multiply_fusion
  183.4 4.0 %collective-permute-start.18 = (f32[16,8,256]{2,1,0:T(8,128)}, f32[16,8,256]{2,1,0:T(8,128)S(1)}, u32[]{:S(2)}, u32[]{:S(2)}) collective-permute-start(f32[16,8,256]{2,1,0:T(8,128)} %get-tuple-element.32), channel_id=1, source_target_pairs={{0,3},{3,0},{4,7},{7,4},{8,11},{11,8},{12,15},{15,12},{16,19},{19,... | collective-permute-start | bytes 393224 | tf_op jit(solution)/shard_map/ppermute | solution.py:553
  187.4 2.1 extra.1
  189.6 6.3 %collective-permute-done.10 = f32[16,8,1024]{2,1,0:T(8,128)} collective-permute-done((f32[16,8,1024]{2,1,0:T(8,128)}, f32[16,8,1024]{2,1,0:T(8,128)}, u32[]{:S(2)}, u32[]{:S(2)}) %collective-permute-start.10) | collective-permute-done | bytes 524320 | tf_op jit(solution)/shard_map/ppermute | solution.py:553
  195.8 3.6 %collective-permute-start.13 = (f32[16,8,512]{2,1,0:T(8,128)}, f32[16,8,512]{2,1,0:T(8,128)S(1)}, u32[]{:S(2)}, u32[]{:S(2)}) collective-permute-start(f32[16,8,512]{2,1,0:T(8,128)} %get-tuple-element.28), channel_id=1, source_target_pairs={{0,2},{1,3},{2,0},{3,1},{4,6},{5,7},{6,4},{7,5},{8,10},{9,11},{10,... | collective-permute-start | bytes 786440 | tf_op jit(solution)/shard_map/ppermute | solution.py:553
  199.5 1.1 constant_dynamic-update-slice_fusion.4
  200.5 1.3 collective-permute-start.14
  201.9 1.3 collective-permute-start.17
  203.2 0.9 constant_dynamic-update-slice_fusion.2
  204.1 11.6 %collective-permute-done.13 = f32[16,8,512]{2,1,0:T(8,128)S(1)} collective-permute-done((f32[16,8,512]{2,1,0:T(8,128)}, f32[16,8,512]{2,1,0:T(8,128)S(1)}, u32[]{:S(2)}, u32[]{:S(2)}) %collective-permute-start.13) | collective-permute-done | bytes 262176 | tf_op jit(solution)/shard_map/ppermute | solution.py:553
  215.9 1.3 copy-done.5
  (94 shorter events, 9.1 us)
Async XLA Ops:
  0.6 7.7 %copy-start.14 = (s32[32,1024]{1,0:T(8,128)S(1)}, s32[32,1024]{1,0:T(8,128)}, u32[]{:S(2)}) copy-start(s32[32,1024]{1,0:T(8,128)} %param.4) | copy-start | bytes 393220
  3.0 25.5 %copy-start.6 = (f32[16,32,1024]{2,1,0:T(8,128)S(1)}, f32[16,32,1024]{2,1,0:T(8,128)}, u32[]{:S(2)}) copy-start(f32[16,32,1024]{2,1,0:T(8,128)} %param.3) | copy-start | bytes 6291460
  3.0 26.7 %all-to-all-start = ((f32[8,32,1024]{2,1,0:T(8,128)}), f32[8,32,1024]{2,1,0:T(8,128)S(1)}, u32[]{:S(2)}, u32[]{:S(2)}) async-start(f32[8,32,1024]{2,1,0:T(8,128)} %slice.27), calls=%async_computation | async-start | bytes 2097152 | tf_op jit(solution)/shard_map/all_to_all | solution.py:406
  9.0 18.1 %collective-permute-start.3 = (f32[32,1024]{1,0:T(8,128)}, f32[32,1024]{1,0:T(8,128)S(1)}, u32[]{:S(2)}, u32[]{:S(2)}) collective-permute-start(f32[32,1024]{1,0:T(8,128)} %convert_element_type.15.here_ref.refs_3_), channel_id=1, source_target_pairs={{0,24},{4,28},{8,16},{12,20},{16,8},{20,12},{24,0},{28,4},{1,25},{... | collective-permute-start | bytes 393224 | tf_op jit(solution)/shard_map/ppermute | solution.py:400
  11.9 16.4 %collective-permute-start.2 = (f32[32,1024]{1,0:T(8,128)}, f32[32,1024]{1,0:T(8,128)S(1)}, u32[]{:S(2)}, u32[]{:S(2)}) collective-permute-start(f32[32,1024]{1,0:T(8,128)} %convert_element_type.15.here_ref.refs_3_), channel_id=1, source_target_pairs={{0,16},{4,20},{8,24},{12,28},{16,0},{20,4},{24,8},{28,12},{1,17},{... | collective-permute-start | bytes 393224 | tf_op jit(solution)/shard_map/ppermute | solution.py:400
  12.5 16.0 %collective-permute-start.1 = (f32[32,1024]{1,0:T(8,128)}, f32[32,1024]{1,0:T(8,128)S(1)}, u32[]{:S(2)}, u32[]{:S(2)}) collective-permute-start(f32[32,1024]{1,0:T(8,128)} %convert_element_type.15.here_ref.refs_3_), channel_id=1, source_target_pairs={{0,8},{4,12},{8,0},{12,4},{16,24},{20,28},{24,16},{28,20},{1,9},{5... | collective-permute-start | bytes 393224 | tf_op jit(solution)/shard_map/ppermute | solution.py:400
  28.5 5.1 %copy-start.7 = (f32[3,32,1024]{2,1,0:T(8,128)}, f32[3,32,1024]{2,1,0:T(8,128)S(1)}, u32[]{:S(2)}) copy-start(f32[3,32,1024]{2,1,0:T(8,128)S(1)} %pad_maximum_fusion.own_ref) | copy-start | bytes 1179652
  28.5 5.1 %copy-start.21 = (s32[4]{0:T(128)S(1)}, s32[4]{0:T(128)}, u32[]{:S(2)}) copy-start(s32[4]{0:T(128)} %param.5) | copy-start | bytes 52
  29.6 14.8 %copy-start.3 = (f32[8,32,1024]{2,1,0:T(8,128)}, f32[8,32,1024]{2,1,0:T(8,128)S(1)}, u32[]{:S(2)}) copy-start(f32[8,32,1024]{2,1,0:T(8,128)S(1)} %all-to-all-done.vec_ref) | copy-start | bytes 3145732
  29.6 29.4 %all-to-all-start.2 = ((f32[8,32,1024]{2,1,0:T(8,128)}), f32[8,32,1024]{2,1,0:T(8,128)S(1)}, u32[]{:S(2)}, u32[]{:S(2)}) async-start(f32[8,32,1024]{2,1,0:T(8,128)} %slice.28), calls=%async_computation.2 | async-start | bytes 2097152 | tf_op jit(solution)/shard_map/all_to_all | solution.py:406
  33.2 6.2 %collective-permute-start = (f32[32,1024]{1,0:T(8,128)}, f32[32,1024]{1,0:T(8,128)S(1)}, u32[]{:S(2)}, u32[]{:S(2)}) collective-permute-start(f32[32,1024]{1,0:T(8,128)} %convert_element_type.15.here_ref.refs_3_), channel_id=1, source_target_pairs={{0,4},{4,0},{8,12},{12,8},{16,20},{20,16},{24,28},{28,24},{1,5},{5... | collective-permute-start | bytes 393224 | tf_op jit(solution)/shard_map/ppermute | solution.py:400
  33.6 5.8 %collective-permute-start.4 = (f32[3,32,1024]{2,1,0:T(8,128)S(1)}, f32[3,32,1024]{2,1,0:T(8,128)S(1)}, u32[]{:S(2)}, u32[]{:S(2)}) collective-permute-start(f32[3,32,1024]{2,1,0:T(8,128)S(1)} %pad_maximum_fusion.own_ref), channel_id=1, source_target_pairs={{0,4},{4,0},{8,12},{12,8},{16,20},{20,16},{24,28},{28,24},{1,5},{5... | collective-permute-start | bytes 1179656 | tf_op jit(solution)/shard_map/ppermute | solution.py:400
  39.4 0.8 copy-start.11
  59.1 6.2 %copy-start.4 = (f32[8,32,1024]{2,1,0:T(8,128)}, f32[8,32,1024]{2,1,0:T(8,128)S(1)}, u32[]{:S(2)}) copy-start(f32[8,32,1024]{2,1,0:T(8,128)S(1)} %all-to-all-done.2.vec_ref) | copy-start | bytes 3145732
  59.1 32.4 %all-to-all-start.1 = ((f32[32,8,1024]{2,1,0:T(8,128)}), f32[32,8,1024]{2,1,0:T(8,128)S(1)}, u32[]{:S(2)}, u32[]{:S(2)}) async-start(f32[32,8,1024]{2,1,0:T(8,128)} %bitcast.22), calls=%async_computation.1 | async-start | bytes 2097152 | tf_op jit(solution)/shard_map/all_to_all | solution.py:457
  91.5 29.8 %copy-start.1 = (f32[32,8,1024]{2,1,0:T(8,128)}, f32[32,8,1024]{2,1,0:T(8,128)S(1)}, u32[]{:S(2)}) copy-start(f32[32,8,1024]{2,1,0:T(8,128)S(1)} %all-to-all-done.1.refs_0_) | copy-start | bytes 3145732
  91.5 29.8 %all-to-all-start.3 = ((f32[32,8,1024]{2,1,0:T(8,128)}), f32[32,8,1024]{2,1,0:T(8,128)S(1)}, u32[]{:S(2)}, u32[]{:S(2)}) async-start(f32[32,8,1024]{2,1,0:T(8,128)} %bitcast.21), calls=%async_computation.3 | async-start | bytes 2097152 | tf_op jit(solution)/shard_map/all_to_all | solution.py:457
  121.3 1.0 copy-start.2
  129.2 25.6 %copy-start = (f32[8,64,256]{2,1,0:T(8,128)S(1)}, f32[8,64,256]{2,1,0:T(8,128)}, u32[]{:S(2)}) copy-start(f32[8,64,256]{2,1,0:T(8,128)} %get-tuple-element.23.high_ref) | copy-start | bytes 1572868
  129.3 15.3 %collective-permute-start.19 = (f32[64,1024]{1,0:T(8,128)}, f32[64,1024]{1,0:T(8,128)S(1)}, u32[]{:S(2)}, u32[]{:S(2)}) collective-permute-start(f32[64,1024]{1,0:T(8,128)} %get-tuple-element.35), channel_id=1, source_target_pairs={{1,0},{2,1},{3,2},{7,3},{6,7},{5,6},{4,5},{8,4},{9,8},{10,9},{11,1... | collective-permute-start | bytes 786440 | tf_op jit(solution)/shard_map/ppermute | solution.py:477
  130.7 5.6 %collective-permute-start.5 = (f32[64,128]{1,0:T(8,128)}, f32[64,128]{1,0:T(8,128)S(1)}, u32[]{:S(2)}, u32[]{:S(2)}) collective-permute-start(f32[64,128]{1,0:T(8,128)} %get-tuple-element.20), channel_id=1, source_target_pairs={{0,1},{1,0},{2,3},{3,2},{4,5},{5,4},{6,7},{7,6},{8,9},{9,8},{10,11... | collective-permute-start | bytes 98312 | tf_op jit(solution)/shard_map/ppermute | solution.py:497
  137.0 4.8 %collective-permute-start.6 = (f32[64,128]{1,0:T(8,128)S(1)}, f32[64,128]{1,0:T(8,128)S(1)}, u32[]{:S(2)}, u32[]{:S(2)}) collective-permute-start(f32[64,128]{1,0:T(8,128)S(1)} %add.113), channel_id=1, source_target_pairs={{0,2},{1,3},{2,0},{3,1},{4,6},{5,7},{6,4},{7,5},{8,10},{9,11},{10,... | collective-permute-start | bytes 98312 | tf_op jit(solution)/shard_map/ppermute | solution.py:497
  141.8 1.2 collective-permute-start.7
  143.1 4.2 %collective-permute-start.8 = (f32[64,128]{1,0:T(8,128)S(1)}, f32[64,128]{1,0:T(8,128)S(1)}, u32[]{:S(2)}, u32[]{:S(2)}) collective-permute-start(f32[64,128]{1,0:T(8,128)S(1)} %add.115), channel_id=1, source_target_pairs={{0,8},{4,12},{8,0},{12,4},{16,24},{20,28},{24,16},{28,20},{1,9},{5... | collective-permute-start | bytes 98312 | tf_op jit(solution)/shard_map/ppermute | solution.py:497
  147.3 1.5 collective-permute-start.20
  147.3 8.2 %copy-start.13 = (f32[64,128]{1,0:T(8,128)}, f32[64,128]{1,0:T(8,128)S(1)}, u32[]{:S(2)}) copy-start(f32[64,128]{1,0:T(8,128)S(1)} %add.116.mine_ref) | copy-start | bytes 98308
  147.3 8.2 %collective-permute-start.9 = (f32[64,128]{1,0:T(8,128)S(1)}, f32[64,128]{1,0:T(8,128)S(1)}, u32[]{:S(2)}, u32[]{:S(2)}) collective-permute-start(f32[64,128]{1,0:T(8,128)S(1)} %add.116.mine_ref), channel_id=1, source_target_pairs={{0,16},{4,20},{8,24},{12,28},{16,0},{20,4},{24,8},{28,12},{1,17},{... | collective-permute-start | bytes 98312 | tf_op jit(solution)/shard_map/ppermute | solution.py:497
  149.6 3.9 %collective-permute-start.21 = (f32[64,64]{1,0:T(8,128)S(1)}, f32[64,64]{1,0:T(8,128)S(1)}, u32[]{:S(2)}, u32[]{:S(2)}) collective-permute-start(f32[64,64]{1,0:T(8,128)S(1)} %add.126), channel_id=1, source_target_pairs={{0,8},{4,12},{8,0},{12,4},{16,24},{20,28},{24,16},{28,20},{1,9},{5... | collective-permute-start | bytes 49160 | tf_op jit(solution)/shard_map/ppermute | solution.py:497
  153.5 14.4 %collective-permute-start.22 = (f32[64,64]{1,0:T(8,128)S(1)}, f32[64,64]{1,0:T(8,128)S(1)}, u32[]{:S(2)}, u32[]{:S(2)}) collective-permute-start(f32[64,64]{1,0:T(8,128)S(1)} %add.127), channel_id=1, source_target_pairs={{0,16},{4,20},{8,24},{12,28},{16,0},{20,4},{24,8},{28,12},{1,17},{... | collective-permute-start | bytes 49160 | tf_op jit(solution)/shard_map/ppermute | solution.py:497
  154.8 28.6 %collective-permute-start.16 = (f32[8,64,256]{2,1,0:T(8,128)S(1)}, f32[8,64,256]{2,1,0:T(8,128)S(1)}, u32[]{:S(2)}, u32[]{:S(2)}) collective-permute-start(f32[8,64,256]{2,1,0:T(8,128)S(1)} %copy-done), channel_id=1, source_target_pairs={{1,2},{2,1},{5,6},{6,5},{9,10},{10,9},{13,14},{14,13},{17,18},{18,... | collective-permute-start | bytes 1572872 | tf_op jit(solution)/shard_map/ppermute | solution.py:480
  162.0 38.6 %collective-permute-start.11 = (f32[16,8,256]{2,1,0:T(8,128)}, f32[16,8,256]{2,1,0:T(8,128)S(1)}, u32[]{:S(2)}, u32[]{:S(2)}) collective-permute-start(f32[16,8,256]{2,1,0:T(8,128)} %get-tuple-element.26), channel_id=1, source_target_pairs={{0,2},{1,3},{2,0},{3,1},{4,6},{5,7},{6,4},{7,5},{8,10},{9,11},{10,... | collective-permute-start | bytes 393224 | tf_op jit(solution)/shard_map/ppermute | solution.py:553
  167.9 4.7 %copy-start.10 = (f32[16,8,1024]{2,1,0:T(8,128)S(1)}, f32[16,8,1024]{2,1,0:T(8,128)}, u32[]{:S(2)}) copy-start(f32[16,8,1024]{2,1,0:T(8,128)} %get-tuple-element.24) | copy-start | bytes 1572868
  167.9 7.9 %collective-permute-start.25 = (f32[64,64]{1,0:T(8,128)S(1)}, f32[64,64]{1,0:T(8,128)S(1)}, u32[]{:S(2)}, u32[]{:S(2)}) collective-permute-start(f32[64,64]{1,0:T(8,128)S(1)} %add.128), channel_id=1, source_target_pairs={{0,3},{1,2},{2,1},{3,0},{4,7},{5,6},{6,5},{7,4},{8,11},{9,10},{10,... | collective-permute-start | bytes 49160 | tf_op jit(solution)/shard_map/ppermute | solution.py:507
  170.1 7.9 %collective-permute-start.24 = (f32[64,64]{1,0:T(8,128)S(1)}, f32[64,64]{1,0:T(8,128)S(1)}, u32[]{:S(2)}, u32[]{:S(2)}) collective-permute-start(f32[64,64]{1,0:T(8,128)S(1)} %add.128), channel_id=1, source_target_pairs={{0,2},{1,3},{2,0},{3,1},{4,6},{5,7},{6,4},{7,5},{8,10},{9,11},{10,... | collective-permute-start | bytes 49160 | tf_op jit(solution)/shard_map/ppermute | solution.py:507
  170.1 11.2 %collective-permute-start.23 = (f32[64,64]{1,0:T(8,128)S(1)}, f32[64,64]{1,0:T(8,128)}, u32[]{:S(2)}, u32[]{:S(2)}) collective-permute-start(f32[64,64]{1,0:T(8,128)S(1)} %add.128), channel_id=1, source_target_pairs={{0,1},{1,0},{2,3},{3,2},{4,5},{5,4},{6,7},{7,6},{8,9},{9,8},{10,11... | collective-permute-start | bytes 49160 | tf_op jit(solution)/shard_map/ppermute | solution.py:507
  172.6 8.8 %copy-start.18 = (f32[64,128]{1,0:T(8,128)S(1)}, f32[64,128]{1,0:T(8,128)}, u32[]{:S(2)}) copy-start(f32[64,128]{1,0:T(8,128)} %get-tuple-element.34) | copy-start | bytes 98308
  172.6 9.7 %copy-start.8 = (f32[64,64]{1,0:T(8,128)S(1)}, f32[64,64]{1,0:T(8,128)}, u32[]{:S(2)}) copy-start(f32[64,64]{1,0:T(8,128)} %get-tuple-element.22.inv_ref) | copy-start | bytes 49156
  175.8 5.6 %copy-start.19 = (f32[64,64]{1,0:T(8,128)}, f32[64,64]{1,0:T(8,128)S(1)}, u32[]{:S(2)}) copy-start(f32[64,64]{1,0:T(8,128)S(1)} %collective-permute-done.25) | copy-start | bytes 49156
  175.8 26.0 %collective-permute-start.12 = (f32[16,8,256]{2,1,0:T(8,128)}, f32[16,8,256]{2,1,0:T(8,128)}, u32[]{:S(2)}, u32[]{:S(2)}) collective-permute-start(f32[16,8,256]{2,1,0:T(8,128)} %get-tuple-element.27), channel_id=1, source_target_pairs={{0,3},{1,2},{2,1},{3,0},{4,7},{5,6},{6,5},{7,4},{8,11},{9,10},{10,... | collective-permute-start | bytes 393224 | tf_op jit(solution)/shard_map/ppermute | solution.py:553
  178.6 37.1 %collective-permute-start.15 = (f32[16,8,256]{2,1,0:T(8,128)}, f32[16,8,256]{2,1,0:T(8,128)S(1)}, u32[]{:S(2)}, u32[]{:S(2)}) collective-permute-start(f32[16,8,256]{2,1,0:T(8,128)} %get-tuple-element.30), channel_id=1, source_target_pairs={{0,2},{3,1},{4,6},{7,5},{8,10},{11,9},{12,14},{15,13},{16,18},{19,... | collective-permute-start | bytes 393224 | tf_op jit(solution)/shard_map/ppermute | solution.py:553
  181.3 14.5 %collective-permute-start.10 = (f32[16,8,1024]{2,1,0:T(8,128)}, f32[16,8,1024]{2,1,0:T(8,128)}, u32[]{:S(2)}, u32[]{:S(2)}) collective-permute-start(f32[16,8,1024]{2,1,0:T(8,128)} %get-tuple-element.25), channel_id=1, source_target_pairs={{0,1},{1,0},{2,3},{3,2},{4,5},{5,4},{6,7},{7,6},{8,9},{9,8},{10,11... | collective-permute-start | bytes 1572872 | tf_op jit(solution)/shard_map/ppermute | solution.py:553
  183.4 4.0 %copy-start.9 = (f32[8,64,256]{2,1,0:T(8,128)}, f32[8,64,256]{2,1,0:T(8,128)S(1)}, u32[]{:S(2)}) copy-start(f32[8,64,256]{2,1,0:T(8,128)S(1)} %collective-permute-done.16.lines_ref) | copy-start | bytes 1572868
  183.4 32.4 %collective-permute-start.18 = (f32[16,8,256]{2,1,0:T(8,128)}, f32[16,8,256]{2,1,0:T(8,128)S(1)}, u32[]{:S(2)}, u32[]{:S(2)}) collective-permute-start(f32[16,8,256]{2,1,0:T(8,128)} %get-tuple-element.32), channel_id=1, source_target_pairs={{0,3},{3,0},{4,7},{7,4},{8,11},{11,8},{12,15},{15,12},{16,19},{19,... | collective-permute-start | bytes 393224 | tf_op jit(solution)/shard_map/ppermute | solution.py:553
  189.6 26.3 %copy-start.15 = (f32[16,8,256]{2,1,0:T(8,128)S(1)}, f32[16,8,256]{2,1,0:T(8,128)}, u32[]{:S(2)}) copy-start(f32[16,8,256]{2,1,0:T(8,128)} %get-tuple-element.33) | copy-start | bytes 393220
  195.8 19.8 %collective-permute-start.13 = (f32[16,8,512]{2,1,0:T(8,128)}, f32[16,8,512]{2,1,0:T(8,128)S(1)}, u32[]{:S(2)}, u32[]{:S(2)}) collective-permute-start(f32[16,8,512]{2,1,0:T(8,128)} %get-tuple-element.28), channel_id=1, source_target_pairs={{0,2},{1,3},{2,0},{3,1},{4,6},{5,7},{6,4},{7,5},{8,10},{9,11},{10,... | collective-permute-start | bytes 786440 | tf_op jit(solution)/shard_map/ppermute | solution.py:553
  200.5 15.2 %collective-permute-start.14 = (f32[16,8,512]{2,1,0:T(8,128)}, f32[16,8,512]{2,1,0:T(8,128)S(1)}, u32[]{:S(2)}, u32[]{:S(2)}) collective-permute-start(f32[16,8,512]{2,1,0:T(8,128)} %get-tuple-element.29), channel_id=1, source_target_pairs={{0,3},{1,2},{2,1},{3,0},{4,7},{5,6},{6,5},{7,4},{8,11},{9,10},{10,... | collective-permute-start | bytes 786440 | tf_op jit(solution)/shard_map/ppermute | solution.py:553
  201.9 13.9 %collective-permute-start.17 = (f32[16,8,256]{2,1,0:T(8,128)}, f32[16,8,256]{2,1,0:T(8,128)S(1)}, u32[]{:S(2)}, u32[]{:S(2)}) collective-permute-start(f32[16,8,256]{2,1,0:T(8,128)} %get-tuple-element.31), channel_id=1, source_target_pairs={{1,0},{2,3},{5,4},{6,7},{9,8},{10,11},{13,12},{14,15},{17,16},{18,... | collective-permute-start | bytes 393224 | tf_op jit(solution)/shard_map/ppermute | solution.py:553
  215.9 1.3 copy-start.5
  (4 other events, 2.6 us)

commit v7 on v6

--- a/solution.py
+++ b/solution.py
@@ -377,6 +377,10 @@
 
 def extra_kernel(place_ref, inv_ref, lines_ref, *rest, **static):
     products(inv_ref, [(lines_ref, 0, lines_ref.shape[2], rest[:-1], 0)], rest[-1], place_ref[0], **static)
+
+
+def held(value):
+    return pltpu.with_memory_space_constraint(value, pltpu.VMEM)
 
 
 def whole_shards(start_vectors, potential, bounds):
@@ -453,7 +457,7 @@
                 pltpu.VMEM(padded, jnp.float32),
             ],
             name="filter",
-        )(terms, inner[chunk], site)
+        )(terms, held(inner[chunk]), site)
         slab = lax.all_to_all(done.reshape(devices, slab_rows, columns), both, split_axis=0, concat_axis=0, tiled=True)
         slabs.append(slab)
 
@@ -473,7 +477,7 @@
             high_shape,
         ],
         name="gram",
-    )(*slabs, turned(place, me, groups)[None], level)
+    )(*map(held, slabs), turned(place, me, groups)[None], level)
     next_row = lax.ppermute(first_row, ("strip", "vec"), ring)
     half = groups // 2
     middle = (half - 1, half)
@@ -489,7 +493,7 @@
         out_specs=vmem,
         out_shape=jax.ShapeDtypeStruct((total_vecs, total_vecs), jnp.float32),
         name="edge",
-    )(next_row, low, high)
+    )(held(next_row), low, high)
 
     def pairwise(value, order):
         rounds = [(axis, count, 1 << n) for axis, count in order for n in range(count.bit_length() - 1)]
@@ -523,7 +527,7 @@
         + [head_piece] * half,
         scratch_shapes=products_scratch,
         name="solve",
-    )(place[None], sums, pending, low)
+    )(place[None], sums, held(pending), low)
     blocks = pl.pallas_call(
         functools.partial(rest_kernel, targets=far, **static),
         in_specs=[smem] + [vmem] * 3,
@@ -547,7 +551,7 @@
         out_shape=[high_piece] * half,
         scratch_shapes=products_scratch,
         name="extra",
-    )(place[None], inverse, raw)
+    )(place[None], inverse, held(raw))
 
     def across(block, d, sources=range(groups)):
         return lax.ppermute(block, "vec", [(i, i ^ d) for i in sources])
@@ -563,13 +567,13 @@
     ortho_basis = jnp.zeros((vec_local, rows, columns), jnp.float32)
     for d, block, at in (
         (0, own_block, 0),
-        (1, beside_block, 0),
         (2, far_head[0], 0),
         (3, far_head[1], 0),
         (2, far_tail[0], head),
         (3, far_tail[1], head),
+        (3, far_high[1], width),
+        (1, beside_block, 0),
         (2, far_high[0], width),
-        (3, far_high[1], width),
     ):
         start = turned(place ^ d, me, groups) * slab_rows
         ortho_basis = lax.dynamic_update_slice(ortho_basis, block, (0, start, at))

time: 219 us -> 223 us (1.018)
  waiting for transfers between devices: 84.3 us -> 93.7 us
  local copies, waits for them, and re-layouts: 11.6 us -> 8.67 us
    ppermute x8, waiting for transfers between devices: 12.9 us -> 18.5 us  [pairwise(): other = lax.ppermute(value, axis, [(i, i ^ bit) for i in range(count)])]
    ppermute x8, starting transfers between devices: 17.5 us -> 13.8 us  [across(): return lax.ppermute(block, 'vec', [(i, i ^ d) for i in sources])]
    ppermute x3, starting transfers between devices: 4.45 us -> 7.93 us  [whole_shards(): lax.ppermute(edge, 'vec', [(i, i ^ d) for i in range(groups)])]
    unnamed x44 -> x28, local copies, waits for them, and re-layouts: 5.07 us -> 2.15 us
    ppermute x8, waiting for transfers between devices: 17.9 us -> 20.6 us  [across(): return lax.ppermute(block, 'vec', [(i, i ^ d) for i in sources])]
  transfers between devices with their start and end apart: 30 -> 30, of which waited for: 11 -> 15; matrix products, arithmetic and copies ran while one was open for 4% -> 4% of each run, Pallas kernels for 23% -> 22%
where the time goes in v7:
time: 223 us; the launch traced here: 222 us
  waiting for transfers between devices  93.7 us (42%)
  Pallas kernels  55.4 us (25%)
  starting transfers between devices  53.5 us (24%)
  local copies, waits for them, and re-layouts  8.67 us (4%)
  between operations  5.11 us (2%)
  other arithmetic  4.29 us (2%)
    all_to_all x2, waiting for transfers between devices, whole_shards(): lax.all_to_all(done.reshape(devices, slab_rows, columns), both, split_axi...  37.9 us
    pallas_call x2, Pallas kernels, whole_shards(): pl.pallas_call(functools.partial(filter_kernel, slabs=groups), in_specs=[...  28.6 us
    ppermute x8, waiting for transfers between devices, across(): return lax.ppermute(block, 'vec', [(i, i ^ d) for i in sources])  20.6 us
    ppermute x8, waiting for transfers between devices, pairwise(): other = lax.ppermute(value, axis, [(i, i ^ bit) for i in range(count)])  18.5 us
    ppermute x5, waiting for transfers between devices, swap(): return lax.ppermute(value, 'strip', [(i, i ^ bit) for i in range(strips)])  16 us
    ppermute x8, starting transfers between devices, across(): return lax.ppermute(block, 'vec', [(i, i ^ d) for i in sources])  13.8 us
    all_to_all x2, starting transfers between devices, whole_shards(): lax.all_to_all(done.reshape(devices, slab_rows, columns), both, split_axi...  9.99 us
    all_to_all x2, starting transfers between devices, spread(): lax.all_to_all(part, 'strip', split_axis=0, concat_axis=0, tiled=True)  8.89 us
  transfers between devices with their start and end apart: 30, of which 15 were waited for; matrix products, arithmetic and copies ran while one was open for 4% of the time, Pallas kernels for 22%

profile of v7, /device:TPU:0, one launch (start us, length us, event | category | flops | bytes accessed | tf_op | source)
XLA Modules:
  0.0 221.7 jit_solution(18228730004962830775)
XLA Ops:
  0.6 2.3 %slice.27 = f32[8,32,1024]{2,1,0:T(8,128)} slice(f32[16,32,1024]{2,1,0:T(8,128)} %param.3), slice={[0:8], [0:32], [0:1024]} | slice | bytes 2097152 | tf_op jit(solution)/shard_map/slice | solution.py:409
  3.0 5.3 %all-to-all-start = ((f32[8,32,1024]{2,1,0:T(8,128)}), f32[8,32,1024]{2,1,0:T(8,128)S(1)}, u32[]{:S(2)}, u32[]{:S(2)}) async-start(f32[8,32,1024]{2,1,0:T(8,128)} %slice.27), calls=%async_computation | async-start | bytes 2097152 | tf_op jit(solution)/shard_map/all_to_all | solution.py:410
  9.0 2.9 %collective-permute-start.3 = (f32[32,1024]{1,0:T(8,128)}, f32[32,1024]{1,0:T(8,128)S(1)}, u32[]{:S(2)}, u32[]{:S(2)}) collective-permute-start(f32[32,1024]{1,0:T(8,128)} %convert_element_type.15.here_ref.refs_3_), channel_id=1, source_target_pairs={{0,24},{4,28},{8,16},{12,20},{16,8},{20,12},{24,0},{28,4},{1,25},{... | collective-permute-start | bytes 393224 | tf_op jit(solution)/shard_map/ppermute | solution.py:404
  12.5 14.6 %collective-permute-done.3 = f32[32,1024]{1,0:T(8,128)S(1)} collective-permute-done((f32[32,1024]{1,0:T(8,128)}, f32[32,1024]{1,0:T(8,128)S(1)}, u32[]{:S(2)}, u32[]{:S(2)}) %collective-permute-start.3) | collective-permute-done | bytes 131104 | tf_op jit(solution)/shard_map/ppermute | solution.py:404
  27.1 1.2 collective-permute-done.2
  28.5 1.1 slice.28
  29.6 3.6 %all-to-all-start.2 = ((f32[8,32,1024]{2,1,0:T(8,128)}), f32[8,32,1024]{2,1,0:T(8,128)S(1)}, u32[]{:S(2)}, u32[]{:S(2)}) async-start(f32[8,32,1024]{2,1,0:T(8,128)} %slice.28), calls=%async_computation.2 | async-start | bytes 2097152 | tf_op jit(solution)/shard_map/all_to_all | solution.py:410
  40.2 4.2 %site.1 = f32[32,8,8,128]{3,2,1,0:T(8,128)} custom-call(f32[35]{0:T(128)} %pad_maximum_fusion.1.coef_ref, s32[1]{0:T(128)} %bitcast.6.me_ref, f32[32,1024]{1,0:T(8,128)} %convert_element_type.15.here_ref.refs_3_, f32[32,1024]{1,0:T(8,128)} %copy-done.10, f32[3,32,1024]{2,1,0:T(8,128)} %copy-done.3, f32[3,32,1024]{2,1,0:T(8,128)} %copy-done.6), custom_call_target="tpu_custom_call" | custom-call | tf_op jit(solution)/shard_map/site/pallas_call | solution.py:432
  44.4 14.3 %filter.2 = f32[4,8,8,1024]{3,2,1,0:T(8,128)} custom-call(f32[35]{0:T(128)} %pad_maximum_fusion.1.coef_ref, f32[8,32,1024]{2,1,0:T(8,128)S(1)} %all-to-all-done.vec_ref, f32[32,8,8,128]{3,2,1,0:T(8,128)} %site.1), custom_call_target="tpu_custom_call" | custom-call | tf_op jit(solution)/shard_map/filter/pallas_call | solution.py:448
  58.7 6.2 %all-to-all-start.1 = ((f32[32,8,1024]{2,1,0:T(8,128)}), f32[32,8,1024]{2,1,0:T(8,128)S(1)}, u32[]{:S(2)}, u32[]{:S(2)}) async-start(f32[32,8,1024]{2,1,0:T(8,128)} %bitcast.22), calls=%async_computation.1 | async-start | bytes 2097152 | tf_op jit(solution)/shard_map/all_to_all | solution.py:461
  64.9 14.3 %filter.3 = f32[4,8,8,1024]{3,2,1,0:T(8,128)} custom-call(f32[35]{0:T(128)} %pad_maximum_fusion.1.coef_ref, f32[8,32,1024]{2,1,0:T(8,128)S(1)} %all-to-all-done.2.vec_ref, f32[32,8,8,128]{3,2,1,0:T(8,128)} %site.1), custom_call_target="tpu_custom_call" | custom-call | tf_op jit(solution)/shard_map/filter/pallas_call | solution.py:448
  79.2 11.9 %all-to-all-done.1.refs_0_ = f32[32,8,1024]{2,1,0:T(8,128)S(1)} async-done(((f32[32,8,1024]{2,1,0:T(8,128)}), f32[32,8,1024]{2,1,0:T(8,128)S(1)}, u32[]{:S(2)}, u32[]{:S(2)}) %all-to-all-start.1) | async-done | bytes 1048608 | tf_op jit(solution)/shard_map/all_to_all | solution.py:461
  91.1 3.8 %all-to-all-start.3 = ((f32[32,8,1024]{2,1,0:T(8,128)}), f32[32,8,1024]{2,1,0:T(8,128)S(1)}, u32[]{:S(2)}, u32[]{:S(2)}) async-start(f32[32,8,1024]{2,1,0:T(8,128)} %bitcast.21), calls=%async_computation.3 | async-start | bytes 2097152 | tf_op jit(solution)/shard_map/all_to_all | solution.py:461
  94.9 26.0 %all-to-all-done.3.refs_1_ = f32[32,8,1024]{2,1,0:T(8,128)S(1)} async-done(((f32[32,8,1024]{2,1,0:T(8,128)}), f32[32,8,1024]{2,1,0:T(8,128)S(1)}, u32[]{:S(2)}, u32[]{:S(2)}) %all-to-all-start.3) | async-done | bytes 1048608 | tf_op jit(solution)/shard_map/all_to_all | solution.py:461
  120.9 6.3 %gram.1 = (f32[64,128]{1,0:T(8,128)}, f32[64,1024]{1,0:T(8,128)}, f32[8,64,768]{2,1,0:T(8,128)}, f32[8,64,256]{2,1,0:T(8,128)}) custom-call(f32[32,8,1024]{2,1,0:T(8,128)S(1)} %all-to-all-done.1.refs_0_, f32[32,8,1024]{2,1,0:T(8,128)S(1)} %all-to-all-done.3.refs_1_, s32[1]{0:T(128)} %bitcast.12.refs_2_, f32[32,1024]{1,0:T(8,128)} %convert_element_type.15.here_ref.refs_3_), custom_call_target="tpu_custom_call" | custom-call | tf_op jit(solution)/shard_map/gram/pallas_call | solution.py:469
  127.3 1.4 collective-permute-start.19
  129.3 5.0 %collective-permute-done.5 = f32[64,128]{1,0:T(8,128)S(1)} collective-permute-done((f32[64,128]{1,0:T(8,128)}, f32[64,128]{1,0:T(8,128)S(1)}, u32[]{:S(2)}, u32[]{:S(2)}) %collective-permute-start.5) | collective-permute-done | bytes 32800 | tf_op jit(solution)/shard_map/ppermute | solution.py:501
  135.0 0.8 collective-permute-start.6
  135.9 4.0 %collective-permute-done.6 = f32[64,128]{1,0:T(8,128)S(1)} collective-permute-done((f32[64,128]{1,0:T(8,128)S(1)}, f32[64,128]{1,0:T(8,128)S(1)}, u32[]{:S(2)}, u32[]{:S(2)}) %collective-permute-start.6) | collective-permute-done | bytes 32800 | tf_op jit(solution)/shard_map/ppermute | solution.py:501
  139.9 1.2 collective-permute-done.7
  141.1 1.5 collective-permute-start.8
  142.6 2.5 %collective-permute-done.8 = f32[64,128]{1,0:T(8,128)S(1)} collective-permute-done((f32[64,128]{1,0:T(8,128)S(1)}, f32[64,128]{1,0:T(8,128)S(1)}, u32[]{:S(2)}, u32[]{:S(2)}) %collective-permute-start.8) | collective-permute-done | bytes 32800 | tf_op jit(solution)/shard_map/ppermute | solution.py:501
  145.1 1.5 collective-permute-start.9
  146.6 1.9 edge.1
  149.1 5.9 %solve.1 = (f32[64,64]{1,0:T(8,128)}, f32[64,128]{1,0:T(8,128)}, f32[16,8,256]{2,1,0:T(8,128)}, f32[16,8,256]{2,1,0:T(8,128)}) custom-call(s32[1]{0:T(128)} %bitcast.place_ref, f32[64,128]{1,0:T(8,128)} %copy-done.8, f32[64,128]{1,0:T(8,128)S(1)} %collective-permute-done.9.other_ref, f32[8,64,768]{2,1,0:T(8,128)} %get-tuple-element.21.low_ref), custom_call_target="tpu_custom_call" | custom-call | tf_op jit(solution)/shard_map/solve/pallas_call | solution.py:522
  154.9 0.8 collective-permute-start.10
  156.5 3.1 %rest.1 = (f32[16,8,512]{2,1,0:T(8,128)}, f32[16,8,512]{2,1,0:T(8,128)}, f32[16,8,256]{2,1,0:T(8,128)}, f32[16,8,256]{2,1,0:T(8,128)}) custom-call(s32[1]{0:T(128)} %bitcast.place_ref, f32[64,64]{1,0:T(8,128)} %get-tuple-element.22.inv_ref, f32[8,64,768]{2,1,0:T(8,128)} %get-tuple-element.21.low_ref, f32[8,64,256]{2,1,0:T(8,128)} %get-tuple-element.23.high_ref), custom_call_target="tpu_custom_call" | custom-call | tf_op jit(solution)/shard_map/rest/pallas_call | solution.py:531
  159.6 3.6 %near.1 = (f32[16,8,1024]{2,1,0:T(8,128)}, f32[16,8,1024]{2,1,0:T(8,128)}) custom-call(s32[1]{0:T(128)} %bitcast.place_ref, f32[64,64]{1,0:T(8,128)} %get-tuple-element.22.inv_ref, f32[8,64,768]{2,1,0:T(8,128)} %get-tuple-element.21.low_ref, f32[8,64,256]{2,1,0:T(8,128)} %get-tuple-element.23.high_ref), custom_call_target="tpu_custom_call" | custom-call | tf_op jit(solution)/shard_map/near/pallas_call | solution.py:539
  163.2 1.4 collective-permute-start.11
  164.5 4.5 %collective-permute-start.14 = (f32[16,8,256]{2,1,0:T(8,128)}, f32[16,8,256]{2,1,0:T(8,128)}, u32[]{:S(2)}, u32[]{:S(2)}) collective-permute-start(f32[16,8,256]{2,1,0:T(8,128)} %get-tuple-element.29), channel_id=1, source_target_pairs={{0,3},{3,0},{4,7},{7,4},{8,11},{11,8},{12,15},{15,12},{16,19},{19,... | collective-permute-start | bytes 393224 | tf_op jit(solution)/shard_map/ppermute | solution.py:557
  169.1 1.3 collective-permute-start.21
  170.8 2.3 %collective-permute-done.21 = f32[64,64]{1,0:T(8,128)S(1)} collective-permute-done((f32[64,64]{1,0:T(8,128)S(1)}, f32[64,64]{1,0:T(8,128)S(1)}, u32[]{:S(2)}, u32[]{:S(2)}) %collective-permute-start.21) | collective-permute-done | bytes 16416 | tf_op jit(solution)/shard_map/ppermute | solution.py:501
  173.1 0.9 collective-permute-start.22
  174.0 3.0 %collective-permute-done.22 = f32[64,64]{1,0:T(8,128)S(1)} collective-permute-done((f32[64,64]{1,0:T(8,128)S(1)}, f32[64,64]{1,0:T(8,128)S(1)}, u32[]{:S(2)}, u32[]{:S(2)}) %collective-permute-start.22) | collective-permute-done | bytes 16416 | tf_op jit(solution)/shard_map/ppermute | solution.py:501
  177.0 1.3 collective-permute-start.25
  178.3 6.6 %collective-permute-start.23 = (f32[64,64]{1,0:T(8,128)S(1)}, f32[64,64]{1,0:T(8,128)S(1)}, u32[]{:S(2)}, u32[]{:S(2)}) collective-permute-start(f32[64,64]{1,0:T(8,128)S(1)} %add.128), channel_id=1, source_target_pairs={{0,1},{1,0},{2,3},{3,2},{4,5},{5,4},{6,7},{7,6},{8,9},{9,8},{10,11... | collective-permute-start | bytes 49160 | tf_op jit(solution)/shard_map/ppermute | solution.py:511
  185.7 2.3 %collective-permute-start.13 = (f32[16,8,512]{2,1,0:T(8,128)}, f32[16,8,512]{2,1,0:T(8,128)}, u32[]{:S(2)}, u32[]{:S(2)}) collective-permute-start(f32[16,8,512]{2,1,0:T(8,128)} %get-tuple-element.28), channel_id=1, source_target_pairs={{0,3},{1,2},{2,1},{3,0},{4,7},{5,6},{6,5},{7,4},{8,11},{9,10},{10,... | collective-permute-start | bytes 786440 | tf_op jit(solution)/shard_map/ppermute | solution.py:557
  188.0 1.2 collective-permute-start.16
  190.4 15.3 %collective-permute-done.12 = f32[16,8,512]{2,1,0:T(8,128)S(1)} collective-permute-done((f32[16,8,512]{2,1,0:T(8,128)}, f32[16,8,512]{2,1,0:T(8,128)S(1)}, u32[]{:S(2)}, u32[]{:S(2)}) %collective-permute-start.12) | collective-permute-done | bytes 262176 | tf_op jit(solution)/shard_map/ppermute | solution.py:557
  205.7 2.2 collective-permute-start.17
  208.0 1.0 constant_dynamic-update-slice_fusion.1
  208.9 1.8 extra.1
  210.8 1.3 collective-permute-start.18
  212.1 1.0 add_dynamic-update-slice_fusion.1
  213.1 1.1 constant_dynamic-update-slice_fusion
  214.2 5.3 %collective-permute-done.18 = f32[16,8,256]{2,1,0:T(8,128)S(1)} collective-permute-done((f32[16,8,256]{2,1,0:T(8,128)}, f32[16,8,256]{2,1,0:T(8,128)S(1)}, u32[]{:S(2)}, u32[]{:S(2)}) %collective-permute-start.18) | collective-permute-done | bytes 131104 | tf_op jit(solution)/shard_map/ppermute | solution.py:557
  219.4 0.9 add_dynamic-update-slice_fusion
  220.4 1.3 copy-done.1
  (78 shorter events, 9.1 us)
Async XLA Ops:
  0.6 7.7 %copy-start.9 = (s32[32,1024]{1,0:T(8,128)S(1)}, s32[32,1024]{1,0:T(8,128)}, u32[]{:S(2)}) copy-start(s32[32,1024]{1,0:T(8,128)} %param.4) | copy-start | bytes 393220
  3.0 25.5 %copy-start.2 = (f32[16,32,1024]{2,1,0:T(8,128)S(1)}, f32[16,32,1024]{2,1,0:T(8,128)}, u32[]{:S(2)}) copy-start(f32[16,32,1024]{2,1,0:T(8,128)} %param.3) | copy-start | bytes 6291460
  3.0 26.6 %all-to-all-start = ((f32[8,32,1024]{2,1,0:T(8,128)}), f32[8,32,1024]{2,1,0:T(8,128)S(1)}, u32[]{:S(2)}, u32[]{:S(2)}) async-start(f32[8,32,1024]{2,1,0:T(8,128)} %slice.27), calls=%async_computation | async-start | bytes 2097152 | tf_op jit(solution)/shard_map/all_to_all | solution.py:410
  9.0 18.1 %collective-permute-start.3 = (f32[32,1024]{1,0:T(8,128)}, f32[32,1024]{1,0:T(8,128)S(1)}, u32[]{:S(2)}, u32[]{:S(2)}) collective-permute-start(f32[32,1024]{1,0:T(8,128)} %convert_element_type.15.here_ref.refs_3_), channel_id=1, source_target_pairs={{0,24},{4,28},{8,16},{12,20},{16,8},{20,12},{24,0},{28,4},{1,25},{... | collective-permute-start | bytes 393224 | tf_op jit(solution)/shard_map/ppermute | solution.py:404
  11.9 16.5 %collective-permute-start.2 = (f32[32,1024]{1,0:T(8,128)}, f32[32,1024]{1,0:T(8,128)S(1)}, u32[]{:S(2)}, u32[]{:S(2)}) collective-permute-start(f32[32,1024]{1,0:T(8,128)} %convert_element_type.15.here_ref.refs_3_), channel_id=1, source_target_pairs={{0,16},{4,20},{8,24},{12,28},{16,0},{20,4},{24,8},{28,12},{1,17},{... | collective-permute-start | bytes 393224 | tf_op jit(solution)/shard_map/ppermute | solution.py:404
  12.5 16.0 %collective-permute-start.1 = (f32[32,1024]{1,0:T(8,128)}, f32[32,1024]{1,0:T(8,128)S(1)}, u32[]{:S(2)}, u32[]{:S(2)}) collective-permute-start(f32[32,1024]{1,0:T(8,128)} %convert_element_type.15.here_ref.refs_3_), channel_id=1, source_target_pairs={{0,8},{4,12},{8,0},{12,4},{16,24},{20,28},{24,16},{28,20},{1,9},{5... | collective-permute-start | bytes 393224 | tf_op jit(solution)/shard_map/ppermute | solution.py:404
  28.5 5.1 %copy-start.3 = (f32[3,32,1024]{2,1,0:T(8,128)}, f32[3,32,1024]{2,1,0:T(8,128)S(1)}, u32[]{:S(2)}) copy-start(f32[3,32,1024]{2,1,0:T(8,128)S(1)} %pad_maximum_fusion.own_ref) | copy-start | bytes 1179652
  28.5 5.1 %copy-start.13 = (s32[4]{0:T(128)S(1)}, s32[4]{0:T(128)}, u32[]{:S(2)}) copy-start(s32[4]{0:T(128)} %param.5) | copy-start | bytes 52
  29.6 29.1 %all-to-all-start.2 = ((f32[8,32,1024]{2,1,0:T(8,128)}), f32[8,32,1024]{2,1,0:T(8,128)S(1)}, u32[]{:S(2)}, u32[]{:S(2)}) async-start(f32[8,32,1024]{2,1,0:T(8,128)} %slice.28), calls=%async_computation.2 | async-start | bytes 2097152 | tf_op jit(solution)/shard_map/all_to_all | solution.py:410
  33.2 6.2 %collective-permute-start = (f32[32,1024]{1,0:T(8,128)}, f32[32,1024]{1,0:T(8,128)S(1)}, u32[]{:S(2)}, u32[]{:S(2)}) collective-permute-start(f32[32,1024]{1,0:T(8,128)} %convert_element_type.15.here_ref.refs_3_), channel_id=1, source_target_pairs={{0,4},{4,0},{8,12},{12,8},{16,20},{20,16},{24,28},{28,24},{1,5},{5... | collective-permute-start | bytes 393224 | tf_op jit(solution)/shard_map/ppermute | solution.py:404
  33.6 5.8 %collective-permute-start.4 = (f32[3,32,1024]{2,1,0:T(8,128)S(1)}, f32[3,32,1024]{2,1,0:T(8,128)S(1)}, u32[]{:S(2)}, u32[]{:S(2)}) collective-permute-start(f32[3,32,1024]{2,1,0:T(8,128)S(1)} %pad_maximum_fusion.own_ref), channel_id=1, source_target_pairs={{0,4},{4,0},{8,12},{12,8},{16,20},{20,16},{24,28},{28,24},{1,5},{5... | collective-permute-start | bytes 1179656 | tf_op jit(solution)/shard_map/ppermute | solution.py:404
  39.4 0.7 copy-start.10
  39.4 0.8 copy-start.6
  58.7 32.4 %all-to-all-start.1 = ((f32[32,8,1024]{2,1,0:T(8,128)}), f32[32,8,1024]{2,1,0:T(8,128)S(1)}, u32[]{:S(2)}, u32[]{:S(2)}) async-start(f32[32,8,1024]{2,1,0:T(8,128)} %bitcast.22), calls=%async_computation.1 | async-start | bytes 2097152 | tf_op jit(solution)/shard_map/all_to_all | solution.py:461
  91.1 29.8 %all-to-all-start.3 = ((f32[32,8,1024]{2,1,0:T(8,128)}), f32[32,8,1024]{2,1,0:T(8,128)S(1)}, u32[]{:S(2)}, u32[]{:S(2)}) async-start(f32[32,8,1024]{2,1,0:T(8,128)} %bitcast.21), calls=%async_computation.3 | async-start | bytes 2097152 | tf_op jit(solution)/shard_map/all_to_all | solution.py:461
  127.3 19.3 %collective-permute-start.19 = (f32[64,1024]{1,0:T(8,128)}, f32[64,1024]{1,0:T(8,128)S(1)}, u32[]{:S(2)}, u32[]{:S(2)}) collective-permute-start(f32[64,1024]{1,0:T(8,128)} %get-tuple-element.35), channel_id=1, source_target_pairs={{1,0},{2,1},{3,2},{7,3},{6,7},{5,6},{4,5},{8,4},{9,8},{10,9},{11,1... | collective-permute-start | bytes 786440 | tf_op jit(solution)/shard_map/ppermute | solution.py:481
  128.7 5.6 %collective-permute-start.5 = (f32[64,128]{1,0:T(8,128)}, f32[64,128]{1,0:T(8,128)S(1)}, u32[]{:S(2)}, u32[]{:S(2)}) collective-permute-start(f32[64,128]{1,0:T(8,128)} %get-tuple-element.20), channel_id=1, source_target_pairs={{0,1},{1,0},{2,3},{3,2},{4,5},{5,4},{6,7},{7,6},{8,9},{9,8},{10,11... | collective-permute-start | bytes 98312 | tf_op jit(solution)/shard_map/ppermute | solution.py:501
  135.0 4.8 %collective-permute-start.6 = (f32[64,128]{1,0:T(8,128)S(1)}, f32[64,128]{1,0:T(8,128)S(1)}, u32[]{:S(2)}, u32[]{:S(2)}) collective-permute-start(f32[64,128]{1,0:T(8,128)S(1)} %add.113), channel_id=1, source_target_pairs={{0,2},{1,3},{2,0},{3,1},{4,6},{5,7},{6,4},{7,5},{8,10},{9,11},{10,... | collective-permute-start | bytes 98312 | tf_op jit(solution)/shard_map/ppermute | solution.py:501
  139.9 1.2 collective-permute-start.7
  141.1 14.7 %copy-start = (f32[8,64,256]{2,1,0:T(8,128)S(1)}, f32[8,64,256]{2,1,0:T(8,128)}, u32[]{:S(2)}) copy-start(f32[8,64,256]{2,1,0:T(8,128)} %get-tuple-element.23.high_ref) | copy-start | bytes 1572868
  141.1 4.0 %collective-permute-start.8 = (f32[64,128]{1,0:T(8,128)S(1)}, f32[64,128]{1,0:T(8,128)S(1)}, u32[]{:S(2)}, u32[]{:S(2)}) collective-permute-start(f32[64,128]{1,0:T(8,128)S(1)} %add.115), channel_id=1, source_target_pairs={{0,8},{4,12},{8,0},{12,4},{16,24},{20,28},{24,16},{28,20},{1,9},{5... | collective-permute-start | bytes 98312 | tf_op jit(solution)/shard_map/ppermute | solution.py:501
  145.1 4.0 %copy-start.8 = (f32[64,128]{1,0:T(8,128)}, f32[64,128]{1,0:T(8,128)S(1)}, u32[]{:S(2)}) copy-start(f32[64,128]{1,0:T(8,128)S(1)} %add.116.mine_ref) | copy-start | bytes 98308
  145.1 4.0 %collective-permute-start.9 = (f32[64,128]{1,0:T(8,128)S(1)}, f32[64,128]{1,0:T(8,128)S(1)}, u32[]{:S(2)}, u32[]{:S(2)}) collective-permute-start(f32[64,128]{1,0:T(8,128)S(1)} %add.116.mine_ref), channel_id=1, source_target_pairs={{0,16},{4,20},{8,24},{12,28},{16,0},{20,4},{24,8},{28,12},{1,17},{... | collective-permute-start | bytes 98312 | tf_op jit(solution)/shard_map/ppermute | solution.py:501
  148.5 20.6 %collective-permute-start.20 = (f32[64,64]{1,0:T(8,128)}, f32[64,64]{1,0:T(8,128)S(1)}, u32[]{:S(2)}, u32[]{:S(2)}) collective-permute-start(f32[64,64]{1,0:T(8,128)} %edge.1), channel_id=1, source_target_pairs={{0,4},{4,0},{8,12},{12,8},{16,20},{20,16},{24,28},{28,24},{1,5},{5... | collective-permute-start | bytes 49160 | tf_op jit(solution)/shard_map/ppermute | solution.py:501
  154.9 19.1 %collective-permute-start.10 = (f32[16,8,256]{2,1,0:T(8,128)}, f32[16,8,256]{2,1,0:T(8,128)S(1)}, u32[]{:S(2)}, u32[]{:S(2)}) collective-permute-start(f32[16,8,256]{2,1,0:T(8,128)} %get-tuple-element.25), channel_id=1, source_target_pairs={{0,2},{1,3},{2,0},{3,1},{4,6},{5,7},{6,4},{7,5},{8,10},{9,11},{10,... | collective-permute-start | bytes 393224 | tf_op jit(solution)/shard_map/ppermute | solution.py:557
  155.7 53.2 %collective-permute-start.15 = (f32[8,64,256]{2,1,0:T(8,128)S(1)}, f32[8,64,256]{2,1,0:T(8,128)S(1)}, u32[]{:S(2)}, u32[]{:S(2)}) collective-permute-start(f32[8,64,256]{2,1,0:T(8,128)S(1)} %copy-done), channel_id=1, source_target_pairs={{1,2},{2,1},{5,6},{6,5},{9,10},{10,9},{13,14},{14,13},{17,18},{18,... | collective-permute-start | bytes 1572872 | tf_op jit(solution)/shard_map/ppermute | solution.py:484
  156.4 6.7 %copy-start.12 = (f32[16,8,256]{2,1,0:T(8,128)S(1)}, f32[16,8,256]{2,1,0:T(8,128)}, u32[]{:S(2)}) copy-start(f32[16,8,256]{2,1,0:T(8,128)} %get-tuple-element.26) | copy-start | bytes 393220
  156.4 12.7 %copy-start.7 = (f32[64,64]{1,0:T(8,128)S(1)}, f32[64,64]{1,0:T(8,128)}, u32[]{:S(2)}) copy-start(f32[64,64]{1,0:T(8,128)} %edge.1) | copy-start | bytes 49156
  163.1 7.5 %copy-start.5 = (f32[16,8,1024]{2,1,0:T(8,128)S(1)}, f32[16,8,1024]{2,1,0:T(8,128)}, u32[]{:S(2)}) copy-start(f32[16,8,1024]{2,1,0:T(8,128)} %get-tuple-element.24) | copy-start | bytes 1572868
  163.2 26.1 %copy-start.11 = (f32[64,128]{1,0:T(8,128)S(1)}, f32[64,128]{1,0:T(8,128)}, u32[]{:S(2)}) copy-start(f32[64,128]{1,0:T(8,128)} %get-tuple-element.34) | copy-start | bytes 98308
  163.2 15.2 %collective-permute-start.11 = (f32[16,8,256]{2,1,0:T(8,128)S(1)}, f32[16,8,256]{2,1,0:T(8,128)S(1)}, u32[]{:S(2)}, u32[]{:S(2)}) collective-permute-start(f32[16,8,256]{2,1,0:T(8,128)S(1)} %copy-done.12), channel_id=1, source_target_pairs={{0,3},{1,2},{2,1},{3,0},{4,7},{5,6},{6,5},{7,4},{8,11},{9,10},{10,... | collective-permute-start | bytes 393224 | tf_op jit(solution)/shard_map/ppermute | solution.py:557
  164.5 24.9 %copy-start.4 = (f32[64,64]{1,0:T(8,128)S(1)}, f32[64,64]{1,0:T(8,128)}, u32[]{:S(2)}) copy-start(f32[64,64]{1,0:T(8,128)} %get-tuple-element.22.inv_ref) | copy-start | bytes 49156
  164.5 47.5 %collective-permute-start.14 = (f32[16,8,256]{2,1,0:T(8,128)}, f32[16,8,256]{2,1,0:T(8,128)}, u32[]{:S(2)}, u32[]{:S(2)}) collective-permute-start(f32[16,8,256]{2,1,0:T(8,128)} %get-tuple-element.29), channel_id=1, source_target_pairs={{0,3},{3,0},{4,7},{7,4},{8,11},{11,8},{12,15},{15,12},{16,19},{19,... | collective-permute-start | bytes 393224 | tf_op jit(solution)/shard_map/ppermute | solution.py:557
  169.1 4.0 %collective-permute-start.21 = (f32[64,64]{1,0:T(8,128)S(1)}, f32[64,64]{1,0:T(8,128)S(1)}, u32[]{:S(2)}, u32[]{:S(2)}) collective-permute-start(f32[64,64]{1,0:T(8,128)S(1)} %add.126), channel_id=1, source_target_pairs={{0,8},{4,12},{8,0},{12,4},{16,24},{20,28},{24,16},{28,20},{1,9},{5... | collective-permute-start | bytes 49160 | tf_op jit(solution)/shard_map/ppermute | solution.py:501
  173.1 3.9 %collective-permute-start.22 = (f32[64,64]{1,0:T(8,128)S(1)}, f32[64,64]{1,0:T(8,128)S(1)}, u32[]{:S(2)}, u32[]{:S(2)}) collective-permute-start(f32[64,64]{1,0:T(8,128)S(1)} %add.127), channel_id=1, source_target_pairs={{0,16},{4,20},{8,24},{12,28},{16,0},{20,4},{24,8},{28,12},{1,17},{... | collective-permute-start | bytes 49160 | tf_op jit(solution)/shard_map/ppermute | solution.py:501
  177.0 7.9 %collective-permute-start.25 = (f32[64,64]{1,0:T(8,128)S(1)}, f32[64,64]{1,0:T(8,128)S(1)}, u32[]{:S(2)}, u32[]{:S(2)}) collective-permute-start(f32[64,64]{1,0:T(8,128)S(1)} %add.128), channel_id=1, source_target_pairs={{0,3},{1,2},{2,1},{3,0},{4,7},{5,6},{6,5},{7,4},{8,11},{9,10},{10,... | collective-permute-start | bytes 49160 | tf_op jit(solution)/shard_map/ppermute | solution.py:511
  178.3 7.4 %collective-permute-start.24 = (f32[64,64]{1,0:T(8,128)S(1)}, f32[64,64]{1,0:T(8,128)S(1)}, u32[]{:S(2)}, u32[]{:S(2)}) collective-permute-start(f32[64,64]{1,0:T(8,128)S(1)} %add.128), channel_id=1, source_target_pairs={{0,2},{1,3},{2,0},{3,1},{4,6},{5,7},{6,4},{7,5},{8,10},{9,11},{10,... | collective-permute-start | bytes 49160 | tf_op jit(solution)/shard_map/ppermute | solution.py:511
  178.3 9.7 %collective-permute-start.23 = (f32[64,64]{1,0:T(8,128)S(1)}, f32[64,64]{1,0:T(8,128)S(1)}, u32[]{:S(2)}, u32[]{:S(2)}) collective-permute-start(f32[64,64]{1,0:T(8,128)S(1)} %add.128), channel_id=1, source_target_pairs={{0,1},{1,0},{2,3},{3,2},{4,5},{5,4},{6,7},{7,6},{8,9},{9,8},{10,11... | collective-permute-start | bytes 49160 | tf_op jit(solution)/shard_map/ppermute | solution.py:511
  185.0 20.7 %collective-permute-start.12 = (f32[16,8,512]{2,1,0:T(8,128)}, f32[16,8,512]{2,1,0:T(8,128)S(1)}, u32[]{:S(2)}, u32[]{:S(2)}) collective-permute-start(f32[16,8,512]{2,1,0:T(8,128)} %get-tuple-element.27), channel_id=1, source_target_pairs={{0,2},{1,3},{2,0},{3,1},{4,6},{5,7},{6,4},{7,5},{8,10},{9,11},{10,... | collective-permute-start | bytes 786440 | tf_op jit(solution)/shard_map/ppermute | solution.py:557
  185.7 22.2 %collective-permute-start.13 = (f32[16,8,512]{2,1,0:T(8,128)}, f32[16,8,512]{2,1,0:T(8,128)}, u32[]{:S(2)}, u32[]{:S(2)}) collective-permute-start(f32[16,8,512]{2,1,0:T(8,128)} %get-tuple-element.28), channel_id=1, source_target_pairs={{0,3},{1,2},{2,1},{3,0},{4,7},{5,6},{6,5},{7,4},{8,11},{9,10},{10,... | collective-permute-start | bytes 786440 | tf_op jit(solution)/shard_map/ppermute | solution.py:557
  188.0 25.0 %collective-permute-start.16 = (f32[16,8,1024]{2,1,0:T(8,128)}, f32[16,8,1024]{2,1,0:T(8,128)}, u32[]{:S(2)}, u32[]{:S(2)}) collective-permute-start(f32[16,8,1024]{2,1,0:T(8,128)} %get-tuple-element.31), channel_id=1, source_target_pairs={{0,1},{1,0},{2,3},{3,2},{4,5},{5,4},{6,7},{7,6},{8,9},{9,8},{10,11... | collective-permute-start | bytes 1572872 | tf_op jit(solution)/shard_map/ppermute | solution.py:557
  205.7 8.5 %collective-permute-start.17 = (f32[16,8,256]{2,1,0:T(8,128)}, f32[16,8,256]{2,1,0:T(8,128)}, u32[]{:S(2)}, u32[]{:S(2)}) collective-permute-start(f32[16,8,256]{2,1,0:T(8,128)} %get-tuple-element.32), channel_id=1, source_target_pairs={{0,2},{3,1},{4,6},{7,5},{8,10},{11,9},{12,14},{15,13},{16,18},{19,... | collective-permute-start | bytes 393224 | tf_op jit(solution)/shard_map/ppermute | solution.py:557
  210.8 8.7 %collective-permute-start.18 = (f32[16,8,256]{2,1,0:T(8,128)}, f32[16,8,256]{2,1,0:T(8,128)S(1)}, u32[]{:S(2)}, u32[]{:S(2)}) collective-permute-start(f32[16,8,256]{2,1,0:T(8,128)} %get-tuple-element.33), channel_id=1, source_target_pairs={{1,0},{2,3},{5,4},{6,7},{9,8},{10,11},{13,12},{14,15},{17,16},{18,... | collective-permute-start | bytes 393224 | tf_op jit(solution)/shard_map/ppermute | solution.py:557
  220.4 1.3 copy-start.1

commit v8 on v7

--- a/solution.py
+++ b/solution.py
@@ -527,7 +527,7 @@
         + [head_piece] * half,
         scratch_shapes=products_scratch,
         name="solve",
-    )(place[None], sums, held(pending), low)
+    )(place[None], sums, held(pending), held(low))
     blocks = pl.pallas_call(
         functools.partial(rest_kernel, targets=far, **static),
         in_specs=[smem] + [vmem] * 3,
@@ -535,7 +535,7 @@
         out_shape=[tail_piece] * half + [high_piece] * half,
         scratch_shapes=products_scratch,
         name="rest",
-    )(place[None], inverse, low, high)
+    )(place[None], inverse, held(low), held(high))
     own_block, beside_block = pl.pallas_call(
         functools.partial(near_kernel, targets=near, **static),
         in_specs=[smem] + [vmem] * 3,
@@ -543,7 +543,7 @@
         out_shape=[piece] * half,
         scratch_shapes=products_scratch,
         name="near",
-    )(place[None], inverse, low, high)
+    )(place[None], inverse, held(low), held(high))
     own_extra, beside_extra = pl.pallas_call(
         functools.partial(extra_kernel, targets=near, **static),
         in_specs=[smem] + [vmem] * 2,

time: 223 us -> 222 us (level)
  transfers between devices with their start and end apart: 30 -> 30, of which waited for: 15 -> 15; matrix products, arithmetic and copies ran while one was open for 4% -> 3% of each run, Pallas kernels for 22% -> 22%
where the time goes in v8:
time: 222 us; the launch traced here: 221 us
  waiting for transfers between devices  94.8 us (43%)
  Pallas kernels  53.8 us (24%)
  starting transfers between devices  52.9 us (24%)
  local copies, waits for them, and re-layouts  9.04 us (4%)
  between operations  4.95 us (2%)
  other arithmetic  4.18 us (2%)
    all_to_all x2, waiting for transfers between devices, whole_shards(): lax.all_to_all(done.reshape(devices, slab_rows, columns), both, split_axi...  37.9 us
    pallas_call x2, Pallas kernels, whole_shards(): pl.pallas_call(functools.partial(filter_kernel, slabs=groups), in_specs=[...  28.6 us
    ppermute x8, waiting for transfers between devices, across(): return lax.ppermute(block, 'vec', [(i, i ^ d) for i in sources])  21.7 us
    ppermute x8, waiting for transfers between devices, pairwise(): other = lax.ppermute(value, axis, [(i, i ^ bit) for i in range(count)])  18.6 us
    ppermute x5, waiting for transfers between devices, swap(): return lax.ppermute(value, 'strip', [(i, i ^ bit) for i in range(strips)])  16 us
    ppermute x8, starting transfers between devices, across(): return lax.ppermute(block, 'vec', [(i, i ^ d) for i in sources])  13.9 us
    all_to_all x2, starting transfers between devices, whole_shards(): lax.all_to_all(done.reshape(devices, slab_rows, columns), both, split_axi...  9.99 us
    all_to_all x2, starting transfers between devices, spread(): lax.all_to_all(part, 'strip', split_axis=0, concat_axis=0, tiled=True)  8.89 us
  transfers between devices with their start and end apart: 30, of which 15 were waited for; matrix products, arithmetic and copies ran while one was open for 3% of the time, Pallas kernels for 22%

profile of v8, /device:TPU:0, one launch (start us, length us, event | category | flops | bytes accessed | tf_op | source)
XLA Modules:
  0.0 220.7 jit_solution(10289190392924001003)
XLA Ops:
  0.6 2.3 %slice.27 = f32[8,32,1024]{2,1,0:T(8,128)} slice(f32[16,32,1024]{2,1,0:T(8,128)} %param.3), slice={[0:8], [0:32], [0:1024]} | slice | bytes 2097152 | tf_op jit(solution)/shard_map/slice | solution.py:409
  3.0 5.3 %all-to-all-start = ((f32[8,32,1024]{2,1,0:T(8,128)}), f32[8,32,1024]{2,1,0:T(8,128)S(1)}, u32[]{:S(2)}, u32[]{:S(2)}) async-start(f32[8,32,1024]{2,1,0:T(8,128)} %slice.27), calls=%async_computation | async-start | bytes 2097152 | tf_op jit(solution)/shard_map/all_to_all | solution.py:410
  9.0 2.9 %collective-permute-start.3 = (f32[32,1024]{1,0:T(8,128)}, f32[32,1024]{1,0:T(8,128)S(1)}, u32[]{:S(2)}, u32[]{:S(2)}) collective-permute-start(f32[32,1024]{1,0:T(8,128)} %convert_element_type.15.here_ref.refs_3_), channel_id=1, source_target_pairs={{0,24},{4,28},{8,16},{12,20},{16,8},{20,12},{24,0},{28,4},{1,25},{... | collective-permute-start | bytes 393224 | tf_op jit(solution)/shard_map/ppermute | solution.py:404
  12.5 14.6 %collective-permute-done.3 = f32[32,1024]{1,0:T(8,128)S(1)} collective-permute-done((f32[32,1024]{1,0:T(8,128)}, f32[32,1024]{1,0:T(8,128)S(1)}, u32[]{:S(2)}, u32[]{:S(2)}) %collective-permute-start.3) | collective-permute-done | bytes 131104 | tf_op jit(solution)/shard_map/ppermute | solution.py:404
  27.1 1.2 collective-permute-done.2
  28.5 1.1 slice.28
  29.6 3.6 %all-to-all-start.2 = ((f32[8,32,1024]{2,1,0:T(8,128)}), f32[8,32,1024]{2,1,0:T(8,128)S(1)}, u32[]{:S(2)}, u32[]{:S(2)}) async-start(f32[8,32,1024]{2,1,0:T(8,128)} %slice.28), calls=%async_computation.2 | async-start | bytes 2097152 | tf_op jit(solution)/shard_map/all_to_all | solution.py:410
  39.9 4.2 %site.1 = f32[32,8,8,128]{3,2,1,0:T(8,128)} custom-call(f32[35]{0:T(128)} %pad_maximum_fusion.1.coef_ref, s32[1]{0:T(128)} %bitcast.6.me_ref, f32[32,1024]{1,0:T(8,128)} %convert_element_type.15.here_ref.refs_3_, f32[32,1024]{1,0:T(8,128)} %copy-done.11, f32[3,32,1024]{2,1,0:T(8,128)} %copy-done.4, f32[3,32,1024]{2,1,0:T(8,128)} %copy-done.7), custom_call_target="tpu_custom_call" | custom-call | tf_op jit(solution)/shard_map/site/pallas_call | solution.py:432
  44.2 14.3 %filter.2 = f32[4,8,8,1024]{3,2,1,0:T(8,128)} custom-call(f32[35]{0:T(128)} %pad_maximum_fusion.1.coef_ref, f32[8,32,1024]{2,1,0:T(8,128)S(1)} %all-to-all-done.vec_ref, f32[32,8,8,128]{3,2,1,0:T(8,128)} %site.1), custom_call_target="tpu_custom_call" | custom-call | tf_op jit(solution)/shard_map/filter/pallas_call | solution.py:448
  58.5 6.2 %all-to-all-start.1 = ((f32[32,8,1024]{2,1,0:T(8,128)}), f32[32,8,1024]{2,1,0:T(8,128)S(1)}, u32[]{:S(2)}, u32[]{:S(2)}) async-start(f32[32,8,1024]{2,1,0:T(8,128)} %bitcast.22), calls=%async_computation.1 | async-start | bytes 2097152 | tf_op jit(solution)/shard_map/all_to_all | solution.py:461
  64.7 14.3 %filter.3 = f32[4,8,8,1024]{3,2,1,0:T(8,128)} custom-call(f32[35]{0:T(128)} %pad_maximum_fusion.1.coef_ref, f32[8,32,1024]{2,1,0:T(8,128)S(1)} %all-to-all-done.2.vec_ref, f32[32,8,8,128]{3,2,1,0:T(8,128)} %site.1), custom_call_target="tpu_custom_call" | custom-call | tf_op jit(solution)/shard_map/filter/pallas_call | solution.py:448
  79.0 11.9 %all-to-all-done.1.refs_0_ = f32[32,8,1024]{2,1,0:T(8,128)S(1)} async-done(((f32[32,8,1024]{2,1,0:T(8,128)}), f32[32,8,1024]{2,1,0:T(8,128)S(1)}, u32[]{:S(2)}, u32[]{:S(2)}) %all-to-all-start.1) | async-done | bytes 1048608 | tf_op jit(solution)/shard_map/all_to_all | solution.py:461
  90.9 3.8 %all-to-all-start.3 = ((f32[32,8,1024]{2,1,0:T(8,128)}), f32[32,8,1024]{2,1,0:T(8,128)S(1)}, u32[]{:S(2)}, u32[]{:S(2)}) async-start(f32[32,8,1024]{2,1,0:T(8,128)} %bitcast.21), calls=%async_computation.3 | async-start | bytes 2097152 | tf_op jit(solution)/shard_map/all_to_all | solution.py:461
  94.7 26.0 %all-to-all-done.3.refs_1_ = f32[32,8,1024]{2,1,0:T(8,128)S(1)} async-done(((f32[32,8,1024]{2,1,0:T(8,128)}), f32[32,8,1024]{2,1,0:T(8,128)S(1)}, u32[]{:S(2)}, u32[]{:S(2)}) %all-to-all-start.3) | async-done | bytes 1048608 | tf_op jit(solution)/shard_map/all_to_all | solution.py:461
  120.7 6.3 %gram.1 = (f32[64,128]{1,0:T(8,128)}, f32[64,1024]{1,0:T(8,128)}, f32[8,64,768]{2,1,0:T(8,128)}, f32[8,64,256]{2,1,0:T(8,128)}) custom-call(f32[32,8,1024]{2,1,0:T(8,128)S(1)} %all-to-all-done.1.refs_0_, f32[32,8,1024]{2,1,0:T(8,128)S(1)} %all-to-all-done.3.refs_1_, s32[1]{0:T(128)} %bitcast.12.refs_2_, f32[32,1024]{1,0:T(8,128)} %convert_element_type.15.here_ref.refs_3_), custom_call_target="tpu_custom_call" | custom-call | tf_op jit(solution)/shard_map/gram/pallas_call | solution.py:469
  127.0 1.4 collective-permute-start.19
  129.0 5.0 %collective-permute-done.5 = f32[64,128]{1,0:T(8,128)S(1)} collective-permute-done((f32[64,128]{1,0:T(8,128)}, f32[64,128]{1,0:T(8,128)S(1)}, u32[]{:S(2)}, u32[]{:S(2)}) %collective-permute-start.5) | collective-permute-done | bytes 32800 | tf_op jit(solution)/shard_map/ppermute | solution.py:501
  134.8 0.9 collective-permute-start.6
  135.7 3.9 %collective-permute-done.6 = f32[64,128]{1,0:T(8,128)S(1)} collective-permute-done((f32[64,128]{1,0:T(8,128)S(1)}, f32[64,128]{1,0:T(8,128)S(1)}, u32[]{:S(2)}, u32[]{:S(2)}) %collective-permute-start.6) | collective-permute-done | bytes 32800 | tf_op jit(solution)/shard_map/ppermute | solution.py:501
  139.6 1.2 collective-permute-done.7
  140.8 1.5 collective-permute-start.8
  142.3 2.5 %collective-permute-done.8 = f32[64,128]{1,0:T(8,128)S(1)} collective-permute-done((f32[64,128]{1,0:T(8,128)S(1)}, f32[64,128]{1,0:T(8,128)S(1)}, u32[]{:S(2)}, u32[]{:S(2)}) %collective-permute-start.8) | collective-permute-done | bytes 32800 | tf_op jit(solution)/shard_map/ppermute | solution.py:501
  144.7 1.5 collective-permute-start.9
  146.2 1.9 edge.1
  148.7 5.2 %solve.1 = (f32[64,64]{1,0:T(8,128)}, f32[64,128]{1,0:T(8,128)}, f32[16,8,256]{2,1,0:T(8,128)}, f32[16,8,256]{2,1,0:T(8,128)}) custom-call(s32[1]{0:T(128)} %bitcast.place_ref, f32[64,128]{1,0:T(8,128)} %copy-done.9, f32[64,128]{1,0:T(8,128)S(1)} %collective-permute-done.9.other_ref, f32[8,64,768]{2,1,0:T(8,128)S(1)} %copy-done), custom_call_target="tpu_custom_call" | custom-call | tf_op jit(solution)/shard_map/solve/pallas_call | solution.py:522
  153.9 0.9 collective-permute-start.10
  155.5 1.4 copy-done.1
  156.9 2.7 %rest.1 = (f32[16,8,512]{2,1,0:T(8,128)}, f32[16,8,512]{2,1,0:T(8,128)}, f32[16,8,256]{2,1,0:T(8,128)}, f32[16,8,256]{2,1,0:T(8,128)}) custom-call(s32[1]{0:T(128)} %bitcast.place_ref, f32[64,64]{1,0:T(8,128)} %get-tuple-element.22.inv_ref, f32[8,64,768]{2,1,0:T(8,128)S(1)} %copy-done.1, f32[8,64,256]{2,1,0:T(8,128)} %get-tuple-element.23.high_ref), custom_call_target="tpu_custom_call" | custom-call | tf_op jit(solution)/shard_map/rest/pallas_call | solution.py:531
  159.6 3.1 %near.1 = (f32[16,8,1024]{2,1,0:T(8,128)}, f32[16,8,1024]{2,1,0:T(8,128)}) custom-call(s32[1]{0:T(128)} %bitcast.place_ref, f32[64,64]{1,0:T(8,128)} %get-tuple-element.22.inv_ref, f32[8,64,768]{2,1,0:T(8,128)S(1)} %copy-done.1, f32[8,64,256]{2,1,0:T(8,128)} %get-tuple-element.23.high_ref), custom_call_target="tpu_custom_call" | custom-call | tf_op jit(solution)/shard_map/near/pallas_call | solution.py:539
  162.7 1.3 collective-permute-start.11
  164.0 4.6 %collective-permute-start.14 = (f32[16,8,256]{2,1,0:T(8,128)}, f32[16,8,256]{2,1,0:T(8,128)}, u32[]{:S(2)}, u32[]{:S(2)}) collective-permute-start(f32[16,8,256]{2,1,0:T(8,128)} %get-tuple-element.29), channel_id=1, source_target_pairs={{0,3},{3,0},{4,7},{7,4},{8,11},{11,8},{12,15},{15,12},{16,19},{19,... | collective-permute-start | bytes 393224 | tf_op jit(solution)/shard_map/ppermute | solution.py:557
  168.7 1.3 collective-permute-start.21
  170.2 2.4 %collective-permute-done.21 = f32[64,64]{1,0:T(8,128)S(1)} collective-permute-done((f32[64,64]{1,0:T(8,128)S(1)}, f32[64,64]{1,0:T(8,128)S(1)}, u32[]{:S(2)}, u32[]{:S(2)}) %collective-permute-start.21) | collective-permute-done | bytes 16416 | tf_op jit(solution)/shard_map/ppermute | solution.py:501
  172.6 0.8 collective-permute-start.22
  173.5 3.1 %collective-permute-done.22 = f32[64,64]{1,0:T(8,128)S(1)} collective-permute-done((f32[64,64]{1,0:T(8,128)S(1)}, f32[64,64]{1,0:T(8,128)S(1)}, u32[]{:S(2)}, u32[]{:S(2)}) %collective-permute-start.22) | collective-permute-done | bytes 16416 | tf_op jit(solution)/shard_map/ppermute | solution.py:501
  176.6 1.2 collective-permute-start.25
  177.8 6.2 %collective-permute-start.23 = (f32[64,64]{1,0:T(8,128)S(1)}, f32[64,64]{1,0:T(8,128)S(1)}, u32[]{:S(2)}, u32[]{:S(2)}) collective-permute-start(f32[64,64]{1,0:T(8,128)S(1)} %add.128), channel_id=1, source_target_pairs={{0,1},{1,0},{2,3},{3,2},{4,5},{5,4},{6,7},{7,6},{8,9},{9,8},{10,11... | collective-permute-start | bytes 49160 | tf_op jit(solution)/shard_map/ppermute | solution.py:511
  184.7 2.3 %collective-permute-start.13 = (f32[16,8,512]{2,1,0:T(8,128)}, f32[16,8,512]{2,1,0:T(8,128)}, u32[]{:S(2)}, u32[]{:S(2)}) collective-permute-start(f32[16,8,512]{2,1,0:T(8,128)} %get-tuple-element.28), channel_id=1, source_target_pairs={{0,3},{1,2},{2,1},{3,0},{4,7},{5,6},{6,5},{7,4},{8,11},{9,10},{10,... | collective-permute-start | bytes 786440 | tf_op jit(solution)/shard_map/ppermute | solution.py:557
  187.1 1.2 collective-permute-start.16
  189.4 15.3 %collective-permute-done.12 = f32[16,8,512]{2,1,0:T(8,128)S(1)} collective-permute-done((f32[16,8,512]{2,1,0:T(8,128)}, f32[16,8,512]{2,1,0:T(8,128)S(1)}, u32[]{:S(2)}, u32[]{:S(2)}) %collective-permute-start.12) | collective-permute-done | bytes 262176 | tf_op jit(solution)/shard_map/ppermute | solution.py:557
  204.8 2.2 collective-permute-start.17
  207.0 1.0 constant_dynamic-update-slice_fusion.1
  208.0 1.8 extra.1
  209.8 1.3 collective-permute-start.18
  211.1 1.0 add_dynamic-update-slice_fusion.1
  212.2 6.3 %collective-permute-done.18 = f32[16,8,256]{2,1,0:T(8,128)S(1)} collective-permute-done((f32[16,8,256]{2,1,0:T(8,128)}, f32[16,8,256]{2,1,0:T(8,128)S(1)}, u32[]{:S(2)}, u32[]{:S(2)}) %collective-permute-start.18) | collective-permute-done | bytes 131104 | tf_op jit(solution)/shard_map/ppermute | solution.py:557
  218.5 0.9 add_dynamic-update-slice_fusion
  219.4 1.3 copy-done.2
  (80 shorter events, 9.1 us)
Async XLA Ops:
  0.6 7.7 %copy-start.10 = (s32[32,1024]{1,0:T(8,128)S(1)}, s32[32,1024]{1,0:T(8,128)}, u32[]{:S(2)}) copy-start(s32[32,1024]{1,0:T(8,128)} %param.4) | copy-start | bytes 393220
  3.0 25.5 %copy-start.3 = (f32[16,32,1024]{2,1,0:T(8,128)S(1)}, f32[16,32,1024]{2,1,0:T(8,128)}, u32[]{:S(2)}) copy-start(f32[16,32,1024]{2,1,0:T(8,128)} %param.3) | copy-start | bytes 6291460
  3.0 26.6 %all-to-all-start = ((f32[8,32,1024]{2,1,0:T(8,128)}), f32[8,32,1024]{2,1,0:T(8,128)S(1)}, u32[]{:S(2)}, u32[]{:S(2)}) async-start(f32[8,32,1024]{2,1,0:T(8,128)} %slice.27), calls=%async_computation | async-start | bytes 2097152 | tf_op jit(solution)/shard_map/all_to_all | solution.py:410
  9.0 18.1 %collective-permute-start.3 = (f32[32,1024]{1,0:T(8,128)}, f32[32,1024]{1,0:T(8,128)S(1)}, u32[]{:S(2)}, u32[]{:S(2)}) collective-permute-start(f32[32,1024]{1,0:T(8,128)} %convert_element_type.15.here_ref.refs_3_), channel_id=1, source_target_pairs={{0,24},{4,28},{8,16},{12,20},{16,8},{20,12},{24,0},{28,4},{1,25},{... | collective-permute-start | bytes 393224 | tf_op jit(solution)/shard_map/ppermute | solution.py:404
  11.9 16.5 %collective-permute-start.2 = (f32[32,1024]{1,0:T(8,128)}, f32[32,1024]{1,0:T(8,128)S(1)}, u32[]{:S(2)}, u32[]{:S(2)}) collective-permute-start(f32[32,1024]{1,0:T(8,128)} %convert_element_type.15.here_ref.refs_3_), channel_id=1, source_target_pairs={{0,16},{4,20},{8,24},{12,28},{16,0},{20,4},{24,8},{28,12},{1,17},{... | collective-permute-start | bytes 393224 | tf_op jit(solution)/shard_map/ppermute | solution.py:404
  12.5 16.0 %collective-permute-start.1 = (f32[32,1024]{1,0:T(8,128)}, f32[32,1024]{1,0:T(8,128)S(1)}, u32[]{:S(2)}, u32[]{:S(2)}) collective-permute-start(f32[32,1024]{1,0:T(8,128)} %convert_element_type.15.here_ref.refs_3_), channel_id=1, source_target_pairs={{0,8},{4,12},{8,0},{12,4},{16,24},{20,28},{24,16},{28,20},{1,9},{5... | collective-permute-start | bytes 393224 | tf_op jit(solution)/shard_map/ppermute | solution.py:404
  28.5 5.1 %copy-start.4 = (f32[3,32,1024]{2,1,0:T(8,128)}, f32[3,32,1024]{2,1,0:T(8,128)S(1)}, u32[]{:S(2)}) copy-start(f32[3,32,1024]{2,1,0:T(8,128)S(1)} %pad_maximum_fusion.own_ref) | copy-start | bytes 1179652
  28.5 5.1 %copy-start.14 = (s32[4]{0:T(128)S(1)}, s32[4]{0:T(128)}, u32[]{:S(2)}) copy-start(s32[4]{0:T(128)} %param.5) | copy-start | bytes 52
  29.6 28.8 %all-to-all-start.2 = ((f32[8,32,1024]{2,1,0:T(8,128)}), f32[8,32,1024]{2,1,0:T(8,128)S(1)}, u32[]{:S(2)}, u32[]{:S(2)}) async-start(f32[8,32,1024]{2,1,0:T(8,128)} %slice.28), calls=%async_computation.2 | async-start | bytes 2097152 | tf_op jit(solution)/shard_map/all_to_all | solution.py:410
  33.2 5.9 %collective-permute-start = (f32[32,1024]{1,0:T(8,128)}, f32[32,1024]{1,0:T(8,128)S(1)}, u32[]{:S(2)}, u32[]{:S(2)}) collective-permute-start(f32[32,1024]{1,0:T(8,128)} %convert_element_type.15.here_ref.refs_3_), channel_id=1, source_target_pairs={{0,4},{4,0},{8,12},{12,8},{16,20},{20,16},{24,28},{28,24},{1,5},{5... | collective-permute-start | bytes 393224 | tf_op jit(solution)/shard_map/ppermute | solution.py:404
  33.6 5.5 %collective-permute-start.4 = (f32[3,32,1024]{2,1,0:T(8,128)S(1)}, f32[3,32,1024]{2,1,0:T(8,128)S(1)}, u32[]{:S(2)}, u32[]{:S(2)}) collective-permute-start(f32[3,32,1024]{2,1,0:T(8,128)S(1)} %pad_maximum_fusion.own_ref), channel_id=1, source_target_pairs={{0,4},{4,0},{8,12},{12,8},{16,20},{20,16},{24,28},{28,24},{1,5},{5... | collective-permute-start | bytes 1179656 | tf_op jit(solution)/shard_map/ppermute | solution.py:404
  39.1 0.7 copy-start.11
  39.1 0.8 copy-start.7
  58.5 32.4 %all-to-all-start.1 = ((f32[32,8,1024]{2,1,0:T(8,128)}), f32[32,8,1024]{2,1,0:T(8,128)S(1)}, u32[]{:S(2)}, u32[]{:S(2)}) async-start(f32[32,8,1024]{2,1,0:T(8,128)} %bitcast.22), calls=%async_computation.1 | async-start | bytes 2097152 | tf_op jit(solution)/shard_map/all_to_all | solution.py:461
  90.9 29.8 %all-to-all-start.3 = ((f32[32,8,1024]{2,1,0:T(8,128)}), f32[32,8,1024]{2,1,0:T(8,128)S(1)}, u32[]{:S(2)}, u32[]{:S(2)}) async-start(f32[32,8,1024]{2,1,0:T(8,128)} %bitcast.21), calls=%async_computation.3 | async-start | bytes 2097152 | tf_op jit(solution)/shard_map/all_to_all | solution.py:461
  127.0 21.7 %copy-start = (f32[8,64,768]{2,1,0:T(8,128)S(1)}, f32[8,64,768]{2,1,0:T(8,128)}, u32[]{:S(2)}) copy-start(f32[8,64,768]{2,1,0:T(8,128)} %get-tuple-element.21.low_ref) | copy-start | bytes 4718596
  127.0 19.2 %collective-permute-start.19 = (f32[64,1024]{1,0:T(8,128)}, f32[64,1024]{1,0:T(8,128)S(1)}, u32[]{:S(2)}, u32[]{:S(2)}) collective-permute-start(f32[64,1024]{1,0:T(8,128)} %get-tuple-element.35), channel_id=1, source_target_pairs={{1,0},{2,1},{3,2},{7,3},{6,7},{5,6},{4,5},{8,4},{9,8},{10,9},{11,1... | collective-permute-start | bytes 786440 | tf_op jit(solution)/shard_map/ppermute | solution.py:481
  128.5 5.6 %collective-permute-start.5 = (f32[64,128]{1,0:T(8,128)}, f32[64,128]{1,0:T(8,128)S(1)}, u32[]{:S(2)}, u32[]{:S(2)}) collective-permute-start(f32[64,128]{1,0:T(8,128)} %get-tuple-element.20), channel_id=1, source_target_pairs={{0,1},{1,0},{2,3},{3,2},{4,5},{5,4},{6,7},{7,6},{8,9},{9,8},{10,11... | collective-permute-start | bytes 98312 | tf_op jit(solution)/shard_map/ppermute | solution.py:501
  134.8 4.8 %collective-permute-start.6 = (f32[64,128]{1,0:T(8,128)S(1)}, f32[64,128]{1,0:T(8,128)S(1)}, u32[]{:S(2)}, u32[]{:S(2)}) collective-permute-start(f32[64,128]{1,0:T(8,128)S(1)} %add.113), channel_id=1, source_target_pairs={{0,2},{1,3},{2,0},{3,1},{4,6},{5,7},{6,4},{7,5},{8,10},{9,11},{10,... | collective-permute-start | bytes 98312 | tf_op jit(solution)/shard_map/ppermute | solution.py:501
  139.6 1.2 collective-permute-start.7
  140.8 3.9 %collective-permute-start.8 = (f32[64,128]{1,0:T(8,128)S(1)}, f32[64,128]{1,0:T(8,128)S(1)}, u32[]{:S(2)}, u32[]{:S(2)}) collective-permute-start(f32[64,128]{1,0:T(8,128)S(1)} %add.115), channel_id=1, source_target_pairs={{0,8},{4,12},{8,0},{12,4},{16,24},{20,28},{24,16},{28,20},{1,9},{5... | collective-permute-start | bytes 98312 | tf_op jit(solution)/shard_map/ppermute | solution.py:501
  144.7 4.0 %copy-start.9 = (f32[64,128]{1,0:T(8,128)}, f32[64,128]{1,0:T(8,128)S(1)}, u32[]{:S(2)}) copy-start(f32[64,128]{1,0:T(8,128)S(1)} %add.116.mine_ref) | copy-start | bytes 98308
  144.7 4.0 %collective-permute-start.9 = (f32[64,128]{1,0:T(8,128)S(1)}, f32[64,128]{1,0:T(8,128)S(1)}, u32[]{:S(2)}, u32[]{:S(2)}) collective-permute-start(f32[64,128]{1,0:T(8,128)S(1)} %add.116.mine_ref), channel_id=1, source_target_pairs={{0,16},{4,20},{8,24},{12,28},{16,0},{20,4},{24,8},{28,12},{1,17},{... | collective-permute-start | bytes 98312 | tf_op jit(solution)/shard_map/ppermute | solution.py:501
  148.1 20.5 %collective-permute-start.20 = (f32[64,64]{1,0:T(8,128)}, f32[64,64]{1,0:T(8,128)S(1)}, u32[]{:S(2)}, u32[]{:S(2)}) collective-permute-start(f32[64,64]{1,0:T(8,128)} %edge.1), channel_id=1, source_target_pairs={{0,4},{4,0},{8,12},{12,8},{16,20},{20,16},{24,28},{28,24},{1,5},{5... | collective-permute-start | bytes 49160 | tf_op jit(solution)/shard_map/ppermute | solution.py:501
  153.9 19.5 %collective-permute-start.10 = (f32[16,8,256]{2,1,0:T(8,128)}, f32[16,8,256]{2,1,0:T(8,128)S(1)}, u32[]{:S(2)}, u32[]{:S(2)}) collective-permute-start(f32[16,8,256]{2,1,0:T(8,128)} %get-tuple-element.25), channel_id=1, source_target_pairs={{0,2},{1,3},{2,0},{3,1},{4,6},{5,7},{6,4},{7,5},{8,10},{9,11},{10,... | collective-permute-start | bytes 393224 | tf_op jit(solution)/shard_map/ppermute | solution.py:557
  154.8 53.1 %collective-permute-start.15 = (f32[8,64,256]{2,1,0:T(8,128)}, f32[8,64,256]{2,1,0:T(8,128)S(1)}, u32[]{:S(2)}, u32[]{:S(2)}) collective-permute-start(f32[8,64,256]{2,1,0:T(8,128)} %get-tuple-element.23.high_ref), channel_id=1, source_target_pairs={{1,2},{2,1},{5,6},{6,5},{9,10},{10,9},{13,14},{14,13},{17,18},{18,... | collective-permute-start | bytes 1572872 | tf_op jit(solution)/shard_map/ppermute | solution.py:484
  155.5 1.4 copy-start.1
  156.9 5.8 %copy-start.13 = (f32[16,8,256]{2,1,0:T(8,128)S(1)}, f32[16,8,256]{2,1,0:T(8,128)}, u32[]{:S(2)}) copy-start(f32[16,8,256]{2,1,0:T(8,128)} %get-tuple-element.26) | copy-start | bytes 393220
  156.9 11.7 %copy-start.8 = (f32[64,64]{1,0:T(8,128)S(1)}, f32[64,64]{1,0:T(8,128)}, u32[]{:S(2)}) copy-start(f32[64,64]{1,0:T(8,128)} %edge.1) | copy-start | bytes 49156
  162.7 7.5 %copy-start.6 = (f32[16,8,1024]{2,1,0:T(8,128)S(1)}, f32[16,8,1024]{2,1,0:T(8,128)}, u32[]{:S(2)}) copy-start(f32[16,8,1024]{2,1,0:T(8,128)} %get-tuple-element.24) | copy-start | bytes 1572868
  162.7 25.6 %copy-start.12 = (f32[64,128]{1,0:T(8,128)S(1)}, f32[64,128]{1,0:T(8,128)}, u32[]{:S(2)}) copy-start(f32[64,128]{1,0:T(8,128)} %get-tuple-element.34) | copy-start | bytes 98308
  162.7 15.1 %collective-permute-start.11 = (f32[16,8,256]{2,1,0:T(8,128)S(1)}, f32[16,8,256]{2,1,0:T(8,128)S(1)}, u32[]{:S(2)}, u32[]{:S(2)}) collective-permute-start(f32[16,8,256]{2,1,0:T(8,128)S(1)} %copy-done.13), channel_id=1, source_target_pairs={{0,3},{1,2},{2,1},{3,0},{4,7},{5,6},{6,5},{7,4},{8,11},{9,10},{10,... | collective-permute-start | bytes 393224 | tf_op jit(solution)/shard_map/ppermute | solution.py:557
  164.0 24.4 %copy-start.5 = (f32[64,64]{1,0:T(8,128)S(1)}, f32[64,64]{1,0:T(8,128)}, u32[]{:S(2)}) copy-start(f32[64,64]{1,0:T(8,128)} %get-tuple-element.22.inv_ref) | copy-start | bytes 49156
  164.0 47.1 %collective-permute-start.14 = (f32[16,8,256]{2,1,0:T(8,128)}, f32[16,8,256]{2,1,0:T(8,128)}, u32[]{:S(2)}, u32[]{:S(2)}) collective-permute-start(f32[16,8,256]{2,1,0:T(8,128)} %get-tuple-element.29), channel_id=1, source_target_pairs={{0,3},{3,0},{4,7},{7,4},{8,11},{11,8},{12,15},{15,12},{16,19},{19,... | collective-permute-start | bytes 393224 | tf_op jit(solution)/shard_map/ppermute | solution.py:557
  168.7 4.0 %collective-permute-start.21 = (f32[64,64]{1,0:T(8,128)S(1)}, f32[64,64]{1,0:T(8,128)S(1)}, u32[]{:S(2)}, u32[]{:S(2)}) collective-permute-start(f32[64,64]{1,0:T(8,128)S(1)} %add.126), channel_id=1, source_target_pairs={{0,8},{4,12},{8,0},{12,4},{16,24},{20,28},{24,16},{28,20},{1,9},{5... | collective-permute-start | bytes 49160 | tf_op jit(solution)/shard_map/ppermute | solution.py:501
  172.6 3.9 %collective-permute-start.22 = (f32[64,64]{1,0:T(8,128)S(1)}, f32[64,64]{1,0:T(8,128)S(1)}, u32[]{:S(2)}, u32[]{:S(2)}) collective-permute-start(f32[64,64]{1,0:T(8,128)S(1)} %add.127), channel_id=1, source_target_pairs={{0,16},{4,20},{8,24},{12,28},{16,0},{20,4},{24,8},{28,12},{1,17},{... | collective-permute-start | bytes 49160 | tf_op jit(solution)/shard_map/ppermute | solution.py:501
  176.6 7.4 %collective-permute-start.25 = (f32[64,64]{1,0:T(8,128)S(1)}, f32[64,64]{1,0:T(8,128)S(1)}, u32[]{:S(2)}, u32[]{:S(2)}) collective-permute-start(f32[64,64]{1,0:T(8,128)S(1)} %add.128), channel_id=1, source_target_pairs={{0,3},{1,2},{2,1},{3,0},{4,7},{5,6},{6,5},{7,4},{8,11},{9,10},{10,... | collective-permute-start | bytes 49160 | tf_op jit(solution)/shard_map/ppermute | solution.py:511
  177.8 6.9 %collective-permute-start.24 = (f32[64,64]{1,0:T(8,128)S(1)}, f32[64,64]{1,0:T(8,128)S(1)}, u32[]{:S(2)}, u32[]{:S(2)}) collective-permute-start(f32[64,64]{1,0:T(8,128)S(1)} %add.128), channel_id=1, source_target_pairs={{0,2},{1,3},{2,0},{3,1},{4,6},{5,7},{6,4},{7,5},{8,10},{9,11},{10,... | collective-permute-start | bytes 49160 | tf_op jit(solution)/shard_map/ppermute | solution.py:511
  177.8 9.3 %collective-permute-start.23 = (f32[64,64]{1,0:T(8,128)S(1)}, f32[64,64]{1,0:T(8,128)S(1)}, u32[]{:S(2)}, u32[]{:S(2)}) collective-permute-start(f32[64,64]{1,0:T(8,128)S(1)} %add.128), channel_id=1, source_target_pairs={{0,1},{1,0},{2,3},{3,2},{4,5},{5,4},{6,7},{7,6},{8,9},{9,8},{10,11... | collective-permute-start | bytes 49160 | tf_op jit(solution)/shard_map/ppermute | solution.py:511
  184.0 20.7 %collective-permute-start.12 = (f32[16,8,512]{2,1,0:T(8,128)}, f32[16,8,512]{2,1,0:T(8,128)S(1)}, u32[]{:S(2)}, u32[]{:S(2)}) collective-permute-start(f32[16,8,512]{2,1,0:T(8,128)} %get-tuple-element.27), channel_id=1, source_target_pairs={{0,2},{1,3},{2,0},{3,1},{4,6},{5,7},{6,4},{7,5},{8,10},{9,11},{10,... | collective-permute-start | bytes 786440 | tf_op jit(solution)/shard_map/ppermute | solution.py:557
  184.7 22.2 %collective-permute-start.13 = (f32[16,8,512]{2,1,0:T(8,128)}, f32[16,8,512]{2,1,0:T(8,128)}, u32[]{:S(2)}, u32[]{:S(2)}) collective-permute-start(f32[16,8,512]{2,1,0:T(8,128)} %get-tuple-element.28), channel_id=1, source_target_pairs={{0,3},{1,2},{2,1},{3,0},{4,7},{5,6},{6,5},{7,4},{8,11},{9,10},{10,... | collective-permute-start | bytes 786440 | tf_op jit(solution)/shard_map/ppermute | solution.py:557
  187.1 25.1 %collective-permute-start.16 = (f32[16,8,1024]{2,1,0:T(8,128)}, f32[16,8,1024]{2,1,0:T(8,128)S(1)}, u32[]{:S(2)}, u32[]{:S(2)}) collective-permute-start(f32[16,8,1024]{2,1,0:T(8,128)} %get-tuple-element.31), channel_id=1, source_target_pairs={{0,1},{1,0},{2,3},{3,2},{4,5},{5,4},{6,7},{7,6},{8,9},{9,8},{10,11... | collective-permute-start | bytes 1572872 | tf_op jit(solution)/shard_map/ppermute | solution.py:557
  204.8 7.4 %collective-permute-start.17 = (f32[16,8,256]{2,1,0:T(8,128)}, f32[16,8,256]{2,1,0:T(8,128)}, u32[]{:S(2)}, u32[]{:S(2)}) collective-permute-start(f32[16,8,256]{2,1,0:T(8,128)} %get-tuple-element.32), channel_id=1, source_target_pairs={{0,2},{3,1},{4,6},{7,5},{8,10},{11,9},{12,14},{15,13},{16,18},{19,... | collective-permute-start | bytes 393224 | tf_op jit(solution)/shard_map/ppermute | solution.py:557
  209.8 8.7 %collective-permute-start.18 = (f32[16,8,256]{2,1,0:T(8,128)}, f32[16,8,256]{2,1,0:T(8,128)S(1)}, u32[]{:S(2)}, u32[]{:S(2)}) collective-permute-start(f32[16,8,256]{2,1,0:T(8,128)} %get-tuple-element.33), channel_id=1, source_target_pairs={{1,0},{2,3},{5,4},{6,7},{9,8},{10,11},{13,12},{14,15},{17,16},{18,... | collective-permute-start | bytes 393224 | tf_op jit(solution)/shard_map/ppermute | solution.py:557
  219.4 1.3 copy-start.2
